TPU v7x, 128 devices: a whole 4x4x4 slice. The times are simulated.
128 devices in a mesh: dom: 64 (over y, z, x), head: 2 (over core).
Axes of the slice: x: 4, y: 4, z: 4, core: 2. Of those that a mesh axis runs over, the one named last changes fastest.
Arguments:
- vertex_state: bfloat16 [131072, 128], P('dom'), may hold values from -6 to 6
- link_state_slotted: bfloat16 [786432, 128], P('dom'), may hold values from -6 to 6
- source_vertex_ids: int32 [786432], P('dom'), may hold values from 0 to 4095
- target_vertex_ids: int32 [786432], P('dom'), may hold values from 0 to 2047
- active_link_tally: int32 [64], P('dom'), may hold values from 6144 to 12288, as said below
- halo_outgoing_ids: int32 [64, 4, 512], P('dom'), may hold values from 0 to 2047
- link_layer_alpha: bfloat16 [384, 128], replicated, may hold values from -0.3125 to 0.3125
- link_layer_beta: bfloat16 [128, 128], replicated, may hold values from -0.5 to 0.5
- link_layer_gamma: bfloat16 [128, 128], replicated, may hold values from -0.5 to 0.5
- link_scale_factor: float32 [128], replicated, may hold values from 0.25 to 1.75
- vertex_layer_alpha: bfloat16 [256, 128], replicated, may hold values from -0.375 to 0.375
- vertex_layer_beta: bfloat16 [128, 128], replicated, may hold values from -0.5 to 0.5
- vertex_layer_gamma: bfloat16 [128, 128], replicated, may hold values from -0.5 to 0.5
- vertex_scale_factor: float32 [128], replicated, may hold values from 0.25 to 1.75
- focus_scale_factor: float32 [128], replicated, may hold values from 0.25 to 1.75
- vertex_content_factor: bfloat16 [128, 128], P(None, 'head'), may hold values from -0.5 to 0.5
- cluster_affinity_factor: bfloat16 [128, 512], P(None, 'head'), may hold values from -0.5 to 0.5
- softness_level: float32 [8], P('head'), may hold values from 0.15 to 2, as said below
- cluster_probe_lookup: float32 [2, 8, 16, 16], P(None, 'head'), may hold values from -8 to 8
- cluster_content_linear: float32 [8, 16, 16], P('head'), may hold values from -1.5 to 1.5
- closing_linear_factor: bfloat16 [128, 128], P('head'), may hold values from -0.5 to 0.5
Outputs:
- result: bfloat16 [131072, 128], P('dom')
Inputs may be any that keep to these rules, and one draw needn't show every extreme that they name: `active_link_tally`: each count lies between half the slots and all of them; in every draw some partition's slots are all valid. `softness_level`: positive.
All inputs are finite; a program needn't handle non-finite values.
Results may differ from a plain program's by a relative error of at most 0.0085.
Values may be sent and summed in bfloat16 or wider, within the bound.
A program may use at most 64 MiB of HBM per device.

v0:
```python
import functools
import math

import jax
import jax.numpy as jnp
from jax import lax
from jax.experimental import pallas as pl
from jax.experimental.pallas import tpu as pltpu
from jax.sharding import PartitionSpec as P

HEAD_DIM = 16
GROUPS_PER_LANE = 64
FOLD = 4


def passed_along(value, axis, steps):
    count = lax.axis_size(axis)
    first, last = (max(0, -steps), min(count, count - steps))
    return lax.ppermute(value, axis, [(source, source + steps) for source in range(first, last)])


def _radix_kernel(radix, steps, x_ref, o_ref, inbox, send_sem, recv_sem):
    me = lax.axis_index("dom")
    spans = [radix**s for s in range(steps)]
    digits = [(me // span) % radix for span in spans]
    partners = [
        [me + ((digit + j) % radix - digit) * span for j in range(1, radix)]
        for digit, span in zip(digits, spans)
    ]
    barrier = pltpu.get_barrier_semaphore()
    for group in partners:
        for partner in group:
            pl.semaphore_signal(
                barrier, 1, device_id={"dom": partner}, device_id_type=pl.DeviceIdType.MESH
            )
    pl.semaphore_wait(barrier, steps * (radix - 1))
    for s in range(steps):
        source = x_ref if s == 0 else o_ref
        copies = []
        for j, partner in enumerate(partners[s]):
            copy = pltpu.make_async_remote_copy(
                src_ref=source,
                dst_ref=inbox.at[s, digits[s]],
                send_sem=send_sem.at[s, j],
                recv_sem=recv_sem.at[s, digits[s]],
                device_id={"dom": partner},
                device_id_type=pl.DeviceIdType.MESH,
            )
            copy.start()
            copies.append(copy)
        inbox[s, digits[s]] = source[...]
        for copy in copies:
            copy.wait_send()
        for j, partner in enumerate(partners[s]):
            slot = (digits[s] + j + 1) % radix
            pltpu.make_async_remote_copy(
                src_ref=source,
                dst_ref=inbox.at[s, slot],
                send_sem=send_sem.at[s, j],
                recv_sem=recv_sem.at[s, slot],
                device_id={"dom": partner},
                device_id_type=pl.DeviceIdType.MESH,
            ).wait_recv()
        total = inbox[s, 0]
        for d in range(1, radix):
            total = total + inbox[s, d]
        o_ref[...] = total


def dom_sum(flat):
    count = lax.axis_size("dom")
    radix = 4
    steps = 0
    while radix ** (steps + 1) <= count:
        steps += 1
    assert radix**steps == count
    return pl.pallas_call(
        functools.partial(_radix_kernel, radix, steps),
        out_shape=jax.ShapeDtypeStruct(flat.shape, flat.dtype),
        in_specs=[pl.BlockSpec(memory_space=pltpu.VMEM)],
        out_specs=pl.BlockSpec(memory_space=pltpu.VMEM),
        scratch_shapes=[
            pltpu.VMEM((steps, radix) + flat.shape, flat.dtype),
            pltpu.SemaphoreType.DMA((steps, radix - 1)),
            pltpu.SemaphoreType.DMA((steps, radix)),
        ],
        compiler_params=pltpu.CompilerParams(collective_id=0, has_side_effects=True),
    )(flat)


def _halo_kernel(offsets, own_ref, out_ref, ext_ref, send_sem, recv_sem):
    me = lax.axis_index("dom")
    count = lax.axis_size("dom")
    rows = own_ref.shape[0]
    halo = out_ref.shape[1]
    barrier = pltpu.get_barrier_semaphore()
    for offset in offsets:
        pl.semaphore_signal(
            barrier,
            1,
            device_id={"dom": (me + offset + count) % count},
            device_id_type=pl.DeviceIdType.MESH,
        )
    pl.semaphore_wait(barrier, len(offsets))
    copies = []
    for k, offset in enumerate(offsets):
        copy = pltpu.make_async_remote_copy(
            src_ref=out_ref.at[k],
            dst_ref=ext_ref.at[pl.ds(rows + k * halo, halo)],
            send_sem=send_sem.at[k],
            recv_sem=recv_sem.at[k],
            device_id={"dom": (me + offset + count) % count},
            device_id_type=pl.DeviceIdType.MESH,
        )
        copy.start()
        copies.append(copy)
    ext_ref[pl.ds(0, rows)] = own_ref[...]
    for copy in copies:
        copy.wait()
    for k, offset in enumerate(offsets):
        if offset > 0:
            inside = (me + count - offset) // count
        else:
            inside = (2 * count - 1 + offset - me) // count
        slot = pl.ds(rows + k * halo, halo)
        ext_ref[slot] = ext_ref[slot] * inside.astype(ext_ref.dtype)


def exchange_halos(own_rows, outgoing, offsets):
    rows = own_rows.shape[0]
    total = rows + outgoing.shape[0] * outgoing.shape[1]
    return pl.pallas_call(
        functools.partial(_halo_kernel, offsets),
        out_shape=jax.ShapeDtypeStruct((total, own_rows.shape[1]), own_rows.dtype),
        in_specs=[pl.BlockSpec(memory_space=pltpu.VMEM)] * 2,
        out_specs=pl.BlockSpec(memory_space=pltpu.VMEM),
        scratch_shapes=[
            pltpu.SemaphoreType.DMA((len(offsets),)),
            pltpu.SemaphoreType.DMA((len(offsets),)),
        ],
        compiler_params=pltpu.CompilerParams(collective_id=1, has_side_effects=True),
    )(own_rows, outgoing)


def psum_slices(numer, denom):
    joined = jnp.concatenate([numer.reshape(-1), denom.reshape(-1)])
    rows = -(-joined.shape[0] // 1024) * 8
    padded = jnp.zeros((rows * 128,), joined.dtype).at[: joined.shape[0]].set(joined)
    total = dom_sum(padded.reshape(rows, 128)).reshape(-1)
    numer_size = numer.size
    return (
        total[:numer_size].reshape(numer.shape),
        total[numer_size : numer_size + denom.size].reshape(denom.shape),
    )


def layer_norm(values, gain_row):
    row_mean = jnp.mean(values, axis=-1, keepdims=True)
    centred = values - row_mean
    row_var = jnp.mean(centred * centred, axis=-1, keepdims=True)
    return centred * lax.rsqrt(row_var + 1e-05) * gain_row


def node_section(
    own_rows,
    summed_b,
    vertex_layer_alpha,
    vertex_layer_beta,
    vertex_layer_gamma,
    vertex_scale_factor,
):
    feature_width = own_rows.shape[1]
    node_pre = jnp.dot(
        own_rows, vertex_layer_alpha[:feature_width], preferred_element_type=jnp.float32
    )
    node_pre = node_pre + jnp.dot(
        summed_b, vertex_layer_alpha[feature_width:], preferred_element_type=jnp.float32
    )
    node_one = jax.nn.silu(node_pre).astype(jnp.bfloat16)
    node_two = jax.nn.silu(
        jnp.dot(node_one, vertex_layer_beta, preferred_element_type=jnp.float32)
    ).astype(jnp.bfloat16)
    node_three = jnp.dot(node_two, vertex_layer_gamma, preferred_element_type=jnp.float32)
    return (own_rows.astype(jnp.float32) + layer_norm(node_three, vertex_scale_factor)).astype(
        jnp.bfloat16
    )


def slice_partial_terms(
    refreshed_vertices,
    focus_scale_factor,
    vertex_content_factor,
    cluster_affinity_factor,
    softness_level,
):
    count_of_rows = refreshed_vertices.shape[0]
    domain_channel_split = softness_level.shape[0]
    standardised_entries = layer_norm(
        refreshed_vertices.astype(jnp.float32), focus_scale_factor
    ).astype(jnp.bfloat16)
    values = jnp.dot(
        standardised_entries, vertex_content_factor, preferred_element_type=jnp.float32
    ).astype(jnp.bfloat16)
    cluster_affinities = jnp.dot(
        standardised_entries, cluster_affinity_factor, preferred_element_type=jnp.float32
    )
    cluster_affinities = (
        cluster_affinities.reshape(count_of_rows, domain_channel_split, GROUPS_PER_LANE)
        / softness_level[None, :, None]
    )
    weights = jax.nn.softmax(cluster_affinities, axis=-1)
    weights_b = weights.astype(jnp.bfloat16)
    numer = jnp.einsum(
        "nhs,nhc->hsc",
        weights_b,
        values.reshape(count_of_rows, domain_channel_split, HEAD_DIM),
        preferred_element_type=jnp.float32,
    )
    denom = jnp.sum(weights, axis=0)
    return (weights_b, numer, denom)


def slice_mixing(numer, denom, cluster_probe_lookup, cluster_content_linear):
    tokens = numer / denom[:, :, None]
    highest = lax.Precision.HIGHEST
    query = jnp.einsum("hsc,hcd->hsd", tokens, cluster_probe_lookup[0], precision=highest)
    keys = jnp.einsum("hsc,hcd->hsd", tokens, cluster_probe_lookup[1], precision=highest)
    carried = jnp.einsum("hsc,hcd->hsd", tokens, cluster_content_linear, precision=highest)
    scores = jnp.einsum("hsd,htd->hst", query, keys, precision=highest) / math.sqrt(HEAD_DIM)
    mixing = jax.nn.softmax(scores, axis=-1)
    return jnp.einsum("hst,htd->hsd", mixing, carried, precision=highest).astype(jnp.bfloat16)


def attend_rows(weights_b, slice_out):
    count_of_rows = weights_b.shape[0]
    domain_channel_split = weights_b.shape[1]
    attended = jnp.einsum("nhs,hsd->nhd", weights_b, slice_out, preferred_element_type=jnp.float32)
    return attended.reshape(count_of_rows, domain_channel_split * HEAD_DIM).astype(jnp.bfloat16)


def pick_rows(table, row_ids):
    table_ids = jnp.arange(table.shape[0], dtype=jnp.int32)
    selector = (row_ids[:, None] == table_ids[None, :]).astype(jnp.bfloat16)
    return jnp.dot(selector, table, preferred_element_type=jnp.float32).astype(jnp.bfloat16)


def gather_rows(table, row_ids, fold):
    count, width = table.shape
    wide = table.reshape(count // fold, fold * width)
    hot = (row_ids[:, None] // fold == jnp.arange(count // fold, dtype=jnp.int32)[None, :]).astype(
        jnp.bfloat16
    )
    picked = jnp.dot(hot, wide, preferred_element_type=jnp.float32)
    lane = row_ids % fold
    rows = picked[:, :width]
    for j in range(1, fold):
        rows = jnp.where((lane == j)[:, None], picked[:, j * width : (j + 1) * width], rows)
    return rows.astype(jnp.bfloat16)


def scatter_rows(messages, row_ids, count, fold):
    width = messages.shape[1]
    lane = row_ids % fold
    spread = jnp.concatenate(
        [jnp.where((lane == j)[:, None], messages, jnp.zeros_like(messages)) for j in range(fold)],
        axis=1,
    )
    hot = (row_ids[:, None] // fold == jnp.arange(count // fold, dtype=jnp.int32)[None, :]).astype(
        jnp.bfloat16
    )
    total = lax.dot_general(
        hot, spread, (((0,), (0,)), ((), ())), preferred_element_type=jnp.float32
    )
    return total.reshape(count, width)


def body(
    vertex_state,
    link_state_slotted,
    source_vertex_ids,
    target_vertex_ids,
    active_link_tally,
    halo_outgoing_ids,
    link_layer_alpha,
    link_layer_beta,
    link_layer_gamma,
    link_scale_factor,
    vertex_layer_alpha,
    vertex_layer_beta,
    vertex_layer_gamma,
    vertex_scale_factor,
    focus_scale_factor,
    vertex_content_factor,
    cluster_affinity_factor,
    softness_level,
    cluster_probe_lookup,
    cluster_content_linear,
    closing_linear_factor,
):
    node_count = vertex_state.shape[0]
    feature_width = vertex_state.shape[1]
    capacity = link_state_slotted.shape[0]
    offsets = (1, -1, 2, -2)
    outgoing = pick_rows(vertex_state, halo_outgoing_ids[0].reshape(-1))
    extended = exchange_halos(
        vertex_state, outgoing.reshape(halo_outgoing_ids.shape[1:] + (feature_width,)), offsets
    )
    extended_ids = jnp.arange(extended.shape[0], dtype=jnp.int32)
    node_ids = jnp.arange(node_count, dtype=jnp.int32)
    block_rows = capacity // lax.axis_size("head")
    share = capacity // lax.axis_size("head")
    first_row = lax.axis_index("head") * share
    edge_rows = lax.dynamic_slice_in_dim(link_state_slotted, first_row, share, 0)
    send_rows = lax.dynamic_slice_in_dim(source_vertex_ids, first_row, share, 0)
    recv_rows = lax.dynamic_slice_in_dim(target_vertex_ids, first_row, share, 0)
    turns = edge_rows.shape[0] // block_rows
    edge_blocks = edge_rows.reshape(turns, block_rows, feature_width)
    send_blocks = send_rows.reshape(turns, block_rows)
    recv_blocks = recv_rows.reshape(turns, block_rows)

    def step(total, item):
        edge_part, send_part, recv_part, turn = item
        sender_rows = gather_rows(extended, send_part, FOLD)
        receiver_rows = gather_rows(vertex_state, recv_part, FOLD)
        pre = jnp.dot(
            edge_part, link_layer_alpha[:feature_width], preferred_element_type=jnp.float32
        )
        pre = pre + jnp.dot(
            sender_rows,
            link_layer_alpha[feature_width : 2 * feature_width],
            preferred_element_type=jnp.float32,
        )
        pre = pre + jnp.dot(
            receiver_rows, link_layer_alpha[2 * feature_width :], preferred_element_type=jnp.float32
        )
        first = jax.nn.silu(pre).astype(jnp.bfloat16)
        second = jax.nn.silu(
            jnp.dot(first, link_layer_beta, preferred_element_type=jnp.float32)
        ).astype(jnp.bfloat16)
        third = jnp.dot(second, link_layer_gamma, preferred_element_type=jnp.float32)
        edge_new = (edge_part.astype(jnp.float32) + layer_norm(third, link_scale_factor)).astype(
            jnp.bfloat16
        )
        position = first_row + turn * block_rows + jnp.arange(block_rows, dtype=jnp.int32)
        live = position < active_link_tally[0]
        messages = jnp.where(live[:, None], edge_new, jnp.zeros_like(edge_new))
        gathered = scatter_rows(messages, recv_part, node_count, FOLD)
        return (total + gathered, None)

    start = jnp.zeros((node_count, feature_width), jnp.float32)
    total, unused = lax.scan(
        step, start, (edge_blocks, send_blocks, recv_blocks, jnp.arange(turns, dtype=jnp.int32))
    )
    summed = lax.psum(total, "head")
    refreshed_vertices = node_section(
        vertex_state,
        summed.astype(jnp.bfloat16),
        vertex_layer_alpha,
        vertex_layer_beta,
        vertex_layer_gamma,
        vertex_scale_factor,
    )
    weights_b, numer, denom = slice_partial_terms(
        refreshed_vertices,
        focus_scale_factor,
        vertex_content_factor,
        cluster_affinity_factor,
        softness_level,
    )
    numer, denom = psum_slices(numer, denom)
    slice_out = slice_mixing(numer, denom, cluster_probe_lookup, cluster_content_linear)
    attended = attend_rows(weights_b, slice_out)
    projected = jnp.dot(attended, closing_linear_factor, preferred_element_type=jnp.float32)
    return (refreshed_vertices.astype(jnp.float32) + projected).astype(jnp.bfloat16)


def solution(mesh):
    in_specs = (
        P("dom", None),
        P("dom", None),
        P("dom"),
        P("dom"),
        P("dom"),
        P("dom", None, None),
        P(),
        P(),
        P(),
        P(),
        P(),
        P(),
        P(),
        P(),
        P(),
        P(),
        P(),
        P(),
        P(),
        P(),
        P(),
    )
    out_specs = P("dom", None)
    return jax.shard_map(body, mesh=mesh, in_specs=in_specs, out_specs=out_specs, check_vma=False)
```

profile of v0, /device:TPU:1, one launch (start us, length us, event | category | flops | bytes accessed | tf_op | source)
XLA Modules:
  0.0 137.3 jit_solution(4633872766600743255)
XLA Ops:
  3.9 4.7 %fusion.25 = bf16[2048,128]{1,0:T(8,128)(2,1)} fusion(bf16[2048,128]{1,0:T(8,128)(2,1)} %own_ref.1, s32[2048]{0:T(1024)S(1)} %bitcast.60), kind=kOutput, calls=%fused_computation.42 | convolution fusion | flops 1078198272 | bytes 1056768 | tf_op jit(solution)/shard_map/dot_general | solution.py:244
  8.6 19.6 %shard_map.199 = bf16[4096,128]{1,0:T(8,128)(2,1)} custom-call(bf16[2048,128]{1,0:T(8,128)(2,1)} %own_ref.1, bf16[4,512,128]{2,1,0:T(8,128)(2,1)} %bitcast.58), custom_call_target="tpu_custom_call" | custom-call | tf_op jit(solution)/shard_map/pallas_call | solution.py:132
  28.2 1.7 %reshape.172 = bf16[1024,512]{1,0:T(8,128)(2,1)S(1)} reshape(bf16[4096,128]{1,0:T(8,128)(2,1)} %shard_map.199) | data formatting | bytes 2097152 | tf_op jit(solution)/shard_map/while/body/eval_jaxpr/reshape | solution.py:249
  29.9 8.4 %fusion = bf16[6144,512]{1,0:T(8,128)(2,1)S(1)} fusion(bf16[1024,512]{1,0:T(8,128)(2,1)S(1)} %reshape.172, s32[6144]{0:T(1024)S(1)} %get-tuple-element.84), kind=kOutput, calls=%fused_computation.1 | convolution fusion | flops 6448742400 | bytes 7364608 | tf_op jit(solution)/shard_map/while/body/eval_jaxpr/dot_general | solution.py:253
  38.9 8.1 %convolution_add_fusion.1 = f32[6144,128]{1,0:T(8,128)} fusion(f32[6144,128]{1,0:T(8,128)S(1)} %fusion.41, bf16[6144,512]{1,0:T(8,128)(2,1)S(1)} %fusion, pred[6144]{0:T(1024)(128)(4,1)S(1)} %get-tuple-element.75, pred[6144]{0:T(1024)(128)(4,1)S(1)} %get-tuple-element.74, pred[6144]{0:T(1024)(128)(4,1)S(1)} %get-tuple-element.65, ...), kind=kOutput, calls=%fused_computation.10 | convolution fusion | flops 204472320 | bytes 12634112 | tf_op jit(solution)/shard_map/while/body/eval_jaxpr/dot_general | solution.py:328
  47.4 5.3 %fusion.4 = bf16[6144,512]{1,0:T(8,128)(2,1)} fusion(bf16[512,512]{1,0:T(8,128)(2,1)S(1)} %reshape.173, s32[6144]{0:T(1024)S(1)} %get-tuple-element.85), kind=kOutput, calls=%fused_computation.7 | convolution fusion | flops 3224371200 | bytes 6840320 | tf_op jit(solution)/shard_map/while/body/eval_jaxpr/dot_general | solution.py:253
  52.7 5.6 %multiply_convert_fusion = bf16[6144,128]{1,0:T(8,128)(2,1)S(1)} fusion(bf16[128,128]{1,0:T(8,128)(2,1)S(1)} %copy-done.17, f32[6144,128]{1,0:T(8,128)} %convolution_add_fusion.1, bf16[6144,512]{1,0:T(8,128)(2,1)} %fusion.4, pred[6144]{0:T(1024)(128)(4,1)S(1)} %get-tuple-element.86, pred[6144]{0:T(1024)(128)(4,1)S(1)} %get-tuple-element.87, ...), kind=kOutput, calls=%fused_computation.37 | convolution fusion | flops 413663232 | bytes 11094016 | tf_op jit(solution)/shard_map/while/body/eval_jaxpr/dot_general | solution.py:338
  58.3 2.3 %fusion.84 = (f32[6144]{0:T(1024)S(1)}, f32[6144,128]{0,1:T(8,128)}) fusion(bf16[6144,128]{1,0:T(8,128)(2,1)S(1)} %multiply_convert_fusion, bf16[128,128]{1,0:T(8,128)(2,1)S(1)} %copy-done), kind=kOutput, calls=%fused_computation.136 | convolution fusion | flops 202106880 | bytes 4775936 | tf_op jit(solution)/shard_map/while/body/eval_jaxpr/dot_general | solution.py:340
  60.6 2.4 %copy.43 = f32[6144,128]{1,0:T(8,128)S(1)} copy(f32[6144,128]{0,1:T(8,128)} %get-tuple-element.77) | data formatting | bytes 6291456 | tf_op jit(solution)/shard_map/while/body/eval_jaxpr/dot_general | solution.py:340
  63.0 1.8 %multiply_reduce_fusion = f32[6144]{0:T(1024)S(1)} fusion(f32[6144,128]{1,0:T(8,128)S(1)} %copy.43, f32[6144]{0:T(1024)S(1)} %broadcast_multiply_fusion), kind=kLoop, calls=%fused_computation.36 | loop fusion | flops 2353152 | bytes 3194880 | tf_op jit(solution)/shard_map/while/body/eval_jaxpr/reduce_sum | solution.py:160
  65.5 5.7 %broadcast_select_fusion.3 = (bf16[6144,128]{1,0:T(8,128)(2,1)S(1)}, bf16[6144,128]{1,0:T(8,128)(2,1)S(1)}) fusion(pred[6144]{0:T(1024)(128)(4,1)S(1)} %get-tuple-element.62, f32[128]{0:T(128)S(1)} %copy-done.14, f32[6144]{0:T(1024)S(1)} %add_rsqrt_fusion, f32[6144,128]{1,0:T(8,128)S(1)} %copy.43, f32[6144]{0:T(1024)S(1)} %broadcast_multiply_fusion, ...), kind=kLoop, calls=%fused_computation.60 | loop fusion | flops 6291456 | bytes 7926276 | tf_op jit(solution)/shard_map/while/body/eval_jaxpr/jit(_where)/select_n | solution.py:265
  71.2 4.8 %broadcast_select_fusion = (bf16[6144,128]{1,0:T(8,128)(2,1)S(1)}, bf16[6144,128]{1,0:T(8,128)(2,1)S(1)}, bf16[6144,128]{1,0:T(8,128)(2,1)S(1)}) fusion(bf16[6144,128]{1,0:T(8,128)(2,1)S(1)} %get-tuple-element.61, pred[6144]{0:T(1024)(128)(4,1)S(1)} %get-tuple-element.86, pred[6144]{0:T(1024)(128)(4,1)S(1)} %get-tuple-element.87, ...), kind=kLoop, calls=%fused_computation.51 | loop fusion | flops 2359296 | bytes 6309888 | tf_op jit(solution)/shard_map/while/body/eval_jaxpr/jit(_where)/select_n | solution.py:265
  76.1 4.3 %fusion.3 = f32[512,512]{1,0:T(8,128)S(1)} fusion(bf16[6144,128]{1,0:T(8,128)(2,1)S(1)} %get-tuple-element.70, bf16[6144,128]{1,0:T(8,128)(2,1)S(1)} %get-tuple-element.69, bf16[6144,128]{1,0:T(8,128)(2,1)S(1)} %get-tuple-element.68, bf16[6144,128]{1,0:T(8,128)(2,1)S(1)} %get-tuple-element.60, s32[6144]{0:T(1024)S(1)} %get-tuple-element.85), kind=kOutput, calls=%fused_computation.6 | convolution fusion | flops 3249537024 | bytes 7364608 | tf_op jit(solution)/shard_map/while/body/eval_jaxpr/dot_general | solution.py:271
  82.0 7.7 %all-reduce.4 = (bf16[2048,128]{1,0:T(8,128)(2,1)S(1)}, f32[8]{0:T(128)S(1)}) all-reduce(f32[2048,128]{1,0:T(8,128)S(1)} %reshape.174, f32[8]{0:T(128)S(1)} %dynamic-update-slice.2), channel_id=1, replica_groups=mesh['dom'=64,'head'=2] {'head'}, use_global_device_ids=true, to_apply=%region_2.3 | all-reduce | flops 262152 | bytes 1572928 | tf_op jit(solution)/shard_map/psum | solution.py:354
  92.0 1.8 %all-gather = bf16[128,128]{0,1:T(8,128)(2,1)S(1)} all-gather(bf16[128,64]{0,1:T(8,128)(2,1)S(1)} %copy-done.11), channel_id=3, replica_groups=mesh['dom'=64,'head'=2] {'head'}, dimensions={1}, use_global_device_ids=true | all-gather | bytes 49152 | tf_op args[15]
  94.2 1.9 %all-gather.1 = bf16[128,512]{1,0:T(8,128)(2,1)S(1)} all-gather(bf16[128,256]{1,0:T(8,128)(2,1)S(1)} %copy-done.6), channel_id=4, replica_groups=mesh['dom'=64,'head'=2] {'head'}, dimensions={1}, use_global_device_ids=true | all-gather | bytes 196608 | tf_op args[16]
  97.8 1.1 copy-done.1
  100.2 3.2 %fusion.16 = f32[512]{0:T(512)S(1)} fusion(f32[2048,512]{0,1:T(8,128)} %copy-done.1, f32[512]{0:T(512)S(1)} %div.136, f32[2048,8]{0,1:T(8,128)S(1)} %fusion.17, f32[2048,8]{0,1:T(8,128)S(1)} %get-tuple-element.80), kind=kLoop, calls=%fused_computation.25 | loop fusion | flops 4193792 | bytes 4329472 | tf_op jit(solution)/shard_map/reduce_sum | solution.py:219
  104.0 16.7 %shard_map.200 = f32[72,128]{1,0:T(8,128)} custom-call(f32[72,128]{1,0:T(8,128)} %fusion.61.x_ref), custom_call_target="tpu_custom_call" | custom-call | tf_op jit(solution)/shard_map/pallas_call | solution.py:77
  122.6 4.8 %all-gather.3 = f32[2,8,16,16]{2,3,1,0:T(8,128)S(1)} all-gather(f32[2,4,16,16]{2,3,1,0:T(8,128)S(1)} %copy.46), channel_id=6, replica_groups=mesh['dom'=64,'head'=2] {'head'}, dimensions={1}, use_global_device_ids=true | all-gather | bytes 24576 | tf_op args[18]
  128.5 1.9 %all-gather.4 = f32[8,16,16]{2,1,0:T(8,128)S(1)} all-gather(f32[4,16,16]{2,1,0:T(8,128)S(1)} %copy-done.9), channel_id=7, replica_groups=mesh['dom'=64,'head'=2] {'head'}, dimensions={0}, use_global_device_ids=true | all-gather | bytes 12288 | tf_op args[19]
  131.0 3.2 %convolution_convert_fusion.1 = bf16[8,16,2048]{2,1,0:T(8,128)(2,1)S(1)} fusion(bf16[8,64,16]{1,2,0:T(8,128)(2,1)S(1)} %convolution_convert_fusion.2, f32[2048,8]{0,1:T(8,128)S(1)} %fusion.17, f32[2048,8]{0,1:T(8,128)S(1)} %get-tuple-element.80, f32[8]{0:T(128)S(1)} %get-tuple-element.57, f32[2048,512]{0,1:T(8,128)} %copy-done.1), kind=kOutput, calls=%fused_computation.44 | convolution fusion | flops 38010880 | bytes 4866080 | tf_op jit(solution)/shard_map/nhs,hsd->nhd/dot_general | solution.py:237
  134.2 1.8 %all-gather.5 = bf16[128,128]{1,0:T(8,128)(2,1)S(1)} all-gather(bf16[64,128]{1,0:T(8,128)(2,1)S(1)} %copy-done.12), channel_id=8, replica_groups=mesh['dom'=64,'head'=2] {'head'}, dimensions={0}, use_global_device_ids=true | all-gather | bytes 49152 | tf_op args[20]
  136.3 1.0 copy.50
  (87 shorter events, 15.7 us)
Async XLA Ops:
  0.0 58.3 %copy-start = (bf16[128,128]{1,0:T(8,128)(2,1)S(1)}, bf16[128,128]{1,0:T(8,128)(2,1)}, u32[]{:S(2)}) copy-start(bf16[128,128]{1,0:T(8,128)(2,1)} %param.31) | copy-start | bytes 98308
  29.9 8.4 %copy-start.4 = (bf16[12288,128]{1,0:T(8,128)(2,1)S(1)}, bf16[12288,128]{1,0:T(8,128)(2,1)}, u32[]{:S(2)}) copy-start(bf16[12288,128]{1,0:T(8,128)(2,1)} %param.24) | copy-start | bytes 9437188
  29.9 8.4 %copy-start.13 = (bf16[384,128]{1,0:T(8,128)(2,1)S(1)}, bf16[384,128]{1,0:T(8,128)(2,1)}, u32[]{:S(2)}) copy-start(bf16[384,128]{1,0:T(8,128)(2,1)} %param.29) | copy-start | bytes 294916
  38.9 8.2 %copy-start.2 = (bf16[2048,128]{1,0:T(8,128)(2,1)S(1)}, bf16[2048,128]{1,0:T(8,128)(2,1)}, u32[]{:S(2)}) copy-start(bf16[2048,128]{1,0:T(8,128)(2,1)} %own_ref.1) | copy-start | bytes 1572868
  47.4 5.3 %copy-start.17 = (bf16[128,128]{1,0:T(8,128)(2,1)S(1)}, bf16[128,128]{1,0:T(8,128)(2,1)}, u32[]{:S(2)}) copy-start(bf16[128,128]{1,0:T(8,128)(2,1)} %param.30) | copy-start | bytes 98308
  63.0 2.6 %copy-start.5 = (bf16[12288,128]{1,0:T(8,128)(2,1)S(1)}, bf16[12288,128]{1,0:T(8,128)(2,1)}, u32[]{:S(2)}) copy-start(bf16[12288,128]{1,0:T(8,128)(2,1)} %param.24) | copy-start | bytes 9437188
  63.0 2.6 %copy-start.14 = (f32[128]{0:T(128)S(1)}, f32[128]{0:T(128)}, u32[]{:S(2)}) copy-start(f32[128]{0:T(128)} %param.32) | copy-start | bytes 1540
  76.0 4.5 %copy-start.20 = (u32[128]{0:T(128)S(1)}, u32[128]{0:T(128)}, u32[]{:S(2)}) copy-start(u32[128]{0:T(128)} %constant.143) | copy-start | bytes 1540
  76.1 5.7 %copy-start.19 = (f32[4]{0:T(128)S(1)}, f32[4]{0:T(128)}, u32[]{:S(2)}) copy-start(f32[4]{0:T(128)} %param.40) | copy-start | bytes 52
  80.4 9.3 %copy-start.3 = (bf16[2048,128]{1,0:T(8,128)(2,1)S(1)}, bf16[2048,128]{1,0:T(8,128)(2,1)}, u32[]{:S(2)}) copy-start(bf16[2048,128]{1,0:T(8,128)(2,1)} %own_ref.1) | copy-start | bytes 1572868
  80.4 9.3 %copy-start.10 = (bf16[256,128]{1,0:T(8,128)(2,1)S(1)}, bf16[256,128]{1,0:T(8,128)(2,1)}, u32[]{:S(2)}) copy-start(bf16[256,128]{1,0:T(8,128)(2,1)} %param.33) | copy-start | bytes 196612
  80.4 9.6 %copy-start.18 = (bf16[128,128]{1,0:T(8,128)(2,1)S(1)}, bf16[128,128]{1,0:T(8,128)(2,1)}, u32[]{:S(2)}) copy-start(bf16[128,128]{1,0:T(8,128)(2,1)} %param.34) | copy-start | bytes 98308
  90.0 0.8 copy-start.8
  90.8 0.8 copy-start.15
  90.8 1.2 copy-start.11
  90.8 3.1 %copy-start.16 = (f32[128]{0:T(128)S(1)}, f32[128]{0:T(128)}, u32[]{:S(2)}) copy-start(f32[128]{0:T(128)} %param.37) | copy-start | bytes 1540
  91.2 3.1 %copy-start.6 = (bf16[128,256]{1,0:T(8,128)(2,1)S(1)}, bf16[128,256]{1,0:T(8,128)(2,1)}, u32[]{:S(2)}) copy-start(bf16[128,256]{1,0:T(8,128)(2,1)} %param.39) | copy-start | bytes 196612
  97.0 1.9 %copy-start.1 = (f32[2048,512]{0,1:T(8,128)}, f32[2048,512]{0,1:T(8,128)S(1)}, u32[]{:S(2)}) copy-start(f32[2048,512]{0,1:T(8,128)S(1)} %get-tuple-element.81) | copy-start | bytes 12582916
  99.9 22.6 %copy-start.7 = (f32[2,4,16,16]{3,2,1,0:T(8,128)S(1)}, f32[2,4,16,16]{3,2,1,0:T(8,128)}, u32[]{:S(2)}) copy-start(f32[2,4,16,16]{3,2,1,0:T(8,128)} %param.41) | copy-start | bytes 24580
  100.2 28.3 %copy-start.9 = (f32[4,16,16]{2,1,0:T(8,128)S(1)}, f32[4,16,16]{2,1,0:T(8,128)}, u32[]{:S(2)}) copy-start(f32[4,16,16]{2,1,0:T(8,128)} %param.42) | copy-start | bytes 12292
  131.0 3.2 %copy-start.12 = (bf16[64,128]{1,0:T(8,128)(2,1)S(1)}, bf16[64,128]{1,0:T(8,128)(2,1)}, u32[]{:S(2)}) copy-start(bf16[64,128]{1,0:T(8,128)(2,1)} %param.43) | copy-start | bytes 49156
where the time goes:
time: 138 us; the launch traced here: 137 us
  matrix products  48 us (35%)
  Pallas kernels  36.3 us (26%)
  other arithmetic  20.8 us (15%)
  blocking collectives  19.9 us (14%)
  local copies, waits for them, and re-layouts  10.5 us (8%)
  between operations  1.85 us (1%)
    pallas_call x1, Pallas kernels, exchange_halos(): pl.pallas_call(functools.partial(_halo_kernel, offsets), out_shape=jax.Sh...  19.6 us
    pallas_call x1, Pallas kernels, dom_sum(): pl.pallas_call(functools.partial(_radix_kernel, radix, steps), out_shape=...  16.7 us
    dot_general x2, matrix products, gather_rows(): picked = jnp.dot(hot, wide, preferred_element_type=jnp.float32)  13.7 us
    unnamed x5, blocking collectives  12.2 us
    select_n x2, other arithmetic, scatter_rows(): jnp.where((lane == j)[:, None], messages, jnp.zeros_like(messages))  10.5 us
    dot_general x1, matrix products, step(): jnp.dot(sender_rows, link_layer_alpha[feature_width:2 * feature_width], p...  8.14 us
    psum x1, blocking collectives, body(): summed = lax.psum(total, 'head')  7.67 us
    dot_general x1, matrix products, step(): jnp.dot(first, link_layer_beta, preferred_element_type=jnp.float32)  5.61 us

commit v1 on v0

--- a/solution.py
+++ b/solution.py
@@ -88,35 +88,52 @@
     )(flat)
 
 
-def _halo_kernel(offsets, own_ref, out_ref, ext_ref, send_sem, recv_sem):
+def _halo_kernel(offsets, own_ref, out_ref, ext_ref, send_sem, recv_sem, pass_sem, land_sem):
     me = lax.axis_index("dom")
     count = lax.axis_size("dom")
+    core = lax.axis_index("head")
+    sibling = 1 - core
     rows = own_ref.shape[0]
     halo = out_ref.shape[1]
+    half = halo // 2
+    mesh_ids = pl.DeviceIdType.MESH
     barrier = pltpu.get_barrier_semaphore()
     for offset in offsets:
         pl.semaphore_signal(
-            barrier,
-            1,
-            device_id={"dom": (me + offset + count) % count},
-            device_id_type=pl.DeviceIdType.MESH,
-        )
-    pl.semaphore_wait(barrier, len(offsets))
-    copies = []
+            barrier, 1, device_id={"dom": (me + offset + count) % count}, device_id_type=mesh_ids
+        )
+    pl.semaphore_signal(barrier, 1, device_id={"head": sibling}, device_id_type=mesh_ids)
+    pl.semaphore_wait(barrier, len(offsets) + 1)
+    sends = []
     for k, offset in enumerate(offsets):
         copy = pltpu.make_async_remote_copy(
-            src_ref=out_ref.at[k],
-            dst_ref=ext_ref.at[pl.ds(rows + k * halo, halo)],
+            src_ref=out_ref.at[k, pl.ds(core * half, half)],
+            dst_ref=ext_ref.at[pl.ds(rows + k * halo + core * half, half)],
             send_sem=send_sem.at[k],
             recv_sem=recv_sem.at[k],
             device_id={"dom": (me + offset + count) % count},
-            device_id_type=pl.DeviceIdType.MESH,
+            device_id_type=mesh_ids,
         )
         copy.start()
-        copies.append(copy)
+        sends.append(copy)
     ext_ref[pl.ds(0, rows)] = own_ref[...]
-    for copy in copies:
-        copy.wait()
+    passes = []
+    for k in range(len(offsets)):
+        sends[k].wait_recv()
+        forward = pltpu.make_async_remote_copy(
+            src_ref=ext_ref.at[pl.ds(rows + k * halo + core * half, half)],
+            dst_ref=ext_ref.at[pl.ds(rows + k * halo + core * half, half)],
+            send_sem=pass_sem.at[k],
+            recv_sem=land_sem.at[k],
+            device_id={"head": sibling},
+            device_id_type=mesh_ids,
+        )
+        forward.start()
+        passes.append(forward)
+    for copy in sends:
+        copy.wait_send()
+    for forward in passes:
+        forward.wait()
     for k, offset in enumerate(offsets):
         if offset > 0:
             inside = (me + count - offset) // count
@@ -134,10 +151,7 @@
         out_shape=jax.ShapeDtypeStruct((total, own_rows.shape[1]), own_rows.dtype),
         in_specs=[pl.BlockSpec(memory_space=pltpu.VMEM)] * 2,
         out_specs=pl.BlockSpec(memory_space=pltpu.VMEM),
-        scratch_shapes=[
-            pltpu.SemaphoreType.DMA((len(offsets),)),
-            pltpu.SemaphoreType.DMA((len(offsets),)),
-        ],
+        scratch_shapes=[pltpu.SemaphoreType.DMA((len(offsets),))] * 4,
         compiler_params=pltpu.CompilerParams(collective_id=1, has_side_effects=True),
     )(own_rows, outgoing)
 

time: 138 us -> 135 us (0.978)
  Pallas kernels: 36.3 us -> 34.2 us
    psum x1, blocking collectives: 7.67 us -> 6.26 us  [body(): summed = lax.psum(total, 'head')]
where the time goes in v1:
time: 135 us; the launch traced here: 134 us
  matrix products  48 us (36%)
  Pallas kernels  34.2 us (25%)
  other arithmetic  20.8 us (15%)
  blocking collectives  18.7 us (14%)
  local copies, waits for them, and re-layouts  10.5 us (8%)
  between operations  1.85 us (1%)
    pallas_call x1, Pallas kernels, exchange_halos(): pl.pallas_call(functools.partial(_halo_kernel, offsets), out_shape=jax.Sh...  18.8 us
    pallas_call x1, Pallas kernels, dom_sum(): pl.pallas_call(functools.partial(_radix_kernel, radix, steps), out_shape=...  15.4 us
    dot_general x2, matrix products, gather_rows(): picked = jnp.dot(hot, wide, preferred_element_type=jnp.float32)  13.7 us
    unnamed x5, blocking collectives  12.4 us
    select_n x2, other arithmetic, scatter_rows(): jnp.where((lane == j)[:, None], messages, jnp.zeros_like(messages))  10.5 us
    dot_general x1, matrix products, step(): jnp.dot(sender_rows, link_layer_alpha[feature_width:2 * feature_width], p...  8.14 us
    psum x1, blocking collectives, body(): summed = lax.psum(total, 'head')  6.26 us
    dot_general x1, matrix products, step(): jnp.dot(first, link_layer_beta, preferred_element_type=jnp.float32)  5.61 us

profile of v1, /device:TPU:1, one launch (start us, length us, event | category | flops | bytes accessed | tf_op | source)
XLA Modules:
  0.0 134.1 jit_solution(6318444671727262342)
XLA Ops:
  3.9 4.7 %fusion.25 = bf16[2048,128]{1,0:T(8,128)(2,1)} fusion(bf16[2048,128]{1,0:T(8,128)(2,1)} %own_ref.1, s32[2048]{0:T(1024)S(1)} %bitcast.60), kind=kOutput, calls=%fused_computation.42 | convolution fusion | flops 1078198272 | bytes 1056768 | tf_op jit(solution)/shard_map/dot_general | solution.py:258
  8.6 18.8 %shard_map.199 = bf16[4096,128]{1,0:T(8,128)(2,1)} custom-call(bf16[2048,128]{1,0:T(8,128)(2,1)} %own_ref.1, bf16[4,512,128]{2,1,0:T(8,128)(2,1)} %bitcast.58), custom_call_target="tpu_custom_call" | custom-call | tf_op jit(solution)/shard_map/pallas_call | solution.py:149
  27.4 1.7 %reshape.172 = bf16[1024,512]{1,0:T(8,128)(2,1)S(1)} reshape(bf16[4096,128]{1,0:T(8,128)(2,1)} %shard_map.199) | data formatting | bytes 2097152 | tf_op jit(solution)/shard_map/while/body/eval_jaxpr/reshape | solution.py:263
  29.1 8.4 %fusion = bf16[6144,512]{1,0:T(8,128)(2,1)S(1)} fusion(bf16[1024,512]{1,0:T(8,128)(2,1)S(1)} %reshape.172, s32[6144]{0:T(1024)S(1)} %get-tuple-element.84), kind=kOutput, calls=%fused_computation.1 | convolution fusion | flops 6448742400 | bytes 7364608 | tf_op jit(solution)/shard_map/while/body/eval_jaxpr/dot_general | solution.py:267
  38.1 8.1 %convolution_add_fusion.1 = f32[6144,128]{1,0:T(8,128)} fusion(f32[6144,128]{1,0:T(8,128)S(1)} %fusion.41, bf16[6144,512]{1,0:T(8,128)(2,1)S(1)} %fusion, pred[6144]{0:T(1024)(128)(4,1)S(1)} %get-tuple-element.75, pred[6144]{0:T(1024)(128)(4,1)S(1)} %get-tuple-element.74, pred[6144]{0:T(1024)(128)(4,1)S(1)} %get-tuple-element.65, ...), kind=kOutput, calls=%fused_computation.10 | convolution fusion | flops 204472320 | bytes 12634112 | tf_op jit(solution)/shard_map/while/body/eval_jaxpr/dot_general | solution.py:342
  46.6 5.3 %fusion.4 = bf16[6144,512]{1,0:T(8,128)(2,1)} fusion(bf16[512,512]{1,0:T(8,128)(2,1)S(1)} %reshape.173, s32[6144]{0:T(1024)S(1)} %get-tuple-element.85), kind=kOutput, calls=%fused_computation.7 | convolution fusion | flops 3224371200 | bytes 6840320 | tf_op jit(solution)/shard_map/while/body/eval_jaxpr/dot_general | solution.py:267
  51.9 5.6 %multiply_convert_fusion = bf16[6144,128]{1,0:T(8,128)(2,1)S(1)} fusion(bf16[128,128]{1,0:T(8,128)(2,1)S(1)} %copy-done.17, f32[6144,128]{1,0:T(8,128)} %convolution_add_fusion.1, bf16[6144,512]{1,0:T(8,128)(2,1)} %fusion.4, pred[6144]{0:T(1024)(128)(4,1)S(1)} %get-tuple-element.86, pred[6144]{0:T(1024)(128)(4,1)S(1)} %get-tuple-element.87, ...), kind=kOutput, calls=%fused_computation.37 | convolution fusion | flops 413663232 | bytes 11094016 | tf_op jit(solution)/shard_map/while/body/eval_jaxpr/dot_general | solution.py:352
  57.5 2.3 %fusion.84 = (f32[6144]{0:T(1024)S(1)}, f32[6144,128]{0,1:T(8,128)}) fusion(bf16[6144,128]{1,0:T(8,128)(2,1)S(1)} %multiply_convert_fusion, bf16[128,128]{1,0:T(8,128)(2,1)S(1)} %copy-done), kind=kOutput, calls=%fused_computation.136 | convolution fusion | flops 202106880 | bytes 4775936 | tf_op jit(solution)/shard_map/while/body/eval_jaxpr/dot_general | solution.py:354
  59.8 2.4 %copy.43 = f32[6144,128]{1,0:T(8,128)S(1)} copy(f32[6144,128]{0,1:T(8,128)} %get-tuple-element.77) | data formatting | bytes 6291456 | tf_op jit(solution)/shard_map/while/body/eval_jaxpr/dot_general | solution.py:354
  62.2 1.8 %multiply_reduce_fusion = f32[6144]{0:T(1024)S(1)} fusion(f32[6144,128]{1,0:T(8,128)S(1)} %copy.43, f32[6144]{0:T(1024)S(1)} %broadcast_multiply_fusion), kind=kLoop, calls=%fused_computation.36 | loop fusion | flops 2353152 | bytes 3194880 | tf_op jit(solution)/shard_map/while/body/eval_jaxpr/reduce_sum | solution.py:174
  64.7 5.7 %broadcast_select_fusion.3 = (bf16[6144,128]{1,0:T(8,128)(2,1)S(1)}, bf16[6144,128]{1,0:T(8,128)(2,1)S(1)}) fusion(pred[6144]{0:T(1024)(128)(4,1)S(1)} %get-tuple-element.62, f32[128]{0:T(128)S(1)} %copy-done.14, f32[6144]{0:T(1024)S(1)} %add_rsqrt_fusion, f32[6144,128]{1,0:T(8,128)S(1)} %copy.43, f32[6144]{0:T(1024)S(1)} %broadcast_multiply_fusion, ...), kind=kLoop, calls=%fused_computation.60 | loop fusion | flops 6291456 | bytes 7926276 | tf_op jit(solution)/shard_map/while/body/eval_jaxpr/jit(_where)/select_n | solution.py:279
  70.4 4.8 %broadcast_select_fusion = (bf16[6144,128]{1,0:T(8,128)(2,1)S(1)}, bf16[6144,128]{1,0:T(8,128)(2,1)S(1)}, bf16[6144,128]{1,0:T(8,128)(2,1)S(1)}) fusion(bf16[6144,128]{1,0:T(8,128)(2,1)S(1)} %get-tuple-element.61, pred[6144]{0:T(1024)(128)(4,1)S(1)} %get-tuple-element.86, pred[6144]{0:T(1024)(128)(4,1)S(1)} %get-tuple-element.87, ...), kind=kLoop, calls=%fused_computation.51 | loop fusion | flops 2359296 | bytes 6309888 | tf_op jit(solution)/shard_map/while/body/eval_jaxpr/jit(_where)/select_n | solution.py:279
  75.3 4.3 %fusion.3 = f32[512,512]{1,0:T(8,128)S(1)} fusion(bf16[6144,128]{1,0:T(8,128)(2,1)S(1)} %get-tuple-element.70, bf16[6144,128]{1,0:T(8,128)(2,1)S(1)} %get-tuple-element.69, bf16[6144,128]{1,0:T(8,128)(2,1)S(1)} %get-tuple-element.68, bf16[6144,128]{1,0:T(8,128)(2,1)S(1)} %get-tuple-element.60, s32[6144]{0:T(1024)S(1)} %get-tuple-element.85), kind=kOutput, calls=%fused_computation.6 | convolution fusion | flops 3249537024 | bytes 7364608 | tf_op jit(solution)/shard_map/while/body/eval_jaxpr/dot_general | solution.py:285
  81.2 6.3 %all-reduce.4 = (bf16[2048,128]{1,0:T(8,128)(2,1)S(1)}, f32[8]{0:T(128)S(1)}) all-reduce(f32[2048,128]{1,0:T(8,128)S(1)} %reshape.174, f32[8]{0:T(128)S(1)} %dynamic-update-slice.2), channel_id=1, replica_groups=mesh['dom'=64,'head'=2] {'head'}, use_global_device_ids=true, to_apply=%region_2.3 | all-reduce | flops 262152 | bytes 1572928 | tf_op jit(solution)/shard_map/psum | solution.py:368
  89.8 1.9 %all-gather = bf16[128,128]{0,1:T(8,128)(2,1)S(1)} all-gather(bf16[128,64]{0,1:T(8,128)(2,1)S(1)} %copy-done.11), channel_id=3, replica_groups=mesh['dom'=64,'head'=2] {'head'}, dimensions={1}, use_global_device_ids=true | all-gather | bytes 49152 | tf_op args[15]
  92.1 1.9 %all-gather.1 = bf16[128,512]{1,0:T(8,128)(2,1)S(1)} all-gather(bf16[128,256]{1,0:T(8,128)(2,1)S(1)} %copy-done.6), channel_id=4, replica_groups=mesh['dom'=64,'head'=2] {'head'}, dimensions={1}, use_global_device_ids=true | all-gather | bytes 196608 | tf_op args[16]
  95.6 1.1 copy-done.1
  98.0 3.2 %fusion.16 = f32[512]{0:T(512)S(1)} fusion(f32[2048,512]{0,1:T(8,128)} %copy-done.1, f32[512]{0:T(512)S(1)} %div.136, f32[2048,8]{0,1:T(8,128)S(1)} %fusion.17, f32[2048,8]{0,1:T(8,128)S(1)} %get-tuple-element.80), kind=kLoop, calls=%fused_computation.25 | loop fusion | flops 4193792 | bytes 4329472 | tf_op jit(solution)/shard_map/reduce_sum | solution.py:233
  101.8 15.4 %shard_map.200 = f32[72,128]{1,0:T(8,128)} custom-call(f32[72,128]{1,0:T(8,128)} %fusion.61.x_ref), custom_call_target="tpu_custom_call" | custom-call | tf_op jit(solution)/shard_map/pallas_call | solution.py:77
  119.1 5.0 %all-gather.3 = f32[2,8,16,16]{2,3,1,0:T(8,128)S(1)} all-gather(f32[2,4,16,16]{2,3,1,0:T(8,128)S(1)} %copy.46), channel_id=6, replica_groups=mesh['dom'=64,'head'=2] {'head'}, dimensions={1}, use_global_device_ids=true | all-gather | bytes 24576 | tf_op args[18]
  125.2 1.9 %all-gather.4 = f32[8,16,16]{2,1,0:T(8,128)S(1)} all-gather(f32[4,16,16]{2,1,0:T(8,128)S(1)} %copy-done.9), channel_id=7, replica_groups=mesh['dom'=64,'head'=2] {'head'}, dimensions={0}, use_global_device_ids=true | all-gather | bytes 12288 | tf_op args[19]
  127.8 3.2 %convolution_convert_fusion.1 = bf16[8,16,2048]{2,1,0:T(8,128)(2,1)S(1)} fusion(bf16[8,64,16]{1,2,0:T(8,128)(2,1)S(1)} %convolution_convert_fusion.2, f32[2048,8]{0,1:T(8,128)S(1)} %fusion.17, f32[2048,8]{0,1:T(8,128)S(1)} %get-tuple-element.80, f32[8]{0:T(128)S(1)} %get-tuple-element.57, f32[2048,512]{0,1:T(8,128)} %copy-done.1), kind=kOutput, calls=%fused_computation.44 | convolution fusion | flops 38010880 | bytes 4866080 | tf_op jit(solution)/shard_map/nhs,hsd->nhd/dot_general | solution.py:251
  130.9 1.8 %all-gather.5 = bf16[128,128]{1,0:T(8,128)(2,1)S(1)} all-gather(bf16[64,128]{1,0:T(8,128)(2,1)S(1)} %copy-done.12), channel_id=8, replica_groups=mesh['dom'=64,'head'=2] {'head'}, dimensions={0}, use_global_device_ids=true | all-gather | bytes 49152 | tf_op args[20]
  133.1 1.0 copy.50
  (87 shorter events, 15.7 us)
Async XLA Ops:
  0.0 57.5 %copy-start = (bf16[128,128]{1,0:T(8,128)(2,1)S(1)}, bf16[128,128]{1,0:T(8,128)(2,1)}, u32[]{:S(2)}) copy-start(bf16[128,128]{1,0:T(8,128)(2,1)} %param.31) | copy-start | bytes 98308
  29.1 8.4 %copy-start.4 = (bf16[12288,128]{1,0:T(8,128)(2,1)S(1)}, bf16[12288,128]{1,0:T(8,128)(2,1)}, u32[]{:S(2)}) copy-start(bf16[12288,128]{1,0:T(8,128)(2,1)} %param.24) | copy-start | bytes 9437188
  29.1 8.4 %copy-start.13 = (bf16[384,128]{1,0:T(8,128)(2,1)S(1)}, bf16[384,128]{1,0:T(8,128)(2,1)}, u32[]{:S(2)}) copy-start(bf16[384,128]{1,0:T(8,128)(2,1)} %param.29) | copy-start | bytes 294916
  38.1 8.2 %copy-start.2 = (bf16[2048,128]{1,0:T(8,128)(2,1)S(1)}, bf16[2048,128]{1,0:T(8,128)(2,1)}, u32[]{:S(2)}) copy-start(bf16[2048,128]{1,0:T(8,128)(2,1)} %own_ref.1) | copy-start | bytes 1572868
  46.6 5.3 %copy-start.17 = (bf16[128,128]{1,0:T(8,128)(2,1)S(1)}, bf16[128,128]{1,0:T(8,128)(2,1)}, u32[]{:S(2)}) copy-start(bf16[128,128]{1,0:T(8,128)(2,1)} %param.30) | copy-start | bytes 98308
  62.2 2.6 %copy-start.5 = (bf16[12288,128]{1,0:T(8,128)(2,1)S(1)}, bf16[12288,128]{1,0:T(8,128)(2,1)}, u32[]{:S(2)}) copy-start(bf16[12288,128]{1,0:T(8,128)(2,1)} %param.24) | copy-start | bytes 9437188
  62.2 2.6 %copy-start.14 = (f32[128]{0:T(128)S(1)}, f32[128]{0:T(128)}, u32[]{:S(2)}) copy-start(f32[128]{0:T(128)} %param.32) | copy-start | bytes 1540
  75.2 4.5 %copy-start.20 = (u32[128]{0:T(128)S(1)}, u32[128]{0:T(128)}, u32[]{:S(2)}) copy-start(u32[128]{0:T(128)} %constant.143) | copy-start | bytes 1540
  75.3 5.7 %copy-start.19 = (f32[4]{0:T(128)S(1)}, f32[4]{0:T(128)}, u32[]{:S(2)}) copy-start(f32[4]{0:T(128)} %param.40) | copy-start | bytes 52
  79.6 7.9 %copy-start.3 = (bf16[2048,128]{1,0:T(8,128)(2,1)S(1)}, bf16[2048,128]{1,0:T(8,128)(2,1)}, u32[]{:S(2)}) copy-start(bf16[2048,128]{1,0:T(8,128)(2,1)} %own_ref.1) | copy-start | bytes 1572868
  79.6 7.9 %copy-start.10 = (bf16[256,128]{1,0:T(8,128)(2,1)S(1)}, bf16[256,128]{1,0:T(8,128)(2,1)}, u32[]{:S(2)}) copy-start(bf16[256,128]{1,0:T(8,128)(2,1)} %param.33) | copy-start | bytes 196612
  79.6 8.2 %copy-start.18 = (bf16[128,128]{1,0:T(8,128)(2,1)S(1)}, bf16[128,128]{1,0:T(8,128)(2,1)}, u32[]{:S(2)}) copy-start(bf16[128,128]{1,0:T(8,128)(2,1)} %param.34) | copy-start | bytes 98308
  87.8 0.8 copy-start.8
  88.6 0.8 copy-start.15
  88.6 1.2 copy-start.11
  88.6 3.1 %copy-start.16 = (f32[128]{0:T(128)S(1)}, f32[128]{0:T(128)}, u32[]{:S(2)}) copy-start(f32[128]{0:T(128)} %param.37) | copy-start | bytes 1540
  88.9 3.1 %copy-start.6 = (bf16[128,256]{1,0:T(8,128)(2,1)S(1)}, bf16[128,256]{1,0:T(8,128)(2,1)}, u32[]{:S(2)}) copy-start(bf16[128,256]{1,0:T(8,128)(2,1)} %param.39) | copy-start | bytes 196612
  94.8 1.9 %copy-start.1 = (f32[2048,512]{0,1:T(8,128)}, f32[2048,512]{0,1:T(8,128)S(1)}, u32[]{:S(2)}) copy-start(f32[2048,512]{0,1:T(8,128)S(1)} %get-tuple-element.81) | copy-start | bytes 12582916
  97.7 21.4 %copy-start.7 = (f32[2,4,16,16]{3,2,1,0:T(8,128)S(1)}, f32[2,4,16,16]{3,2,1,0:T(8,128)}, u32[]{:S(2)}) copy-start(f32[2,4,16,16]{3,2,1,0:T(8,128)} %param.41) | copy-start | bytes 24580
  98.0 27.2 %copy-start.9 = (f32[4,16,16]{2,1,0:T(8,128)S(1)}, f32[4,16,16]{2,1,0:T(8,128)}, u32[]{:S(2)}) copy-start(f32[4,16,16]{2,1,0:T(8,128)} %param.42) | copy-start | bytes 12292
  127.7 3.2 %copy-start.12 = (bf16[64,128]{1,0:T(8,128)(2,1)S(1)}, bf16[64,128]{1,0:T(8,128)(2,1)}, u32[]{:S(2)}) copy-start(bf16[64,128]{1,0:T(8,128)(2,1)} %param.43) | copy-start | bytes 49156

commit v2 on v1

--- a/solution.py
+++ b/solution.py
@@ -156,6 +156,42 @@
     )(own_rows, outgoing)
 
 
+def _sibling_kernel(x_ref, o_ref, inbox, send_sem, recv_sem):
+    sibling = 1 - lax.axis_index("head")
+    mesh_ids = pl.DeviceIdType.MESH
+    barrier = pltpu.get_barrier_semaphore()
+    pl.semaphore_signal(barrier, 1, device_id={"head": sibling}, device_id_type=mesh_ids)
+    pl.semaphore_wait(barrier, 1)
+    copy = pltpu.make_async_remote_copy(
+        src_ref=x_ref,
+        dst_ref=inbox,
+        send_sem=send_sem,
+        recv_sem=recv_sem,
+        device_id={"head": sibling},
+        device_id_type=mesh_ids,
+    )
+    copy.start()
+    copy.wait()
+    o_ref[...] = x_ref[...] + inbox[...]
+
+
+def sibling_sum(x, collective_id):
+    return pl.pallas_call(
+        _sibling_kernel,
+        out_shape=jax.ShapeDtypeStruct(x.shape, x.dtype),
+        in_specs=[pl.BlockSpec(memory_space=pltpu.VMEM)],
+        out_specs=pl.BlockSpec(memory_space=pltpu.VMEM),
+        scratch_shapes=[
+            pltpu.VMEM(x.shape, x.dtype),
+            pltpu.SemaphoreType.DMA(()),
+            pltpu.SemaphoreType.DMA(()),
+        ],
+        compiler_params=pltpu.CompilerParams(
+            collective_id=collective_id, has_side_effects=True
+        ),
+    )(x)
+
+
 def psum_slices(numer, denom):
     joined = jnp.concatenate([numer.reshape(-1), denom.reshape(-1)])
     rows = -(-joined.shape[0] // 1024) * 8
@@ -365,7 +401,7 @@
     total, unused = lax.scan(
         step, start, (edge_blocks, send_blocks, recv_blocks, jnp.arange(turns, dtype=jnp.int32))
     )
-    summed = lax.psum(total, "head")
+    summed = sibling_sum(total, 2)
     refreshed_vertices = node_section(
         vertex_state,
         summed.astype(jnp.bfloat16),
@@ -384,7 +420,9 @@
     numer, denom = psum_slices(numer, denom)
     slice_out = slice_mixing(numer, denom, cluster_probe_lookup, cluster_content_linear)
     attended = attend_rows(weights_b, slice_out)
-    projected = jnp.dot(attended, closing_linear_factor, preferred_element_type=jnp.float32)
+    projected = sibling_sum(
+        jnp.dot(attended, closing_linear_factor, preferred_element_type=jnp.float32), 3
+    )
     return (refreshed_vertices.astype(jnp.float32) + projected).astype(jnp.bfloat16)
 
 
@@ -405,12 +443,12 @@
         P(),
         P(),
         P(),
-        P(),
-        P(),
-        P(),
-        P(),
-        P(),
-        P(),
+        P(None, "head"),
+        P(None, "head"),
+        P("head"),
+        P(None, "head", None, None),
+        P("head", None, None),
+        P("head", None),
     )
     out_specs = P("dom", None)
     return jax.shard_map(body, mesh=mesh, in_specs=in_specs, out_specs=out_specs, check_vma=False)

time: 135 us -> 126 us (0.933)
  blocking collectives: 18.7 us -> 0 us
  Pallas kernels: 34.2 us -> 45.9 us
  local copies, waits for them, and re-layouts: 10.5 us -> 8.54 us
    pallas_call x0 -> x2, Pallas kernels: none -> 12.8 us  [sibling_sum(): pl.pallas_call(_sibling_kernel, out_shape=jax.ShapeDtypeStruct(x.shape, x...]
    unnamed x5 -> x0, blocking collectives: 12.4 us -> none
    psum x1 -> x0, blocking collectives: 6.26 us -> none  [body(): summed = lax.psum(total, 'head')]
    reduce_sum x1, other arithmetic: 3.2 us -> 0.59 us  [slice_partial_terms(): denom = jnp.sum(weights, axis=0)]
    dot_general x1, matrix products: 3.16 us -> 0.58 us  [attend_rows(): jnp.einsum('nhs,hsd->nhd', weights_b, slice_out, preferred_element_type=j...]
    convert_element_type x0 -> x1, other arithmetic: none -> 2.12 us  [body(): (refreshed_vertices.astype(jnp.float32) + projected).astype(jnp.bfloat16)]
    unnamed x48 -> x39, local copies, waits for them, and re-layouts: 3.03 us -> 0.96 us
where the time goes in v2:
time: 126 us
  matrix products  48 us (38%)
  Pallas kernels  45.9 us (36%)
  other arithmetic  21.9 us (17%)
  local copies, waits for them, and re-layouts  8.54 us (7%)
    pallas_call x1, Pallas kernels, exchange_halos(): pl.pallas_call(functools.partial(_halo_kernel, offsets), out_shape=jax.Sh...  18.8 us
    pallas_call x1, Pallas kernels, dom_sum(): pl.pallas_call(functools.partial(_radix_kernel, radix, steps), out_shape=...  14.3 us
    dot_general x2, matrix products, gather_rows(): picked = jnp.dot(hot, wide, preferred_element_type=jnp.float32)  13.7 us
    pallas_call x2, Pallas kernels, sibling_sum(): pl.pallas_call(_sibling_kernel, out_shape=jax.ShapeDtypeStruct(x.shape, x...  12.8 us
    select_n x2, other arithmetic, scatter_rows(): jnp.where((lane == j)[:, None], messages, jnp.zeros_like(messages))  10.5 us
    dot_general x1, matrix products, step(): jnp.dot(sender_rows, link_layer_alpha[feature_width:2 * feature_width], p...  8.14 us
    dot_general x1, matrix products, step(): jnp.dot(first, link_layer_beta, preferred_element_type=jnp.float32)  5.62 us
    dot_general x1, matrix products, pick_rows(): jnp.dot(selector, table, preferred_element_type=jnp.float32)  4.7 us

profile of v2, /device:TPU:1, one launch (start us, length us, event | category | flops | bytes accessed | tf_op | source)
XLA Modules:
  0.0 125.5 jit_solution(6781880754988494713)
XLA Ops:
  1.6 0.8 broadcast_compare_fusion.1
  2.4 0.8 add_select_fusion
  3.9 4.7 %fusion.21 = bf16[2048,128]{1,0:T(8,128)(2,1)} fusion(bf16[2048,128]{1,0:T(8,128)(2,1)} %own_ref.1, s32[2048]{0:T(1024)S(1)} %bitcast.58), kind=kOutput, calls=%fused_computation.33 | convolution fusion | flops 1078198272 | bytes 1056768 | tf_op jit(solution)/shard_map/dot_general | solution.py:294
  8.6 18.8 %shard_map.199 = bf16[4096,128]{1,0:T(8,128)(2,1)} custom-call(bf16[2048,128]{1,0:T(8,128)(2,1)} %own_ref.1, bf16[4,512,128]{2,1,0:T(8,128)(2,1)} %bitcast.55), custom_call_target="tpu_custom_call" | custom-call | tf_op jit(solution)/shard_map/pallas_call | solution.py:149
  27.4 1.7 %reshape.172 = bf16[1024,512]{1,0:T(8,128)(2,1)S(1)} reshape(bf16[4096,128]{1,0:T(8,128)(2,1)} %shard_map.199) | data formatting | bytes 2097152 | tf_op jit(solution)/shard_map/while/body/eval_jaxpr/reshape | solution.py:299
  29.1 8.4 %fusion = bf16[6144,512]{1,0:T(8,128)(2,1)S(1)} fusion(bf16[1024,512]{1,0:T(8,128)(2,1)S(1)} %reshape.172, s32[6144]{0:T(1024)S(1)} %get-tuple-element.82), kind=kOutput, calls=%fused_computation.1 | convolution fusion | flops 6448742400 | bytes 7364608 | tf_op jit(solution)/shard_map/while/body/eval_jaxpr/dot_general | solution.py:303
  38.1 8.1 %convolution_add_fusion.1 = f32[6144,128]{1,0:T(8,128)} fusion(f32[6144,128]{1,0:T(8,128)S(1)} %fusion.40, bf16[6144,512]{1,0:T(8,128)(2,1)S(1)} %fusion, pred[6144]{0:T(1024)(128)(4,1)S(1)} %get-tuple-element.73, pred[6144]{0:T(1024)(128)(4,1)S(1)} %get-tuple-element.72, pred[6144]{0:T(1024)(128)(4,1)S(1)} %get-tuple-element.63, ...), kind=kOutput, calls=%fused_computation.10 | convolution fusion | flops 204472320 | bytes 12634112 | tf_op jit(solution)/shard_map/while/body/eval_jaxpr/dot_general | solution.py:378
  46.6 5.3 %fusion.4 = bf16[6144,512]{1,0:T(8,128)(2,1)} fusion(bf16[512,512]{1,0:T(8,128)(2,1)S(1)} %reshape.173, s32[6144]{0:T(1024)S(1)} %get-tuple-element.83), kind=kOutput, calls=%fused_computation.7 | convolution fusion | flops 3224371200 | bytes 6840320 | tf_op jit(solution)/shard_map/while/body/eval_jaxpr/dot_general | solution.py:303
  51.9 5.6 %multiply_convert_fusion = bf16[6144,128]{1,0:T(8,128)(2,1)S(1)} fusion(bf16[128,128]{1,0:T(8,128)(2,1)S(1)} %copy-done.15, f32[6144,128]{1,0:T(8,128)} %convolution_add_fusion.1, bf16[6144,512]{1,0:T(8,128)(2,1)} %fusion.4, pred[6144]{0:T(1024)(128)(4,1)S(1)} %get-tuple-element.84, pred[6144]{0:T(1024)(128)(4,1)S(1)} %get-tuple-element.85, ...), kind=kOutput, calls=%fused_computation.30 | convolution fusion | flops 413663232 | bytes 11094016 | tf_op jit(solution)/shard_map/while/body/eval_jaxpr/dot_general | solution.py:388
  57.5 2.3 %fusion.88 = (f32[6144]{0:T(1024)S(1)}, f32[6144,128]{0,1:T(8,128)}) fusion(bf16[6144,128]{1,0:T(8,128)(2,1)S(1)} %multiply_convert_fusion, bf16[128,128]{1,0:T(8,128)(2,1)S(1)} %copy-done.5), kind=kOutput, calls=%fused_computation.138 | convolution fusion | flops 202106880 | bytes 4775936 | tf_op jit(solution)/shard_map/while/body/eval_jaxpr/dot_general | solution.py:390
  59.8 2.4 %copy.24 = f32[6144,128]{1,0:T(8,128)S(1)} copy(f32[6144,128]{0,1:T(8,128)} %get-tuple-element.75) | data formatting | bytes 6291456 | tf_op jit(solution)/shard_map/while/body/eval_jaxpr/dot_general | solution.py:390
  62.2 1.8 %multiply_reduce_fusion = f32[6144]{0:T(1024)S(1)} fusion(f32[6144,128]{1,0:T(8,128)S(1)} %copy.24, f32[6144]{0:T(1024)S(1)} %broadcast_multiply_fusion), kind=kLoop, calls=%fused_computation.29 | loop fusion | flops 2353152 | bytes 3194880 | tf_op jit(solution)/shard_map/while/body/eval_jaxpr/reduce_sum | solution.py:210
  64.8 5.7 %broadcast_select_fusion.3 = (bf16[6144,128]{1,0:T(8,128)(2,1)S(1)}, bf16[6144,128]{1,0:T(8,128)(2,1)S(1)}) fusion(pred[6144]{0:T(1024)(128)(4,1)S(1)} %get-tuple-element.60, f32[128]{0:T(128)S(1)} %copy-done.11, f32[6144]{0:T(1024)S(1)} %add_rsqrt_fusion, f32[6144,128]{1,0:T(8,128)S(1)} %copy.24, f32[6144]{0:T(1024)S(1)} %broadcast_multiply_fusion, ...), kind=kLoop, calls=%fused_computation.58 | loop fusion | flops 6291456 | bytes 7926276 | tf_op jit(solution)/shard_map/while/body/eval_jaxpr/jit(_where)/select_n | solution.py:315
  70.4 4.8 %broadcast_select_fusion = (bf16[6144,128]{1,0:T(8,128)(2,1)S(1)}, bf16[6144,128]{1,0:T(8,128)(2,1)S(1)}, bf16[6144,128]{1,0:T(8,128)(2,1)S(1)}) fusion(bf16[6144,128]{1,0:T(8,128)(2,1)S(1)} %get-tuple-element.59, pred[6144]{0:T(1024)(128)(4,1)S(1)} %get-tuple-element.84, pred[6144]{0:T(1024)(128)(4,1)S(1)} %get-tuple-element.85, ...), kind=kLoop, calls=%fused_computation.49 | loop fusion | flops 2359296 | bytes 6309888 | tf_op jit(solution)/shard_map/while/body/eval_jaxpr/jit(_where)/select_n | solution.py:315
  75.3 4.3 %fusion.3 = f32[512,512]{1,0:T(8,128)S(1)} fusion(bf16[6144,128]{1,0:T(8,128)(2,1)S(1)} %get-tuple-element.68, bf16[6144,128]{1,0:T(8,128)(2,1)S(1)} %get-tuple-element.67, bf16[6144,128]{1,0:T(8,128)(2,1)S(1)} %get-tuple-element.66, bf16[6144,128]{1,0:T(8,128)(2,1)S(1)} %get-tuple-element.58, s32[6144]{0:T(1024)S(1)} %get-tuple-element.83), kind=kOutput, calls=%fused_computation.6 | convolution fusion | flops 3249537024 | bytes 7364608 | tf_op jit(solution)/shard_map/while/body/eval_jaxpr/dot_general | solution.py:321
  79.6 1.1 reshape.174.x_ref
  80.7 5.0 %shard_map.200 = f32[2048,128]{1,0:T(8,128)} custom-call(f32[2048,128]{1,0:T(8,128)} %reshape.174.x_ref), custom_call_target="tpu_custom_call" | custom-call | tf_op jit(solution)/shard_map/pallas_call | solution.py:179
  86.1 1.9 %multiply_convert_fusion.2 = bf16[2048,128]{1,0:T(8,128)(2,1)S(1)} fusion(bf16[128,128]{1,0:T(8,128)(2,1)S(1)} %copy-done.16, f32[2048,128]{1,0:T(8,128)S(1)} %fusion.68, f32[2048,128]{1,0:T(8,128)} %shard_map.200, bf16[256,128]{1,0:T(8,128)(2,1)S(1)} %copy-done.7), kind=kOutput, calls=%fused_computation.72 | convolution fusion | flops 137363456 | bytes 2686976 | tf_op jit(solution)/shard_map/dot_general | solution.py:231
  89.4 1.2 convert_reduce_fusion
  92.2 0.9 fusion.83
  95.7 14.3 %shard_map.201 = f32[40,128]{1,0:T(8,128)} custom-call(f32[40,128]{1,0:T(8,128)} %fusion.72.x_ref), custom_call_target="tpu_custom_call" | custom-call | tf_op jit(solution)/shard_map/pallas_call | solution.py:77
  114.3 1.3 %fusion.91.x_ref = f32[2048,128]{1,0:T(8,128)} fusion(bf16[2048,64]{0,1:T(8,128)(2,1)S(1)} %bitcast.56, bf16[64,128]{1,0:T(8,128)(2,1)S(1)} %copy-done.8), kind=kOutput, calls=%fused_computation.141 | convolution fusion | flops 33554432 | bytes 1327104 | tf_op jit(solution)/shard_map/dot_general | solution.py:424
  115.7 7.7 %shard_map.202 = f32[2048,128]{1,0:T(8,128)} custom-call(f32[2048,128]{1,0:T(8,128)} %fusion.91.x_ref), custom_call_target="tpu_custom_call" | custom-call | tf_op jit(solution)/shard_map/pallas_call | solution.py:179
  123.4 2.1 %fusion.47 = bf16[2048,128]{1,0:T(8,128)(2,1)} fusion(f32[2048,128]{1,0:T(8,128)} %shard_map.202, bf16[2048,128]{1,0:T(8,128)(2,1)S(1)} %get-tuple-element.57), kind=kLoop, calls=%fused_computation.68 | loop fusion | flops 786432 | bytes 2097152 | tf_op jit(solution)/shard_map/convert_element_type | solution.py:426
  (74 shorter events, 13.1 us)
Async XLA Ops:
  0.0 92.2 %copy-start = (bf16[128,256]{1,0:T(8,128)(2,1)S(1)}, bf16[128,256]{1,0:T(8,128)(2,1)}, u32[]{:S(2)}) copy-start(bf16[128,256]{1,0:T(8,128)(2,1)} %param.39) | copy-start | bytes 196612
  29.1 8.4 %copy-start.3 = (bf16[12288,128]{1,0:T(8,128)(2,1)S(1)}, bf16[12288,128]{1,0:T(8,128)(2,1)}, u32[]{:S(2)}) copy-start(bf16[12288,128]{1,0:T(8,128)(2,1)} %param.24) | copy-start | bytes 9437188
  29.1 8.4 %copy-start.9 = (bf16[384,128]{1,0:T(8,128)(2,1)S(1)}, bf16[384,128]{1,0:T(8,128)(2,1)}, u32[]{:S(2)}) copy-start(bf16[384,128]{1,0:T(8,128)(2,1)} %param.29) | copy-start | bytes 294916
  38.1 8.2 %copy-start.1 = (bf16[2048,128]{1,0:T(8,128)(2,1)S(1)}, bf16[2048,128]{1,0:T(8,128)(2,1)}, u32[]{:S(2)}) copy-start(bf16[2048,128]{1,0:T(8,128)(2,1)} %own_ref.1) | copy-start | bytes 1572868
  46.6 5.3 %copy-start.15 = (bf16[128,128]{1,0:T(8,128)(2,1)S(1)}, bf16[128,128]{1,0:T(8,128)(2,1)}, u32[]{:S(2)}) copy-start(bf16[128,128]{1,0:T(8,128)(2,1)} %param.30) | copy-start | bytes 98308
  51.9 5.6 %copy-start.5 = (bf16[128,128]{1,0:T(8,128)(2,1)S(1)}, bf16[128,128]{1,0:T(8,128)(2,1)}, u32[]{:S(2)}) copy-start(bf16[128,128]{1,0:T(8,128)(2,1)} %param.31) | copy-start | bytes 98308
  62.2 2.6 %copy-start.4 = (bf16[12288,128]{1,0:T(8,128)(2,1)S(1)}, bf16[12288,128]{1,0:T(8,128)(2,1)}, u32[]{:S(2)}) copy-start(bf16[12288,128]{1,0:T(8,128)(2,1)} %param.24) | copy-start | bytes 9437188
  62.2 2.6 %copy-start.11 = (f32[128]{0:T(128)S(1)}, f32[128]{0:T(128)}, u32[]{:S(2)}) copy-start(f32[128]{0:T(128)} %param.32) | copy-start | bytes 1540
  79.6 6.1 %copy-start.2 = (bf16[2048,128]{1,0:T(8,128)(2,1)S(1)}, bf16[2048,128]{1,0:T(8,128)(2,1)}, u32[]{:S(2)}) copy-start(bf16[2048,128]{1,0:T(8,128)(2,1)} %own_ref.1) | copy-start | bytes 1572868
  79.6 6.1 %copy-start.7 = (bf16[256,128]{1,0:T(8,128)(2,1)S(1)}, bf16[256,128]{1,0:T(8,128)(2,1)}, u32[]{:S(2)}) copy-start(bf16[256,128]{1,0:T(8,128)(2,1)} %param.33) | copy-start | bytes 196612
  80.7 5.4 %copy-start.16 = (bf16[128,128]{1,0:T(8,128)(2,1)S(1)}, bf16[128,128]{1,0:T(8,128)(2,1)}, u32[]{:S(2)}) copy-start(bf16[128,128]{1,0:T(8,128)(2,1)} %param.34) | copy-start | bytes 98308
  86.1 1.9 %copy-start.6 = (bf16[128,128]{1,0:T(8,128)(2,1)S(1)}, bf16[128,128]{1,0:T(8,128)(2,1)}, u32[]{:S(2)}) copy-start(bf16[128,128]{1,0:T(8,128)(2,1)} %param.35) | copy-start | bytes 98308
  88.0 1.4 %copy-start.12 = (f32[128]{0:T(128)S(1)}, f32[128]{0:T(128)}, u32[]{:S(2)}) copy-start(f32[128]{0:T(128)} %param.36) | copy-start | bytes 1540
  88.7 2.6 %copy-start.13 = (f32[128]{0:T(128)S(1)}, f32[128]{0:T(128)}, u32[]{:S(2)}) copy-start(f32[128]{0:T(128)} %param.37) | copy-start | bytes 1540
  88.7 2.6 %copy-start.18 = (bf16[128,64]{0,1:T(8,128)(2,1)S(1)}, bf16[128,64]{0,1:T(8,128)(2,1)}, u32[]{:S(2)}) copy-start(bf16[128,64]{0,1:T(8,128)(2,1)} %param.38) | copy-start | bytes 49156
  89.4 2.8 %copy-start.10 = (f32[4]{0:T(128)S(1)}, f32[4]{0:T(128)}, u32[]{:S(2)}) copy-start(f32[4]{0:T(128)} %param.40) | copy-start | bytes 52
  94.2 17.4 %copy-start.14 = (f32[2,4,16,16]{3,2,1,0:T(8,128)S(1)}, f32[2,4,16,16]{3,2,1,0:T(8,128)}, u32[]{:S(2)}) copy-start(f32[2,4,16,16]{3,2,1,0:T(8,128)} %param.41) | copy-start | bytes 24580
  94.2 18.7 %copy-start.17 = (f32[4,16,16]{2,1,0:T(8,128)S(1)}, f32[4,16,16]{2,1,0:T(8,128)}, u32[]{:S(2)}) copy-start(f32[4,16,16]{2,1,0:T(8,128)} %param.42) | copy-start | bytes 12292
  113.6 0.7 copy-start.8

commit v3 on v2

--- a/solution.py
+++ b/solution.py
@@ -192,6 +192,114 @@
     )(x)
 
 
+def _silu(values):
+    return values * (1.0 / (1.0 + jnp.exp(-values)))
+
+
+def _fold_pick(table_ref, ids, fold):
+    chunk = ids.shape[0]
+    groups = table_ref.shape[0]
+    width = table_ref.shape[1] // fold
+    shift = fold.bit_length() - 1
+    hot = (
+        lax.shift_right_logical(ids, shift) == lax.broadcasted_iota(jnp.int32, (chunk, groups), 1)
+    ).astype(jnp.bfloat16)
+    picked = jnp.dot(hot, table_ref[...], preferred_element_type=jnp.float32)
+    lane = jnp.bitwise_and(ids, fold - 1)
+    rows = picked[:, :width]
+    for j in range(1, fold):
+        rows = jnp.where(lane == j, picked[:, j * width : (j + 1) * width], rows)
+    return rows.astype(jnp.bfloat16)
+
+
+def _edge_kernel(fold, scalars, edge_ref, src_ref, dst_ref, dst_row_ref, ext_ref, own_ref,
+                 alpha_ref, beta_ref, gamma_ref, gain_ref, out_ref):
+    step = pl.program_id(0)
+    chunk, width = edge_ref.shape
+
+    @pl.when(step == 0)
+    def _():
+        out_ref[...] = jnp.zeros_like(out_ref)
+
+    edge = edge_ref[...]
+    dst = dst_ref[...]
+    sender = _fold_pick(ext_ref, src_ref[...], fold)
+    receiver = _fold_pick(own_ref, dst, fold)
+    pre = jnp.dot(edge, alpha_ref[0:width], preferred_element_type=jnp.float32)
+    pre = pre + jnp.dot(sender, alpha_ref[width : 2 * width], preferred_element_type=jnp.float32)
+    pre = pre + jnp.dot(receiver, alpha_ref[2 * width :], preferred_element_type=jnp.float32)
+    first = _silu(pre).astype(jnp.bfloat16)
+    second = _silu(jnp.dot(first, beta_ref[...], preferred_element_type=jnp.float32)).astype(
+        jnp.bfloat16
+    )
+    third = jnp.dot(second, gamma_ref[...], preferred_element_type=jnp.float32)
+    row_mean = jnp.mean(third, axis=-1, keepdims=True)
+    centred = third - row_mean
+    row_var = jnp.mean(centred * centred, axis=-1, keepdims=True)
+    normed = centred * lax.rsqrt(row_var + 1e-05) * gain_ref[...]
+    edge_new = (edge.astype(jnp.float32) + normed).astype(jnp.bfloat16)
+    position = scalars[1] + step * chunk + lax.broadcasted_iota(jnp.int32, (chunk, 1), 0)
+    live = position < scalars[2]
+    messages = jnp.where(live, edge_new, jnp.zeros_like(edge_new))
+    lane = jnp.bitwise_and(dst, fold - 1)
+    spread = jnp.concatenate(
+        [jnp.where(lane == j, messages, jnp.zeros_like(messages)) for j in range(fold)], axis=1
+    )
+    groups = out_ref.shape[0]
+    shift = fold.bit_length() - 1
+    hot_t = (
+        lax.broadcasted_iota(jnp.int32, (groups, chunk), 0)
+        == lax.shift_right_logical(dst_row_ref[0], shift)
+    ).astype(jnp.bfloat16)
+    out_ref[...] += jnp.dot(hot_t, spread, preferred_element_type=jnp.float32)
+
+
+def edge_messages(edges, send_ids, recv_ids, extended, own_rows, alpha, beta, gamma, gain,
+                  first_row, share, tally, chunk=512, fold=FOLD):
+    slots, width = edges.shape
+    nodes = own_rows.shape[0]
+    turns = share // chunk
+    scalars = jnp.stack([first_row // chunk, first_row, tally]).astype(jnp.int32)
+    ext_wide = extended.reshape(extended.shape[0] // fold, fold * width)
+    own_wide = own_rows.reshape(nodes // fold, fold * width)
+    full = lambda shape: pl.BlockSpec(shape, lambda i, s: (0,) * len(shape))
+    grid_spec = pltpu.PrefetchScalarGridSpec(
+        num_scalar_prefetch=1,
+        grid=(turns,),
+        in_specs=[
+            pl.BlockSpec((chunk, width), lambda i, s: (s[0] + i, 0)),
+            pl.BlockSpec((chunk, 1), lambda i, s: (s[0] + i, 0)),
+            pl.BlockSpec((chunk, 1), lambda i, s: (s[0] + i, 0)),
+            pl.BlockSpec((1, 1, chunk), lambda i, s: (s[0] + i, 0, 0)),
+            full(ext_wide.shape),
+            full(own_wide.shape),
+            full(alpha.shape),
+            full(beta.shape),
+            full(gamma.shape),
+            full((1, width)),
+        ],
+        out_specs=full((nodes // fold, fold * width)),
+    )
+    total = pl.pallas_call(
+        functools.partial(_edge_kernel, fold),
+        out_shape=jax.ShapeDtypeStruct((nodes // fold, fold * width), jnp.float32),
+        grid_spec=grid_spec,
+    )(
+        scalars,
+        edges,
+        send_ids.reshape(slots, 1),
+        recv_ids.reshape(slots, 1),
+        recv_ids.reshape(slots // chunk, 1, chunk),
+        ext_wide,
+        own_wide,
+        alpha,
+        beta,
+        gamma,
+        gain.reshape(1, width).astype(jnp.float32),
+    )
+    return total.reshape(nodes, width)
+
+
 def psum_slices(numer, denom):
     joined = jnp.concatenate([numer.reshape(-1), denom.reshape(-1)])
     rows = -(-joined.shape[0] // 1024) * 8
@@ -355,51 +463,21 @@
     extended = exchange_halos(
         vertex_state, outgoing.reshape(halo_outgoing_ids.shape[1:] + (feature_width,)), offsets
     )
-    extended_ids = jnp.arange(extended.shape[0], dtype=jnp.int32)
-    node_ids = jnp.arange(node_count, dtype=jnp.int32)
-    block_rows = capacity // lax.axis_size("head")
     share = capacity // lax.axis_size("head")
     first_row = lax.axis_index("head") * share
-    edge_rows = lax.dynamic_slice_in_dim(link_state_slotted, first_row, share, 0)
-    send_rows = lax.dynamic_slice_in_dim(source_vertex_ids, first_row, share, 0)
-    recv_rows = lax.dynamic_slice_in_dim(target_vertex_ids, first_row, share, 0)
-    turns = edge_rows.shape[0] // block_rows
-    edge_blocks = edge_rows.reshape(turns, block_rows, feature_width)
-    send_blocks = send_rows.reshape(turns, block_rows)
-    recv_blocks = recv_rows.reshape(turns, block_rows)
-
-    def step(total, item):
-        edge_part, send_part, recv_part, turn = item
-        sender_rows = gather_rows(extended, send_part, FOLD)
-        receiver_rows = gather_rows(vertex_state, recv_part, FOLD)
-        pre = jnp.dot(
-            edge_part, link_layer_alpha[:feature_width], preferred_element_type=jnp.float32
-        )
-        pre = pre + jnp.dot(
-            sender_rows,
-            link_layer_alpha[feature_width : 2 * feature_width],
-            preferred_element_type=jnp.float32,
-        )
-        pre = pre + jnp.dot(
-            receiver_rows, link_layer_alpha[2 * feature_width :], preferred_element_type=jnp.float32
-        )
-        first = jax.nn.silu(pre).astype(jnp.bfloat16)
-        second = jax.nn.silu(
-            jnp.dot(first, link_layer_beta, preferred_element_type=jnp.float32)
-        ).astype(jnp.bfloat16)
-        third = jnp.dot(second, link_layer_gamma, preferred_element_type=jnp.float32)
-        edge_new = (edge_part.astype(jnp.float32) + layer_norm(third, link_scale_factor)).astype(
-            jnp.bfloat16
-        )
-        position = first_row + turn * block_rows + jnp.arange(block_rows, dtype=jnp.int32)
-        live = position < active_link_tally[0]
-        messages = jnp.where(live[:, None], edge_new, jnp.zeros_like(edge_new))
-        gathered = scatter_rows(messages, recv_part, node_count, FOLD)
-        return (total + gathered, None)
-
-    start = jnp.zeros((node_count, feature_width), jnp.float32)
-    total, unused = lax.scan(
-        step, start, (edge_blocks, send_blocks, recv_blocks, jnp.arange(turns, dtype=jnp.int32))
+    total = edge_messages(
+        link_state_slotted,
+        source_vertex_ids,
+        target_vertex_ids,
+        extended,
+        vertex_state,
+        link_layer_alpha,
+        link_layer_beta,
+        link_layer_gamma,
+        link_scale_factor,
+        first_row,
+        share,
+        active_link_tally[0],
     )
     summed = sibling_sum(total, 2)
     refreshed_vertices = node_section(

time: 126 us -> 114 us (0.905)
  matrix products: 48 us -> 12.4 us
  Pallas kernels: 45.9 us -> 76.5 us
  other arithmetic: 21.9 us -> 7 us
  local copies, waits for them, and re-layouts: 8.54 us -> 17 us
    dot_general x7 -> x0, matrix products: 34.6 us -> none  [the longest x2 13.7 us: gather_rows(): picked = jnp.dot(hot, wide, preferred_element_type=jnp.float32)]
    pallas_call x0 -> x1, Pallas kernels: none -> 30.5 us  [edge_messages(): pl.pallas_call(functools.partial(_edge_kernel, fold), out_shape=jax.Shape...]
    reshape x3 -> x5, local copies, waits for them, and re-layouts: 3.08 us -> 14.6 us  [the longest x1 4.69 us: edge_messages(): send_ids.reshape(slots, 1)]
    select_n x3 -> x0, other arithmetic: 11.3 us -> none  [the longest x2 10.5 us: scatter_rows(): jnp.where((lane == j)[:, None], messages, jnp.zeros_like(messages))]
    eq x3 -> x0, other arithmetic: 2.37 us -> none  [the longest x2 1.58 us: gather_rows(): lane == j]
    dot_general x1 -> x0, local copies, waits for them, and re-layouts: 2.36 us -> none  [step(): jnp.dot(second, link_layer_gamma, preferred_element_type=jnp.float32)]
    reduce_sum x3 -> x2, other arithmetic: 3.08 us -> 1.26 us  [layer_norm(): row_var = jnp.mean(centred * centred, axis=-1, keepdims=True)]
where the time goes in v3:
time: 114 us
  Pallas kernels  76.5 us (67%)
  local copies, waits for them, and re-layouts  17 us (15%)
  matrix products  12.4 us (11%)
  other arithmetic  7 us (6%)
    pallas_call x1, Pallas kernels, edge_messages(): pl.pallas_call(functools.partial(_edge_kernel, fold), out_shape=jax.Shape...  30.5 us
    pallas_call x1, Pallas kernels, exchange_halos(): pl.pallas_call(functools.partial(_halo_kernel, offsets), out_shape=jax.Sh...  18.8 us
    pallas_call x1, Pallas kernels, dom_sum(): pl.pallas_call(functools.partial(_radix_kernel, radix, steps), out_shape=...  14.3 us
    pallas_call x2, Pallas kernels, sibling_sum(): pl.pallas_call(_sibling_kernel, out_shape=jax.ShapeDtypeStruct(x.shape, x...  12.8 us
    reshape x1, local copies, waits for them, and re-layouts, edge_messages(): send_ids.reshape(slots, 1)  4.69 us
    reshape x1, local copies, waits for them, and re-layouts, edge_messages(): recv_ids.reshape(slots, 1)  3.95 us
    dot_general x1, matrix products, pick_rows(): jnp.dot(selector, table, preferred_element_type=jnp.float32)  3.69 us
    reshape x1, local copies, waits for them, and re-layouts, edge_messages(): ext_wide = extended.reshape(extended.shape[0] // fold, fold * width)  2.54 us

profile of v3, /device:TPU:1, one launch (start us, length us, event | category | flops | bytes accessed | tf_op | source)
XLA Modules:
  0.0 113.8 jit_solution(3955282539386866894)
XLA Ops:
  0.7 0.7 pad_add_fusion.scalars
  1.3 4.7 %copy.23.src_ref = s32[12288,1]{1,0:T(8,128)} copy(s32[12288,1]{0,1:T(1,128)} %bitcast.58) | data formatting | bytes 98304 | tf_op jit(solution)/shard_map/reshape | solution.py:290
  6.0 4.0 %copy.24.dst_ref = s32[12288,1]{1,0:T(8,128)} copy(s32[12288,1]{0,1:T(1,128)S(1)} %bitcast.57) | data formatting | bytes 98304 | tf_op jit(solution)/shard_map/reshape | solution.py:291
  10.0 3.7 %fusion.2 = bf16[2048,128]{1,0:T(8,128)(2,1)} fusion(bf16[2048,128]{1,0:T(8,128)(2,1)S(1)} %copy-done.1, s32[2048]{0:T(1024)S(1)} %bitcast.60), kind=kOutput, calls=%fused_computation.4 | convolution fusion | flops 1078198272 | bytes 1056768 | tf_op jit(solution)/shard_map/dot_general | solution.py:402
  13.7 18.8 %shard_map.199 = bf16[4096,128]{1,0:T(8,128)(2,1)} custom-call(bf16[2048,128]{1,0:T(8,128)(2,1)} %own_ref.1, bf16[4,512,128]{2,1,0:T(8,128)(2,1)} %bitcast.54), custom_call_target="tpu_custom_call" | custom-call | tf_op jit(solution)/shard_map/pallas_call | solution.py:149
  32.5 2.5 %reshape.111.ext_ref = bf16[1024,512]{1,0:T(8,128)(2,1)} reshape(bf16[4096,128]{1,0:T(8,128)(2,1)} %shard_map.199) | data formatting | bytes 2097152 | tf_op jit(solution)/shard_map/reshape | solution.py:263
  35.1 1.1 reshape.112.own_ref
  36.2 30.5 %shard_map.200 = f32[512,512]{1,0:T(8,128)} custom-call(s32[3]{0:T(128)} %pad_add_fusion.scalars, bf16[12288,128]{1,0:T(8,128)(2,1)} %edge_ref.1, s32[12288,1]{1,0:T(8,128)} %copy.23.src_ref, s32[12288,1]{1,0:T(8,128)} %copy.24.dst_ref, s32[24,1,512]{2,1,0:T(1,128)} %bitcast.56, bf16[1024,512]{1,0:T(8,128)(2,1)} %reshape.111.ext_ref, ...), custom_call_target="tpu_custom_call" | custom-call | tf_op jit(solution)/shard_map/pallas_call | solution.py:283
  66.7 2.3 %reshape.114.x_ref = f32[2048,128]{1,0:T(8,128)} reshape(f32[512,512]{1,0:T(8,128)} %shard_map.200) | data formatting | bytes 2097152 | tf_op jit(solution)/shard_map/reshape | solution.py:300
  69.0 5.0 %shard_map.201 = f32[2048,128]{1,0:T(8,128)} custom-call(f32[2048,128]{1,0:T(8,128)} %reshape.114.x_ref), custom_call_target="tpu_custom_call" | custom-call | tf_op jit(solution)/shard_map/pallas_call | solution.py:179
  74.4 1.9 %multiply_convert_fusion = bf16[2048,128]{1,0:T(8,128)(2,1)S(1)} fusion(bf16[128,128]{1,0:T(8,128)(2,1)S(1)} %copy-done.12, f32[2048,128]{1,0:T(8,128)S(1)} %fusion.28, f32[2048,128]{1,0:T(8,128)} %shard_map.201, bf16[256,128]{1,0:T(8,128)(2,1)S(1)} %copy-done.5), kind=kOutput, calls=%fused_computation.28 | convolution fusion | flops 137363456 | bytes 2686976 | tf_op jit(solution)/shard_map/dot_general | solution.py:339
  77.1 0.6 multiply_reduce_fusion
  77.8 1.2 %convert_reduce_fusion = (f32[2048]{0:T(1024)S(1)}, bf16[2048,128]{1,0:T(8,128)(2,1)S(1)}) fusion(f32[128]{0:T(128)S(1)} %copy-done.9, f32[2048]{0:T(1024)S(1)} %add_rsqrt_fusion.1, f32[2048,128]{1,0:T(8,128)S(1)} %copy.25, f32[2048]{0:T(1024)S(1)} %broadcast_multiply_fusion.1, bf16[2048,128]{1,0:T(8,128)(2,1)S(1)} %copy-done.2), kind=kLoop, calls=%fused_computation.16 | loop fusion | flops 2095104 | bytes 2122240 | tf_op jit(solution)/shard_map/reduce_sum | solution.py:316
  79.0 0.6 fusion.8
  79.7 0.8 convolution_convert_fusion.1
  80.5 0.9 fusion.36
  81.9 0.6 fusion.37
  83.3 0.6 fusion.30.x_ref
  84.0 14.3 %shard_map.202 = f32[40,128]{1,0:T(8,128)} custom-call(f32[40,128]{1,0:T(8,128)} %fusion.30.x_ref), custom_call_target="tpu_custom_call" | custom-call | tf_op jit(solution)/shard_map/pallas_call | solution.py:77
  98.3 0.7 slice.33
  99.1 0.7 slice.34
  102.6 1.3 %fusion.40.x_ref = f32[2048,128]{1,0:T(8,128)} fusion(bf16[2048,64]{0,1:T(8,128)(2,1)S(1)} %bitcast.55, bf16[64,128]{1,0:T(8,128)(2,1)S(1)} %copy-done.6), kind=kOutput, calls=%fused_computation.63 | convolution fusion | flops 33554432 | bytes 1327104 | tf_op jit(solution)/shard_map/dot_general | solution.py:502
  104.0 7.7 %shard_map.203 = f32[2048,128]{1,0:T(8,128)} custom-call(f32[2048,128]{1,0:T(8,128)} %fusion.40.x_ref), custom_call_target="tpu_custom_call" | custom-call | tf_op jit(solution)/shard_map/pallas_call | solution.py:179
  111.7 2.1 %fusion.11 = bf16[2048,128]{1,0:T(8,128)(2,1)} fusion(f32[2048,128]{1,0:T(8,128)} %shard_map.203, bf16[2048,128]{1,0:T(8,128)(2,1)S(1)} %get-tuple-element.18), kind=kLoop, calls=%fused_computation.24 | loop fusion | flops 786432 | bytes 2097152 | tf_op jit(solution)/shard_map/convert_element_type | solution.py:504
  (52 shorter events, 5.3 us)
Async XLA Ops:
  0.0 80.4 %copy-start = (bf16[128,256]{1,0:T(8,128)(2,1)S(1)}, bf16[128,256]{1,0:T(8,128)(2,1)}, u32[]{:S(2)}) copy-start(bf16[128,256]{1,0:T(8,128)(2,1)} %param.39) | copy-start | bytes 196612
  1.3 4.7 %copy-start.3 = (s32[12288]{0:T(1024)S(1)}, s32[12288]{0:T(1024)}, u32[]{:S(2)}) copy-start(s32[12288]{0:T(1024)} %param.26) | copy-start | bytes 147460
  6.0 4.0 %copy-start.7 = (s32[1,4,512]{2,1,0:T(4,128)S(1)}, s32[1,4,512]{2,1,0:T(4,128)}, u32[]{:S(2)}) copy-start(s32[1,4,512]{2,1,0:T(4,128)} %param.28) | copy-start | bytes 24580
  6.0 4.0 %copy-start.1 = (bf16[2048,128]{1,0:T(8,128)(2,1)S(1)}, bf16[2048,128]{1,0:T(8,128)(2,1)}, u32[]{:S(2)}) copy-start(bf16[2048,128]{1,0:T(8,128)(2,1)} %own_ref.1) | copy-start | bytes 1572868
  13.7 21.4 %copy-start.2 = (bf16[2048,128]{1,0:T(8,128)(2,1)S(1)}, bf16[2048,128]{1,0:T(8,128)(2,1)}, u32[]{:S(2)}) copy-start(bf16[2048,128]{1,0:T(8,128)(2,1)} %own_ref.1) | copy-start | bytes 1572868
  66.7 7.4 %copy-start.5 = (bf16[256,128]{1,0:T(8,128)(2,1)S(1)}, bf16[256,128]{1,0:T(8,128)(2,1)}, u32[]{:S(2)}) copy-start(bf16[256,128]{1,0:T(8,128)(2,1)} %param.33) | copy-start | bytes 196612
  69.0 5.3 %copy-start.12 = (bf16[128,128]{1,0:T(8,128)(2,1)S(1)}, bf16[128,128]{1,0:T(8,128)(2,1)}, u32[]{:S(2)}) copy-start(bf16[128,128]{1,0:T(8,128)(2,1)} %param.34) | copy-start | bytes 98308
  74.4 1.9 %copy-start.4 = (bf16[128,128]{1,0:T(8,128)(2,1)S(1)}, bf16[128,128]{1,0:T(8,128)(2,1)}, u32[]{:S(2)}) copy-start(bf16[128,128]{1,0:T(8,128)(2,1)} %param.35) | copy-start | bytes 98308
  76.4 1.4 %copy-start.9 = (f32[128]{0:T(128)S(1)}, f32[128]{0:T(128)}, u32[]{:S(2)}) copy-start(f32[128]{0:T(128)} %param.36) | copy-start | bytes 1540
  77.1 2.6 %copy-start.10 = (f32[128]{0:T(128)S(1)}, f32[128]{0:T(128)}, u32[]{:S(2)}) copy-start(f32[128]{0:T(128)} %param.37) | copy-start | bytes 1540
  77.1 2.6 %copy-start.14 = (bf16[128,64]{0,1:T(8,128)(2,1)S(1)}, bf16[128,64]{0,1:T(8,128)(2,1)}, u32[]{:S(2)}) copy-start(bf16[128,64]{0,1:T(8,128)(2,1)} %param.38) | copy-start | bytes 49156
  77.7 2.7 %copy-start.8 = (f32[4]{0:T(128)S(1)}, f32[4]{0:T(128)}, u32[]{:S(2)}) copy-start(f32[4]{0:T(128)} %param.40) | copy-start | bytes 52
  82.5 17.4 %copy-start.11 = (f32[2,4,16,16]{3,2,1,0:T(8,128)S(1)}, f32[2,4,16,16]{3,2,1,0:T(8,128)}, u32[]{:S(2)}) copy-start(f32[2,4,16,16]{3,2,1,0:T(8,128)} %param.41) | copy-start | bytes 24580
  82.5 18.7 %copy-start.13 = (f32[4,16,16]{2,1,0:T(8,128)S(1)}, f32[4,16,16]{2,1,0:T(8,128)}, u32[]{:S(2)}) copy-start(f32[4,16,16]{2,1,0:T(8,128)} %param.42) | copy-start | bytes 12292
  101.9 0.7 copy-start.6

commit v4 on v3

--- a/solution.py
+++ b/solution.py
@@ -255,11 +255,13 @@
 
 
 def edge_messages(edges, send_ids, recv_ids, extended, own_rows, alpha, beta, gamma, gain,
-                  first_row, share, tally, chunk=512, fold=FOLD):
+                  first_row, share, tally, chunk=1024, fold=FOLD):
     slots, width = edges.shape
     nodes = own_rows.shape[0]
     turns = share // chunk
     scalars = jnp.stack([first_row // chunk, first_row, tally]).astype(jnp.int32)
+    send_ids = lax.dynamic_slice_in_dim(send_ids, first_row, share, 0)
+    recv_ids = lax.dynamic_slice_in_dim(recv_ids, first_row, share, 0)
     ext_wide = extended.reshape(extended.shape[0] // fold, fold * width)
     own_wide = own_rows.reshape(nodes // fold, fold * width)
     full = lambda shape: pl.BlockSpec(shape, lambda i, s: (0,) * len(shape))
@@ -268,9 +270,9 @@
         grid=(turns,),
         in_specs=[
             pl.BlockSpec((chunk, width), lambda i, s: (s[0] + i, 0)),
-            pl.BlockSpec((chunk, 1), lambda i, s: (s[0] + i, 0)),
-            pl.BlockSpec((chunk, 1), lambda i, s: (s[0] + i, 0)),
-            pl.BlockSpec((1, 1, chunk), lambda i, s: (s[0] + i, 0, 0)),
+            pl.BlockSpec((chunk, 1), lambda i, s: (i, 0)),
+            pl.BlockSpec((chunk, 1), lambda i, s: (i, 0)),
+            pl.BlockSpec((1, 1, chunk), lambda i, s: (i, 0, 0)),
             full(ext_wide.shape),
             full(own_wide.shape),
             full(alpha.shape),
@@ -287,9 +289,9 @@
     )(
         scalars,
         edges,
-        send_ids.reshape(slots, 1),
-        recv_ids.reshape(slots, 1),
-        recv_ids.reshape(slots // chunk, 1, chunk),
+        send_ids.reshape(share, 1),
+        recv_ids.reshape(share, 1),
+        recv_ids.reshape(turns, 1, chunk),
         ext_wide,
         own_wide,
         alpha,

time: 114 us -> 106 us (0.930)
  Pallas kernels: 76.5 us -> 71.7 us
  local copies, waits for them, and re-layouts: 17 us -> 13.5 us
    pallas_call x1, Pallas kernels: 30.5 us -> 25.8 us  [edge_messages(): pl.pallas_call(functools.partial(_edge_kernel, fold), out_shape=jax.Shape...]
    reshape x2, local copies, waits for them, and re-layouts: 8.64 us -> 4.42 us  [the longest x1 2.22 us: edge_messages(): recv_ids.reshape(share, 1)]
where the time goes in v4:
time: 106 us; the launch traced here: 105 us
  Pallas kernels  71.7 us (68%)
  local copies, waits for them, and re-layouts  13.5 us (13%)
  matrix products  12.4 us (12%)
  other arithmetic  6.94 us (7%)
    pallas_call x1, Pallas kernels, edge_messages(): pl.pallas_call(functools.partial(_edge_kernel, fold), out_shape=jax.Shape...  25.8 us
    pallas_call x1, Pallas kernels, exchange_halos(): pl.pallas_call(functools.partial(_halo_kernel, offsets), out_shape=jax.Sh...  18.8 us
    pallas_call x1, Pallas kernels, dom_sum(): pl.pallas_call(functools.partial(_radix_kernel, radix, steps), out_shape=...  14.3 us
    pallas_call x2, Pallas kernels, sibling_sum(): pl.pallas_call(_sibling_kernel, out_shape=jax.ShapeDtypeStruct(x.shape, x...  12.8 us
    dot_general x1, matrix products, pick_rows(): jnp.dot(selector, table, preferred_element_type=jnp.float32)  3.68 us
    reshape x1, local copies, waits for them, and re-layouts, edge_messages(): ext_wide = extended.reshape(extended.shape[0] // fold, fold * width)  2.51 us
    reshape x1, local copies, waits for them, and re-layouts, edge_messages(): return total.reshape(nodes, width)  2.31 us
    reshape x1, local copies, waits for them, and re-layouts, edge_messages(): recv_ids.reshape(share, 1)  2.22 us

profile of v4, /device:TPU:1, one launch (start us, length us, event | category | flops | bytes accessed | tf_op | source)
XLA Modules:
  0.0 105.5 jit_solution(11883153181249634143)
XLA Ops:
  1.3 0.7 dynamic_slice.7
  2.0 2.2 %copy.24.dst_ref = s32[6144,1]{1,0:T(8,128)} copy(s32[6144,1]{0,1:T(1,128)S(1)} %bitcast.56) | data formatting | bytes 49152 | tf_op jit(solution)/shard_map/reshape | solution.py:293
  4.3 2.2 %copy.23.src_ref = s32[6144,1]{1,0:T(8,128)} copy(s32[6144,1]{0,1:T(1,128)S(1)} %bitcast.58) | data formatting | bytes 49152 | tf_op jit(solution)/shard_map/reshape | solution.py:292
  6.5 3.7 %fusion.2 = bf16[2048,128]{1,0:T(8,128)(2,1)} fusion(bf16[2048,128]{1,0:T(8,128)(2,1)S(1)} %copy-done.1, s32[2048]{0:T(1024)S(1)} %bitcast.60), kind=kOutput, calls=%fused_computation.4 | convolution fusion | flops 1078198272 | bytes 1056768 | tf_op jit(solution)/shard_map/dot_general | solution.py:404
  10.2 18.8 %shard_map.199 = bf16[4096,128]{1,0:T(8,128)(2,1)} custom-call(bf16[2048,128]{1,0:T(8,128)(2,1)} %own_ref.1, bf16[4,512,128]{2,1,0:T(8,128)(2,1)} %bitcast.54), custom_call_target="tpu_custom_call" | custom-call | tf_op jit(solution)/shard_map/pallas_call | solution.py:149
  29.0 2.5 %reshape.111.ext_ref = bf16[1024,512]{1,0:T(8,128)(2,1)} reshape(bf16[4096,128]{1,0:T(8,128)(2,1)} %shard_map.199) | data formatting | bytes 2097152 | tf_op jit(solution)/shard_map/reshape | solution.py:265
  31.5 1.1 %reshape.112.own_ref = bf16[512,512]{1,0:T(8,128)(2,1)} reshape(bf16[2048,128]{1,0:T(8,128)(2,1)S(1)} %copy-done.2) | data formatting | bytes 1048576 | tf_op jit(solution)/shard_map/reshape | solution.py:266
  32.6 25.8 %shard_map.200 = f32[512,512]{1,0:T(8,128)} custom-call(s32[3]{0:T(128)} %pad_add_fusion.scalars, bf16[12288,128]{1,0:T(8,128)(2,1)} %edge_ref.1, s32[6144,1]{1,0:T(8,128)} %copy.23.src_ref, s32[6144,1]{1,0:T(8,128)} %copy.24.dst_ref, s32[6,1,1024]{2,1,0:T(1,128)} %bitcast.57, bf16[1024,512]{1,0:T(8,128)(2,1)} %reshape.111.ext_ref, ...), custom_call_target="tpu_custom_call" | custom-call | tf_op jit(solution)/shard_map/pallas_call | solution.py:285
  58.4 2.3 %reshape.114.x_ref = f32[2048,128]{1,0:T(8,128)} reshape(f32[512,512]{1,0:T(8,128)} %shard_map.200) | data formatting | bytes 2097152 | tf_op jit(solution)/shard_map/reshape | solution.py:302
  60.7 5.0 %shard_map.201 = f32[2048,128]{1,0:T(8,128)} custom-call(f32[2048,128]{1,0:T(8,128)} %reshape.114.x_ref), custom_call_target="tpu_custom_call" | custom-call | tf_op jit(solution)/shard_map/pallas_call | solution.py:179
  66.1 1.9 %multiply_convert_fusion = bf16[2048,128]{1,0:T(8,128)(2,1)S(1)} fusion(bf16[128,128]{1,0:T(8,128)(2,1)S(1)} %copy-done.12, f32[2048,128]{1,0:T(8,128)S(1)} %fusion.28, f32[2048,128]{1,0:T(8,128)} %shard_map.201, bf16[256,128]{1,0:T(8,128)(2,1)S(1)} %copy-done.5), kind=kOutput, calls=%fused_computation.28 | convolution fusion | flops 137363456 | bytes 2686976 | tf_op jit(solution)/shard_map/dot_general | solution.py:341
  68.8 0.6 multiply_reduce_fusion
  69.5 1.2 %convert_reduce_fusion = (f32[2048]{0:T(1024)S(1)}, bf16[2048,128]{1,0:T(8,128)(2,1)S(1)}) fusion(f32[128]{0:T(128)S(1)} %copy-done.9, f32[2048]{0:T(1024)S(1)} %add_rsqrt_fusion.1, f32[2048,128]{1,0:T(8,128)S(1)} %copy.25, f32[2048]{0:T(1024)S(1)} %broadcast_multiply_fusion.1, bf16[2048,128]{1,0:T(8,128)(2,1)S(1)} %copy-done.2), kind=kLoop, calls=%fused_computation.16 | loop fusion | flops 2095104 | bytes 2122240 | tf_op jit(solution)/shard_map/reduce_sum | solution.py:318
  70.7 0.6 fusion.8
  71.3 0.8 convolution_convert_fusion.1
  72.1 0.9 fusion.36
  73.6 0.6 fusion.37
  75.0 0.6 fusion.30.x_ref
  75.7 14.3 %shard_map.202 = f32[40,128]{1,0:T(8,128)} custom-call(f32[40,128]{1,0:T(8,128)} %fusion.30.x_ref), custom_call_target="tpu_custom_call" | custom-call | tf_op jit(solution)/shard_map/pallas_call | solution.py:77
  90.0 0.7 slice.33
  90.8 0.7 slice.34
  94.3 1.3 %fusion.40.x_ref = f32[2048,128]{1,0:T(8,128)} fusion(bf16[2048,64]{0,1:T(8,128)(2,1)S(1)} %bitcast.55, bf16[64,128]{1,0:T(8,128)(2,1)S(1)} %copy-done.6), kind=kOutput, calls=%fused_computation.63 | convolution fusion | flops 33554432 | bytes 1327104 | tf_op jit(solution)/shard_map/dot_general | solution.py:504
  95.6 7.7 %shard_map.203 = f32[2048,128]{1,0:T(8,128)} custom-call(f32[2048,128]{1,0:T(8,128)} %fusion.40.x_ref), custom_call_target="tpu_custom_call" | custom-call | tf_op jit(solution)/shard_map/pallas_call | solution.py:179
  103.4 2.1 %fusion.11 = bf16[2048,128]{1,0:T(8,128)(2,1)} fusion(f32[2048,128]{1,0:T(8,128)} %shard_map.203, bf16[2048,128]{1,0:T(8,128)(2,1)S(1)} %get-tuple-element.18), kind=kLoop, calls=%fused_computation.24 | loop fusion | flops 786432 | bytes 2097152 | tf_op jit(solution)/shard_map/convert_element_type | solution.py:506
  (55 shorter events, 5.9 us)
Async XLA Ops:
  0.0 72.1 %copy-start = (bf16[128,256]{1,0:T(8,128)(2,1)S(1)}, bf16[128,256]{1,0:T(8,128)(2,1)}, u32[]{:S(2)}) copy-start(bf16[128,256]{1,0:T(8,128)(2,1)} %param.39) | copy-start | bytes 196612
  1.3 3.0 %dynamic-slice-start = ((s32[12288]{0:T(1024)}, s32[]{:T(128)}), s32[6144]{0:T(1024)S(1)}, s32[]{:S(2)}) async-start(s32[12288]{0:T(1024)} %param.25, s32[]{:T(128)} %select_n.10), calls=%async_computation | async-start | bytes 49664 | tf_op jit(solution)/shard_map/dynamic_slice | solution.py:263
  2.0 4.4 %copy-start.3 = (s32[6144]{0:T(1024)}, s32[6144]{0:T(1024)S(1)}, u32[]{:S(2)}) copy-start(s32[6144]{0:T(1024)S(1)} %dynamic_slice.7) | copy-start | bytes 73732
  4.2 2.2 %copy-start.7 = (s32[1,4,512]{2,1,0:T(4,128)S(1)}, s32[1,4,512]{2,1,0:T(4,128)}, u32[]{:S(2)}) copy-start(s32[1,4,512]{2,1,0:T(4,128)} %param.28) | copy-start | bytes 24580
  4.3 2.2 %copy-start.1 = (bf16[2048,128]{1,0:T(8,128)(2,1)S(1)}, bf16[2048,128]{1,0:T(8,128)(2,1)}, u32[]{:S(2)}) copy-start(bf16[2048,128]{1,0:T(8,128)(2,1)} %own_ref.1) | copy-start | bytes 1572868
  10.2 21.4 %copy-start.2 = (bf16[2048,128]{1,0:T(8,128)(2,1)S(1)}, bf16[2048,128]{1,0:T(8,128)(2,1)}, u32[]{:S(2)}) copy-start(bf16[2048,128]{1,0:T(8,128)(2,1)} %own_ref.1) | copy-start | bytes 1572868
  58.4 7.4 %copy-start.5 = (bf16[256,128]{1,0:T(8,128)(2,1)S(1)}, bf16[256,128]{1,0:T(8,128)(2,1)}, u32[]{:S(2)}) copy-start(bf16[256,128]{1,0:T(8,128)(2,1)} %param.33) | copy-start | bytes 196612
  60.7 5.3 %copy-start.12 = (bf16[128,128]{1,0:T(8,128)(2,1)S(1)}, bf16[128,128]{1,0:T(8,128)(2,1)}, u32[]{:S(2)}) copy-start(bf16[128,128]{1,0:T(8,128)(2,1)} %param.34) | copy-start | bytes 98308
  66.1 1.9 %copy-start.4 = (bf16[128,128]{1,0:T(8,128)(2,1)S(1)}, bf16[128,128]{1,0:T(8,128)(2,1)}, u32[]{:S(2)}) copy-start(bf16[128,128]{1,0:T(8,128)(2,1)} %param.35) | copy-start | bytes 98308
  68.0 1.4 %copy-start.9 = (f32[128]{0:T(128)S(1)}, f32[128]{0:T(128)}, u32[]{:S(2)}) copy-start(f32[128]{0:T(128)} %param.36) | copy-start | bytes 1540
  68.7 2.6 %copy-start.10 = (f32[128]{0:T(128)S(1)}, f32[128]{0:T(128)}, u32[]{:S(2)}) copy-start(f32[128]{0:T(128)} %param.37) | copy-start | bytes 1540
  68.8 2.6 %copy-start.14 = (bf16[128,64]{0,1:T(8,128)(2,1)S(1)}, bf16[128,64]{0,1:T(8,128)(2,1)}, u32[]{:S(2)}) copy-start(bf16[128,64]{0,1:T(8,128)(2,1)} %param.38) | copy-start | bytes 49156
  69.4 2.7 %copy-start.8 = (f32[4]{0:T(128)S(1)}, f32[4]{0:T(128)}, u32[]{:S(2)}) copy-start(f32[4]{0:T(128)} %param.40) | copy-start | bytes 52
  74.2 17.4 %copy-start.11 = (f32[2,4,16,16]{3,2,1,0:T(8,128)S(1)}, f32[2,4,16,16]{3,2,1,0:T(8,128)}, u32[]{:S(2)}) copy-start(f32[2,4,16,16]{3,2,1,0:T(8,128)} %param.41) | copy-start | bytes 24580
  74.2 18.7 %copy-start.13 = (f32[4,16,16]{2,1,0:T(8,128)S(1)}, f32[4,16,16]{2,1,0:T(8,128)}, u32[]{:S(2)}) copy-start(f32[4,16,16]{2,1,0:T(8,128)} %param.42) | copy-start | bytes 12292
  93.6 0.7 copy-start.6

commit v5 on v4

--- a/solution.py
+++ b/solution.py
@@ -172,13 +172,13 @@
     )
     copy.start()
     copy.wait()
-    o_ref[...] = x_ref[...] + inbox[...]
+    o_ref[...] = x_ref[...].astype(o_ref.dtype) + inbox[...].astype(o_ref.dtype)
 
 
 def sibling_sum(x, collective_id):
     return pl.pallas_call(
         _sibling_kernel,
-        out_shape=jax.ShapeDtypeStruct(x.shape, x.dtype),
+        out_shape=jax.ShapeDtypeStruct(x.shape, jnp.float32),
         in_specs=[pl.BlockSpec(memory_space=pltpu.VMEM)],
         out_specs=pl.BlockSpec(memory_space=pltpu.VMEM),
         scratch_shapes=[
@@ -501,9 +501,14 @@
     slice_out = slice_mixing(numer, denom, cluster_probe_lookup, cluster_content_linear)
     attended = attend_rows(weights_b, slice_out)
     projected = sibling_sum(
-        jnp.dot(attended, closing_linear_factor, preferred_element_type=jnp.float32), 3
-    )
-    return (refreshed_vertices.astype(jnp.float32) + projected).astype(jnp.bfloat16)
+        jnp.dot(attended, closing_linear_factor, preferred_element_type=jnp.float32).astype(
+            jnp.bfloat16
+        ),
+        3,
+    )
+    return (refreshed_vertices.astype(jnp.float32) + projected.astype(jnp.float32)).astype(
+        jnp.bfloat16
+    )
 
 
 def solution(mesh):

time: 106 us -> 105 us (level)
  no operation moved by 1% of the time
where the time goes in v5:
time: 105 us; the launch traced here: 104 us
  Pallas kernels  70.7 us (67%)
  local copies, waits for them, and re-layouts  13.5 us (13%)
  matrix products  12.2 us (12%)
  other arithmetic  6.94 us (7%)
    pallas_call x1, Pallas kernels, edge_messages(): pl.pallas_call(functools.partial(_edge_kernel, fold), out_shape=jax.Shape...  25.8 us
    pallas_call x1, Pallas kernels, exchange_halos(): pl.pallas_call(functools.partial(_halo_kernel, offsets), out_shape=jax.Sh...  18.8 us
    pallas_call x1, Pallas kernels, dom_sum(): pl.pallas_call(functools.partial(_radix_kernel, radix, steps), out_shape=...  14.3 us
    pallas_call x2, Pallas kernels, sibling_sum(): pl.pallas_call(_sibling_kernel, out_shape=jax.ShapeDtypeStruct(x.shape, j...  11.8 us
    dot_general x1, matrix products, pick_rows(): jnp.dot(selector, table, preferred_element_type=jnp.float32)  3.68 us
    reshape x1, local copies, waits for them, and re-layouts, edge_messages(): ext_wide = extended.reshape(extended.shape[0] // fold, fold * width)  2.51 us
    reshape x1, local copies, waits for them, and re-layouts, edge_messages(): return total.reshape(nodes, width)  2.31 us
    reshape x1, local copies, waits for them, and re-layouts, edge_messages(): recv_ids.reshape(share, 1)  2.22 us

profile of v5, /device:TPU:1, one launch (start us, length us, event | category | flops | bytes accessed | tf_op | source)
XLA Modules:
  0.0 104.3 jit_solution(13543578714518076886)
XLA Ops:
  1.3 0.7 dynamic_slice.7
  2.0 2.2 %copy.24.dst_ref = s32[6144,1]{1,0:T(8,128)} copy(s32[6144,1]{0,1:T(1,128)S(1)} %bitcast.56) | data formatting | bytes 49152 | tf_op jit(solution)/shard_map/reshape | solution.py:293
  4.3 2.2 %copy.23.src_ref = s32[6144,1]{1,0:T(8,128)} copy(s32[6144,1]{0,1:T(1,128)S(1)} %bitcast.58) | data formatting | bytes 49152 | tf_op jit(solution)/shard_map/reshape | solution.py:292
  6.5 3.7 %fusion.2 = bf16[2048,128]{1,0:T(8,128)(2,1)} fusion(bf16[2048,128]{1,0:T(8,128)(2,1)S(1)} %copy-done.1, s32[2048]{0:T(1024)S(1)} %bitcast.60), kind=kOutput, calls=%fused_computation.4 | convolution fusion | flops 1078198272 | bytes 1056768 | tf_op jit(solution)/shard_map/dot_general | solution.py:404
  10.2 18.8 %shard_map.199 = bf16[4096,128]{1,0:T(8,128)(2,1)} custom-call(bf16[2048,128]{1,0:T(8,128)(2,1)} %own_ref.1, bf16[4,512,128]{2,1,0:T(8,128)(2,1)} %bitcast.54), custom_call_target="tpu_custom_call" | custom-call | tf_op jit(solution)/shard_map/pallas_call | solution.py:149
  29.0 2.5 %reshape.111.ext_ref = bf16[1024,512]{1,0:T(8,128)(2,1)} reshape(bf16[4096,128]{1,0:T(8,128)(2,1)} %shard_map.199) | data formatting | bytes 2097152 | tf_op jit(solution)/shard_map/reshape | solution.py:265
  31.5 1.1 %reshape.112.own_ref = bf16[512,512]{1,0:T(8,128)(2,1)} reshape(bf16[2048,128]{1,0:T(8,128)(2,1)S(1)} %copy-done.2) | data formatting | bytes 1048576 | tf_op jit(solution)/shard_map/reshape | solution.py:266
  32.6 25.8 %shard_map.200 = f32[512,512]{1,0:T(8,128)} custom-call(s32[3]{0:T(128)} %pad_add_fusion.scalars, bf16[12288,128]{1,0:T(8,128)(2,1)} %edge_ref.1, s32[6144,1]{1,0:T(8,128)} %copy.23.src_ref, s32[6144,1]{1,0:T(8,128)} %copy.24.dst_ref, s32[6,1,1024]{2,1,0:T(1,128)} %bitcast.57, bf16[1024,512]{1,0:T(8,128)(2,1)} %reshape.111.ext_ref, ...), custom_call_target="tpu_custom_call" | custom-call | tf_op jit(solution)/shard_map/pallas_call | solution.py:285
  58.4 2.3 %reshape.114.x_ref = f32[2048,128]{1,0:T(8,128)} reshape(f32[512,512]{1,0:T(8,128)} %shard_map.200) | data formatting | bytes 2097152 | tf_op jit(solution)/shard_map/reshape | solution.py:302
  60.7 5.0 %shard_map.201 = f32[2048,128]{1,0:T(8,128)} custom-call(f32[2048,128]{1,0:T(8,128)} %reshape.114.x_ref), custom_call_target="tpu_custom_call" | custom-call | tf_op jit(solution)/shard_map/pallas_call | solution.py:179
  66.1 1.9 %multiply_convert_fusion = bf16[2048,128]{1,0:T(8,128)(2,1)S(1)} fusion(bf16[128,128]{1,0:T(8,128)(2,1)S(1)} %copy-done.12, f32[2048,128]{1,0:T(8,128)S(1)} %fusion.28, f32[2048,128]{1,0:T(8,128)} %shard_map.201, bf16[256,128]{1,0:T(8,128)(2,1)S(1)} %copy-done.5), kind=kOutput, calls=%fused_computation.29 | convolution fusion | flops 137363456 | bytes 2686976 | tf_op jit(solution)/shard_map/dot_general | solution.py:341
  68.8 0.6 multiply_reduce_fusion
  69.5 1.2 %convert_reduce_fusion = (f32[2048]{0:T(1024)S(1)}, bf16[2048,128]{1,0:T(8,128)(2,1)S(1)}) fusion(f32[128]{0:T(128)S(1)} %copy-done.9, f32[2048]{0:T(1024)S(1)} %add_rsqrt_fusion.1, f32[2048,128]{1,0:T(8,128)S(1)} %copy.25, f32[2048]{0:T(1024)S(1)} %broadcast_multiply_fusion.1, bf16[2048,128]{1,0:T(8,128)(2,1)S(1)} %copy-done.2), kind=kLoop, calls=%fused_computation.17 | loop fusion | flops 2095104 | bytes 2122240 | tf_op jit(solution)/shard_map/reduce_sum | solution.py:318
  70.7 0.6 fusion.8
  71.3 0.8 convolution_convert_fusion.2
  72.1 0.9 fusion.36
  73.6 0.6 fusion.37
  75.0 0.6 fusion.30.x_ref
  75.7 14.3 %shard_map.202 = f32[40,128]{1,0:T(8,128)} custom-call(f32[40,128]{1,0:T(8,128)} %fusion.30.x_ref), custom_call_target="tpu_custom_call" | custom-call | tf_op jit(solution)/shard_map/pallas_call | solution.py:77
  90.0 0.7 slice.33
  90.8 0.7 slice.34
  94.3 1.1 %convolution_convert_fusion.x_ref = bf16[2048,128]{1,0:T(8,128)(2,1)} fusion(bf16[2048,64]{0,1:T(8,128)(2,1)S(1)} %bitcast.55, bf16[64,128]{1,0:T(8,128)(2,1)S(1)} %copy-done.6), kind=kOutput, calls=%fused_computation.5 | convolution fusion | flops 33816576 | bytes 802816 | tf_op jit(solution)/shard_map/dot_general | solution.py:504
  95.4 6.7 %shard_map.203 = f32[2048,128]{1,0:T(8,128)} custom-call(bf16[2048,128]{1,0:T(8,128)(2,1)} %convolution_convert_fusion.x_ref), custom_call_target="tpu_custom_call" | custom-call | tf_op jit(solution)/shard_map/pallas_call | solution.py:179
  102.2 2.1 %fusion.11 = bf16[2048,128]{1,0:T(8,128)(2,1)} fusion(f32[2048,128]{1,0:T(8,128)} %shard_map.203, bf16[2048,128]{1,0:T(8,128)(2,1)S(1)} %get-tuple-element.18), kind=kLoop, calls=%fused_computation.25 | loop fusion | flops 786432 | bytes 2097152 | tf_op jit(solution)/shard_map/convert_element_type | solution.py:509
  (55 shorter events, 5.9 us)
Async XLA Ops:
  0.0 72.1 %copy-start = (bf16[128,256]{1,0:T(8,128)(2,1)S(1)}, bf16[128,256]{1,0:T(8,128)(2,1)}, u32[]{:S(2)}) copy-start(bf16[128,256]{1,0:T(8,128)(2,1)} %param.39) | copy-start | bytes 196612
  1.3 3.0 %dynamic-slice-start = ((s32[12288]{0:T(1024)}, s32[]{:T(128)}), s32[6144]{0:T(1024)S(1)}, s32[]{:S(2)}) async-start(s32[12288]{0:T(1024)} %param.25, s32[]{:T(128)} %select_n.10), calls=%async_computation | async-start | bytes 49664 | tf_op jit(solution)/shard_map/dynamic_slice | solution.py:263
  2.0 4.4 %copy-start.3 = (s32[6144]{0:T(1024)}, s32[6144]{0:T(1024)S(1)}, u32[]{:S(2)}) copy-start(s32[6144]{0:T(1024)S(1)} %dynamic_slice.7) | copy-start | bytes 73732
  4.2 2.2 %copy-start.7 = (s32[1,4,512]{2,1,0:T(4,128)S(1)}, s32[1,4,512]{2,1,0:T(4,128)}, u32[]{:S(2)}) copy-start(s32[1,4,512]{2,1,0:T(4,128)} %param.28) | copy-start | bytes 24580
  4.3 2.2 %copy-start.1 = (bf16[2048,128]{1,0:T(8,128)(2,1)S(1)}, bf16[2048,128]{1,0:T(8,128)(2,1)}, u32[]{:S(2)}) copy-start(bf16[2048,128]{1,0:T(8,128)(2,1)} %own_ref.1) | copy-start | bytes 1572868
  10.2 21.4 %copy-start.2 = (bf16[2048,128]{1,0:T(8,128)(2,1)S(1)}, bf16[2048,128]{1,0:T(8,128)(2,1)}, u32[]{:S(2)}) copy-start(bf16[2048,128]{1,0:T(8,128)(2,1)} %own_ref.1) | copy-start | bytes 1572868
  58.4 7.4 %copy-start.5 = (bf16[256,128]{1,0:T(8,128)(2,1)S(1)}, bf16[256,128]{1,0:T(8,128)(2,1)}, u32[]{:S(2)}) copy-start(bf16[256,128]{1,0:T(8,128)(2,1)} %param.33) | copy-start | bytes 196612
  60.7 5.3 %copy-start.12 = (bf16[128,128]{1,0:T(8,128)(2,1)S(1)}, bf16[128,128]{1,0:T(8,128)(2,1)}, u32[]{:S(2)}) copy-start(bf16[128,128]{1,0:T(8,128)(2,1)} %param.34) | copy-start | bytes 98308
  66.1 1.9 %copy-start.4 = (bf16[128,128]{1,0:T(8,128)(2,1)S(1)}, bf16[128,128]{1,0:T(8,128)(2,1)}, u32[]{:S(2)}) copy-start(bf16[128,128]{1,0:T(8,128)(2,1)} %param.35) | copy-start | bytes 98308
  68.0 1.4 %copy-start.9 = (f32[128]{0:T(128)S(1)}, f32[128]{0:T(128)}, u32[]{:S(2)}) copy-start(f32[128]{0:T(128)} %param.36) | copy-start | bytes 1540
  68.7 2.6 %copy-start.10 = (f32[128]{0:T(128)S(1)}, f32[128]{0:T(128)}, u32[]{:S(2)}) copy-start(f32[128]{0:T(128)} %param.37) | copy-start | bytes 1540
  68.8 2.6 %copy-start.14 = (bf16[128,64]{0,1:T(8,128)(2,1)S(1)}, bf16[128,64]{0,1:T(8,128)(2,1)}, u32[]{:S(2)}) copy-start(bf16[128,64]{0,1:T(8,128)(2,1)} %param.38) | copy-start | bytes 49156
  69.4 2.7 %copy-start.8 = (f32[4]{0:T(128)S(1)}, f32[4]{0:T(128)}, u32[]{:S(2)}) copy-start(f32[4]{0:T(128)} %param.40) | copy-start | bytes 52
  74.2 17.4 %copy-start.11 = (f32[2,4,16,16]{3,2,1,0:T(8,128)S(1)}, f32[2,4,16,16]{3,2,1,0:T(8,128)}, u32[]{:S(2)}) copy-start(f32[2,4,16,16]{3,2,1,0:T(8,128)} %param.41) | copy-start | bytes 24580
  74.2 18.7 %copy-start.13 = (f32[4,16,16]{2,1,0:T(8,128)S(1)}, f32[4,16,16]{2,1,0:T(8,128)}, u32[]{:S(2)}) copy-start(f32[4,16,16]{2,1,0:T(8,128)} %param.42) | copy-start | bytes 12292
  93.6 0.7 copy-start.6

commit v6 on v5

--- a/solution.py
+++ b/solution.py
@@ -260,8 +260,9 @@
     nodes = own_rows.shape[0]
     turns = share // chunk
     scalars = jnp.stack([first_row // chunk, first_row, tally]).astype(jnp.int32)
-    send_ids = lax.dynamic_slice_in_dim(send_ids, first_row, share, 0)
-    recv_ids = lax.dynamic_slice_in_dim(recv_ids, first_row, share, 0)
+    both_ids = lax.dynamic_slice_in_dim(jnp.stack([send_ids, recv_ids]), first_row, share, 1)
+    columns = both_ids.reshape(2, share, 1)
+    recv_ids = both_ids[1]
     ext_wide = extended.reshape(extended.shape[0] // fold, fold * width)
     own_wide = own_rows.reshape(nodes // fold, fold * width)
     full = lambda shape: pl.BlockSpec(shape, lambda i, s: (0,) * len(shape))
@@ -289,8 +290,8 @@
     )(
         scalars,
         edges,
-        send_ids.reshape(share, 1),
-        recv_ids.reshape(share, 1),
+        columns[0],
+        columns[1],
         recv_ids.reshape(turns, 1, chunk),
         ext_wide,
         own_wide,
@@ -299,7 +300,7 @@
         gamma,
         gain.reshape(1, width).astype(jnp.float32),
     )
-    return total.reshape(nodes, width)
+    return total
 
 
 def psum_slices(numer, denom):
@@ -481,7 +482,7 @@
         share,
         active_link_tally[0],
     )
-    summed = sibling_sum(total, 2)
+    summed = sibling_sum(total, 2).astype(jnp.bfloat16).reshape(vertex_state.shape)
     refreshed_vertices = node_section(
         vertex_state,
         summed.astype(jnp.bfloat16),

time: 105 us -> 104 us (level)
  other arithmetic: 6.94 us -> 9.11 us
  local copies, waits for them, and re-layouts: 13.5 us -> 11.4 us
  matrix products: 12.2 us -> 11 us
    reshape x3 -> x1, local copies, waits for them, and re-layouts: 6.73 us -> 0.32 us  [body(): sibling_sum(total, 2).astype(jnp.bfloat16).reshape(vertex_state.shape)]
    squeeze x0 -> x2, local copies, waits for them, and re-layouts: none -> 4.4 us  [the longest x1 2.22 us: edge_messages(): columns[1]]
    convert_element_type x0 -> x1, other arithmetic: none -> 1.3 us  [body(): sibling_sum(total, 2).astype(jnp.bfloat16).reshape(vertex_state.shape)]
    dot_general x1, matrix products: 1.92 us -> 0.69 us  [node_section(): jnp.dot(node_one, vertex_layer_beta, preferred_element_type=jnp.float32)]
where the time goes in v6:
time: 104 us; the launch traced here: 103 us
  Pallas kernels  70.7 us (68%)
  local copies, waits for them, and re-layouts  11.4 us (11%)
  matrix products  11 us (11%)
  other arithmetic  9.11 us (9%)
    pallas_call x1, Pallas kernels, edge_messages(): pl.pallas_call(functools.partial(_edge_kernel, fold), out_shape=jax.Shape...  25.8 us
    pallas_call x1, Pallas kernels, exchange_halos(): pl.pallas_call(functools.partial(_halo_kernel, offsets), out_shape=jax.Sh...  18.8 us
    pallas_call x1, Pallas kernels, dom_sum(): pl.pallas_call(functools.partial(_radix_kernel, radix, steps), out_shape=...  14.3 us
    pallas_call x2, Pallas kernels, sibling_sum(): pl.pallas_call(_sibling_kernel, out_shape=jax.ShapeDtypeStruct(x.shape, j...  11.8 us
    dot_general x1, matrix products, pick_rows(): jnp.dot(selector, table, preferred_element_type=jnp.float32)  3.68 us
    reshape x1, local copies, waits for them, and re-layouts, edge_messages(): ext_wide = extended.reshape(extended.shape[0] // fold, fold * width)  2.51 us
    squeeze x1, local copies, waits for them, and re-layouts, edge_messages(): columns[1]  2.22 us
    squeeze x1, local copies, waits for them, and re-layouts, edge_messages(): columns[0]  2.18 us

profile of v6, /device:TPU:1, one launch (start us, length us, event | category | flops | bytes accessed | tf_op | source)
XLA Modules:
  0.0 103.1 jit_solution(509192121849952302)
XLA Ops:
  1.3 0.9 fusion.18
  2.2 0.6 fusion.37
  2.8 2.2 %copy.23.src_ref = s32[6144,1]{1,0:T(8,128)} copy(s32[6144,1]{0,1:T(1,128)S(1)} %get-tuple-element.21) | data formatting | bytes 49152 | tf_op jit(solution)/shard_map/squeeze | solution.py:293
  5.0 2.2 %copy.24.dst_ref = s32[6144,1]{1,0:T(8,128)} copy(s32[6144,1]{0,1:T(1,128)S(1)} %get-tuple-element.20) | data formatting | bytes 49152 | tf_op jit(solution)/shard_map/squeeze | solution.py:294
  7.2 3.7 %fusion.2 = bf16[2048,128]{1,0:T(8,128)(2,1)} fusion(bf16[2048,128]{1,0:T(8,128)(2,1)S(1)} %copy-done.1, s32[2048]{0:T(1024)S(1)} %bitcast.65), kind=kOutput, calls=%fused_computation.4 | convolution fusion | flops 1078198272 | bytes 1056768 | tf_op jit(solution)/shard_map/dot_general | solution.py:405
  10.9 18.8 %shard_map.199 = bf16[4096,128]{1,0:T(8,128)(2,1)} custom-call(bf16[2048,128]{1,0:T(8,128)(2,1)} %own_ref.1, bf16[4,512,128]{2,1,0:T(8,128)(2,1)} %bitcast.59), custom_call_target="tpu_custom_call" | custom-call | tf_op jit(solution)/shard_map/pallas_call | solution.py:149
  29.8 2.5 %reshape.104.ext_ref = bf16[1024,512]{1,0:T(8,128)(2,1)} reshape(bf16[4096,128]{1,0:T(8,128)(2,1)} %shard_map.199) | data formatting | bytes 2097152 | tf_op jit(solution)/shard_map/reshape | solution.py:266
  32.3 1.1 %reshape.105.own_ref = bf16[512,512]{1,0:T(8,128)(2,1)} reshape(bf16[2048,128]{1,0:T(8,128)(2,1)S(1)} %copy-done.2) | data formatting | bytes 1048576 | tf_op jit(solution)/shard_map/reshape | solution.py:267
  33.4 25.8 %shard_map.200.x_ref = f32[512,512]{1,0:T(8,128)} custom-call(s32[3]{0:T(128)} %pad_add_fusion.scalars, bf16[12288,128]{1,0:T(8,128)(2,1)} %edge_ref.1, s32[6144,1]{1,0:T(8,128)} %copy.23.src_ref, s32[6144,1]{1,0:T(8,128)} %copy.24.dst_ref, s32[6,1,1024]{2,1,0:T(1,128)} %bitcast.61, bf16[1024,512]{1,0:T(8,128)(2,1)} %reshape.104.ext_ref, ...), custom_call_target="tpu_custom_call" | custom-call | tf_op jit(solution)/shard_map/pallas_call | solution.py:286
  59.2 5.0 %shard_map.201 = f32[512,512]{1,0:T(8,128)} custom-call(f32[512,512]{1,0:T(8,128)} %shard_map.200.x_ref), custom_call_target="tpu_custom_call" | custom-call | tf_op jit(solution)/shard_map/pallas_call | solution.py:179
  64.2 1.3 %convert_element_type.52 = bf16[512,512]{1,0:T(8,128)(2,1)S(1)} convert(f32[512,512]{1,0:T(8,128)} %shard_map.201) | non-fusion elementwise | flops 262144 | bytes 1572864 | tf_op jit(solution)/shard_map/convert_element_type | solution.py:485
  66.1 0.7 multiply_convert_fusion
  67.6 0.6 multiply_reduce_fusion
  68.3 1.2 %convert_reduce_fusion = (f32[2048]{0:T(1024)S(1)}, bf16[2048,128]{1,0:T(8,128)(2,1)S(1)}) fusion(f32[128]{0:T(128)S(1)} %copy-done.8, f32[2048]{0:T(1024)S(1)} %add_rsqrt_fusion.1, f32[2048,128]{1,0:T(8,128)S(1)} %copy.25, f32[2048]{0:T(1024)S(1)} %broadcast_multiply_fusion.1, bf16[2048,128]{1,0:T(8,128)(2,1)S(1)} %copy-done.2), kind=kLoop, calls=%fused_computation.17 | loop fusion | flops 2095104 | bytes 2122240 | tf_op jit(solution)/shard_map/reduce_sum | solution.py:319
  69.5 0.6 fusion.8
  70.2 0.8 convolution_convert_fusion.2
  71.0 0.9 fusion.35
  73.9 0.6 fusion.29.x_ref
  74.5 14.3 %shard_map.202 = f32[40,128]{1,0:T(8,128)} custom-call(f32[40,128]{1,0:T(8,128)} %fusion.29.x_ref), custom_call_target="tpu_custom_call" | custom-call | tf_op jit(solution)/shard_map/pallas_call | solution.py:77
  88.8 0.7 slice.44
  89.6 0.7 slice.45
  93.2 1.1 %convolution_convert_fusion.x_ref = bf16[2048,128]{1,0:T(8,128)(2,1)} fusion(bf16[2048,64]{0,1:T(8,128)(2,1)S(1)} %bitcast.60, bf16[64,128]{1,0:T(8,128)(2,1)S(1)} %copy-done.5), kind=kOutput, calls=%fused_computation.5 | convolution fusion | flops 33816576 | bytes 802816 | tf_op jit(solution)/shard_map/dot_general | solution.py:505
  94.3 6.7 %shard_map.203 = f32[2048,128]{1,0:T(8,128)} custom-call(bf16[2048,128]{1,0:T(8,128)(2,1)} %convolution_convert_fusion.x_ref), custom_call_target="tpu_custom_call" | custom-call | tf_op jit(solution)/shard_map/pallas_call | solution.py:179
  101.0 2.1 %fusion.11 = bf16[2048,128]{1,0:T(8,128)(2,1)} fusion(f32[2048,128]{1,0:T(8,128)} %shard_map.203, bf16[2048,128]{1,0:T(8,128)(2,1)S(1)} %get-tuple-element.18), kind=kLoop, calls=%fused_computation.25 | loop fusion | flops 786432 | bytes 2097152 | tf_op jit(solution)/shard_map/convert_element_type | solution.py:510
  (53 shorter events, 6.8 us)
Async XLA Ops:
  0.0 71.0 %copy-start = (bf16[128,256]{1,0:T(8,128)(2,1)S(1)}, bf16[128,256]{1,0:T(8,128)(2,1)}, u32[]{:S(2)}) copy-start(bf16[128,256]{1,0:T(8,128)(2,1)} %param.39) | copy-start | bytes 196612
  5.0 2.2 %copy-start.6 = (s32[1,4,512]{2,1,0:T(4,128)S(1)}, s32[1,4,512]{2,1,0:T(4,128)}, u32[]{:S(2)}) copy-start(s32[1,4,512]{2,1,0:T(4,128)} %param.28) | copy-start | bytes 24580
  5.0 2.2 %copy-start.1 = (bf16[2048,128]{1,0:T(8,128)(2,1)S(1)}, bf16[2048,128]{1,0:T(8,128)(2,1)}, u32[]{:S(2)}) copy-start(bf16[2048,128]{1,0:T(8,128)(2,1)} %own_ref.1) | copy-start | bytes 1572868
  10.9 21.4 %copy-start.2 = (bf16[2048,128]{1,0:T(8,128)(2,1)S(1)}, bf16[2048,128]{1,0:T(8,128)(2,1)}, u32[]{:S(2)}) copy-start(bf16[2048,128]{1,0:T(8,128)(2,1)} %own_ref.1) | copy-start | bytes 1572868
  59.2 6.7 %copy-start.4 = (bf16[256,128]{1,0:T(8,128)(2,1)S(1)}, bf16[256,128]{1,0:T(8,128)(2,1)}, u32[]{:S(2)}) copy-start(bf16[256,128]{1,0:T(8,128)(2,1)} %param.33) | copy-start | bytes 196612
  64.2 1.9 %copy-start.11 = (bf16[128,128]{1,0:T(8,128)(2,1)S(1)}, bf16[128,128]{1,0:T(8,128)(2,1)}, u32[]{:S(2)}) copy-start(bf16[128,128]{1,0:T(8,128)(2,1)} %param.34) | copy-start | bytes 98308
  66.1 0.8 copy-start.3
  66.9 1.4 %copy-start.8 = (f32[128]{0:T(128)S(1)}, f32[128]{0:T(128)}, u32[]{:S(2)}) copy-start(f32[128]{0:T(128)} %param.36) | copy-start | bytes 1540
  67.6 2.6 %copy-start.9 = (f32[128]{0:T(128)S(1)}, f32[128]{0:T(128)}, u32[]{:S(2)}) copy-start(f32[128]{0:T(128)} %param.37) | copy-start | bytes 1540
  67.6 2.6 %copy-start.13 = (bf16[128,64]{0,1:T(8,128)(2,1)S(1)}, bf16[128,64]{0,1:T(8,128)(2,1)}, u32[]{:S(2)}) copy-start(bf16[128,64]{0,1:T(8,128)(2,1)} %param.38) | copy-start | bytes 49156
  68.3 2.7 %copy-start.7 = (f32[4]{0:T(128)S(1)}, f32[4]{0:T(128)}, u32[]{:S(2)}) copy-start(f32[4]{0:T(128)} %param.40) | copy-start | bytes 52
  73.0 17.4 %copy-start.10 = (f32[2,4,16,16]{3,2,1,0:T(8,128)S(1)}, f32[2,4,16,16]{3,2,1,0:T(8,128)}, u32[]{:S(2)}) copy-start(f32[2,4,16,16]{3,2,1,0:T(8,128)} %param.41) | copy-start | bytes 24580
  73.0 18.7 %copy-start.12 = (f32[4,16,16]{2,1,0:T(8,128)S(1)}, f32[4,16,16]{2,1,0:T(8,128)}, u32[]{:S(2)}) copy-start(f32[4,16,16]{2,1,0:T(8,128)} %param.42) | copy-start | bytes 12292
  92.4 0.7 copy-start.5

commit v7 on v6

--- a/solution.py
+++ b/solution.py
@@ -94,7 +94,7 @@
     core = lax.axis_index("head")
     sibling = 1 - core
     rows = own_ref.shape[0]
-    halo = out_ref.shape[1]
+    halo = out_ref.shape[0] // len(offsets)
     half = halo // 2
     mesh_ids = pl.DeviceIdType.MESH
     barrier = pltpu.get_barrier_semaphore()
@@ -107,7 +107,7 @@
     sends = []
     for k, offset in enumerate(offsets):
         copy = pltpu.make_async_remote_copy(
-            src_ref=out_ref.at[k, pl.ds(core * half, half)],
+            src_ref=out_ref.at[pl.ds(k * halo + core * half, half)],
             dst_ref=ext_ref.at[pl.ds(rows + k * halo + core * half, half)],
             send_sem=send_sem.at[k],
             recv_sem=recv_sem.at[k],
@@ -144,8 +144,7 @@
 
 
 def exchange_halos(own_rows, outgoing, offsets):
-    rows = own_rows.shape[0]
-    total = rows + outgoing.shape[0] * outgoing.shape[1]
+    total = own_rows.shape[0] + outgoing.shape[0]
     return pl.pallas_call(
         functools.partial(_halo_kernel, offsets),
         out_shape=jax.ShapeDtypeStruct((total, own_rows.shape[1]), own_rows.dtype),
@@ -257,14 +256,14 @@
 def edge_messages(edges, send_ids, recv_ids, extended, own_rows, alpha, beta, gamma, gain,
                   first_row, share, tally, chunk=1024, fold=FOLD):
     slots, width = edges.shape
-    nodes = own_rows.shape[0]
+    nodes = own_rows.shape[0] * fold
     turns = share // chunk
     scalars = jnp.stack([first_row // chunk, first_row, tally]).astype(jnp.int32)
     both_ids = lax.dynamic_slice_in_dim(jnp.stack([send_ids, recv_ids]), first_row, share, 1)
     columns = both_ids.reshape(2, share, 1)
     recv_ids = both_ids[1]
-    ext_wide = extended.reshape(extended.shape[0] // fold, fold * width)
-    own_wide = own_rows.reshape(nodes // fold, fold * width)
+    ext_wide = extended
+    own_wide = own_rows
     full = lambda shape: pl.BlockSpec(shape, lambda i, s: (0,) * len(shape))
     grid_spec = pltpu.PrefetchScalarGridSpec(
         num_scalar_prefetch=1,
@@ -462,10 +461,12 @@
     feature_width = vertex_state.shape[1]
     capacity = link_state_slotted.shape[0]
     offsets = (1, -1, 2, -2)
-    outgoing = pick_rows(vertex_state, halo_outgoing_ids[0].reshape(-1))
-    extended = exchange_halos(
-        vertex_state, outgoing.reshape(halo_outgoing_ids.shape[1:] + (feature_width,)), offsets
-    )
+    own_wide = vertex_state.reshape(node_count // FOLD, FOLD * feature_width)
+    picked_ids = halo_outgoing_ids[0].reshape(-1, FOLD)
+    outgoing = jnp.concatenate(
+        [pick_rows(vertex_state, picked_ids[:, j]) for j in range(FOLD)], axis=1
+    )
+    extended = exchange_halos(own_wide, outgoing, offsets)
     share = capacity // lax.axis_size("head")
     first_row = lax.axis_index("head") * share
     total = edge_messages(
@@ -473,7 +474,7 @@
         source_vertex_ids,
         target_vertex_ids,
         extended,
-        vertex_state,
+        own_wide,
         link_layer_alpha,
         link_layer_beta,
         link_layer_gamma,

time: 104 us -> 103 us (level)
  local copies, waits for them, and re-layouts: 11.4 us -> 9.7 us
    reshape x2 -> x1, local copies, waits for them, and re-layouts: 3.62 us -> 1.11 us  [body(): own_wide = vertex_state.reshape(node_count // FOLD, FOLD * feature_width)]
    dot_general x1 -> x4, matrix products: 3.68 us -> 3.39 us  [pick_rows(): jnp.dot(selector, table, preferred_element_type=jnp.float32)]
where the time goes in v7:
time: 103 us; the launch traced here: 102 us
  Pallas kernels  70.7 us (69%)
  matrix products  10.7 us (10%)
  other arithmetic  9.95 us (10%)
  local copies, waits for them, and re-layouts  9.7 us (9%)
  between operations  1.03 us (1%)
    pallas_call x1, Pallas kernels, edge_messages(): pl.pallas_call(functools.partial(_edge_kernel, fold), out_shape=jax.Shape...  25.8 us
    pallas_call x1, Pallas kernels, exchange_halos(): pl.pallas_call(functools.partial(_halo_kernel, offsets), out_shape=jax.Sh...  18.8 us
    pallas_call x1, Pallas kernels, dom_sum(): pl.pallas_call(functools.partial(_radix_kernel, radix, steps), out_shape=...  14.3 us
    pallas_call x2, Pallas kernels, sibling_sum(): pl.pallas_call(_sibling_kernel, out_shape=jax.ShapeDtypeStruct(x.shape, j...  11.8 us
    dot_general x4, matrix products, pick_rows(): jnp.dot(selector, table, preferred_element_type=jnp.float32)  3.39 us
    squeeze x1, local copies, waits for them, and re-layouts, edge_messages(): columns[1]  2.22 us
    squeeze x1, local copies, waits for them, and re-layouts, edge_messages(): columns[0]  2.18 us
    convert_element_type x1, other arithmetic, body(): (refreshed_vertices.astype(jnp.float32) + projected.astype(jnp.float32))....  2.12 us

profile of v7, /device:TPU:1, one launch (start us, length us, event | category | flops | bytes accessed | tf_op | source)
XLA Modules:
  0.0 102.0 jit_solution(16209117041241397879)
XLA Ops:
  1.3 0.9 fusion.27
  2.2 0.6 fusion.46
  2.8 2.2 %copy.31.src_ref = s32[6144,1]{1,0:T(8,128)} copy(s32[6144,1]{0,1:T(1,128)S(1)} %get-tuple-element.25) | data formatting | bytes 49152 | tf_op jit(solution)/shard_map/squeeze | solution.py:292
  5.0 2.2 %copy.32.dst_ref = s32[6144,1]{1,0:T(8,128)} copy(s32[6144,1]{0,1:T(1,128)S(1)} %get-tuple-element.24) | data formatting | bytes 49152 | tf_op jit(solution)/shard_map/squeeze | solution.py:293
  8.1 0.8 fusion.13
  8.9 0.8 fusion.14
  9.8 0.8 fusion.15
  10.6 0.8 fusion.16
  11.5 0.8 pad_maximum_fusion.out_ref
  12.3 1.1 %reshape.96.own_ref = bf16[512,512]{1,0:T(8,128)(2,1)} reshape(bf16[2048,128]{1,0:T(8,128)(2,1)S(1)} %copy-done.1) | data formatting | bytes 1048576 | tf_op jit(solution)/shard_map/reshape | solution.py:464
  13.4 18.8 %shard_map.199.ext_ref = bf16[1024,512]{1,0:T(8,128)(2,1)} custom-call(bf16[512,512]{1,0:T(8,128)(2,1)} %reshape.96.own_ref, bf16[512,512]{1,0:T(8,128)(2,1)} %pad_maximum_fusion.out_ref), custom_call_target="tpu_custom_call" | custom-call | tf_op jit(solution)/shard_map/pallas_call | solution.py:148
  32.2 25.8 %shard_map.200.x_ref = f32[512,512]{1,0:T(8,128)} custom-call(s32[3]{0:T(128)} %pad_add_fusion.scalars, bf16[12288,128]{1,0:T(8,128)(2,1)} %edge_ref.1, s32[6144,1]{1,0:T(8,128)} %copy.31.src_ref, s32[6144,1]{1,0:T(8,128)} %copy.32.dst_ref, s32[6,1,1024]{2,1,0:T(1,128)} %bitcast.60, bf16[1024,512]{1,0:T(8,128)(2,1)} %shard_map.199.ext_ref, ...), custom_call_target="tpu_custom_call" | custom-call | tf_op jit(solution)/shard_map/pallas_call | solution.py:285
  58.0 5.0 %shard_map.201 = f32[512,512]{1,0:T(8,128)} custom-call(f32[512,512]{1,0:T(8,128)} %shard_map.200.x_ref), custom_call_target="tpu_custom_call" | custom-call | tf_op jit(solution)/shard_map/pallas_call | solution.py:178
  63.1 1.3 %convert_element_type.67 = bf16[512,512]{1,0:T(8,128)(2,1)S(1)} convert(f32[512,512]{1,0:T(8,128)} %shard_map.201) | non-fusion elementwise | flops 262144 | bytes 1572864 | tf_op jit(solution)/shard_map/convert_element_type | solution.py:486
  65.0 0.7 multiply_convert_fusion
  67.1 1.2 %convert_reduce_fusion = (f32[2048]{0:T(1024)S(1)}, bf16[2048,128]{1,0:T(8,128)(2,1)S(1)}) fusion(f32[128]{0:T(128)S(1)} %copy-done.7, f32[2048]{0:T(1024)S(1)} %add_rsqrt_fusion.1, f32[2048,128]{1,0:T(8,128)S(1)} %copy.33, f32[2048]{0:T(1024)S(1)} %broadcast_multiply_fusion.1, bf16[2048,128]{1,0:T(8,128)(2,1)S(1)} %copy-done.1), kind=kLoop, calls=%fused_computation.25 | loop fusion | flops 2095104 | bytes 2122240 | tf_op jit(solution)/shard_map/reduce_sum | solution.py:318
  69.0 0.8 convolution_convert_fusion.2
  69.8 0.9 fusion.44
  73.3 14.3 %shard_map.202 = f32[40,128]{1,0:T(8,128)} custom-call(f32[40,128]{1,0:T(8,128)} %fusion.38.x_ref), custom_call_target="tpu_custom_call" | custom-call | tf_op jit(solution)/shard_map/pallas_call | solution.py:77
  87.7 0.7 slice.60
  88.5 0.7 slice.61
  92.0 1.1 %convolution_convert_fusion.x_ref = bf16[2048,128]{1,0:T(8,128)(2,1)} fusion(bf16[2048,64]{0,1:T(8,128)(2,1)S(1)} %bitcast.59, bf16[64,128]{1,0:T(8,128)(2,1)S(1)} %copy-done.4), kind=kOutput, calls=%fused_computation.9 | convolution fusion | flops 33816576 | bytes 802816 | tf_op jit(solution)/shard_map/dot_general | solution.py:506
  93.1 6.7 %shard_map.203 = f32[2048,128]{1,0:T(8,128)} custom-call(bf16[2048,128]{1,0:T(8,128)(2,1)} %convolution_convert_fusion.x_ref), custom_call_target="tpu_custom_call" | custom-call | tf_op jit(solution)/shard_map/pallas_call | solution.py:178
  99.9 2.1 %fusion.20 = bf16[2048,128]{1,0:T(8,128)(2,1)} fusion(f32[2048,128]{1,0:T(8,128)} %shard_map.203, bf16[2048,128]{1,0:T(8,128)(2,1)S(1)} %get-tuple-element.22), kind=kLoop, calls=%fused_computation.37 | loop fusion | flops 786432 | bytes 2097152 | tf_op jit(solution)/shard_map/convert_element_type | solution.py:511
  (55 shorter events, 9.5 us)
Async XLA Ops:
  0.0 69.8 %copy-start = (bf16[128,256]{1,0:T(8,128)(2,1)S(1)}, bf16[128,256]{1,0:T(8,128)(2,1)}, u32[]{:S(2)}) copy-start(bf16[128,256]{1,0:T(8,128)(2,1)} %param.39) | copy-start | bytes 196612
  5.0 2.2 %copy-start.5 = (s32[1,4,512]{2,1,0:T(4,128)S(1)}, s32[1,4,512]{2,1,0:T(4,128)}, u32[]{:S(2)}) copy-start(s32[1,4,512]{2,1,0:T(4,128)} %param.28) | copy-start | bytes 24580
  5.0 3.1 %copy-start.1 = (bf16[2048,128]{1,0:T(8,128)(2,1)S(1)}, bf16[2048,128]{1,0:T(8,128)(2,1)}, u32[]{:S(2)}) copy-start(bf16[2048,128]{1,0:T(8,128)(2,1)} %param.23) | copy-start | bytes 1572868
  58.0 6.7 %copy-start.3 = (bf16[256,128]{1,0:T(8,128)(2,1)S(1)}, bf16[256,128]{1,0:T(8,128)(2,1)}, u32[]{:S(2)}) copy-start(bf16[256,128]{1,0:T(8,128)(2,1)} %param.33) | copy-start | bytes 196612
  63.0 1.9 %copy-start.10 = (bf16[128,128]{1,0:T(8,128)(2,1)S(1)}, bf16[128,128]{1,0:T(8,128)(2,1)}, u32[]{:S(2)}) copy-start(bf16[128,128]{1,0:T(8,128)(2,1)} %param.34) | copy-start | bytes 98308
  65.0 0.8 copy-start.2
  65.7 1.4 %copy-start.7 = (f32[128]{0:T(128)S(1)}, f32[128]{0:T(128)}, u32[]{:S(2)}) copy-start(f32[128]{0:T(128)} %param.36) | copy-start | bytes 1540
  66.4 2.6 %copy-start.8 = (f32[128]{0:T(128)S(1)}, f32[128]{0:T(128)}, u32[]{:S(2)}) copy-start(f32[128]{0:T(128)} %param.37) | copy-start | bytes 1540
  66.4 2.6 %copy-start.12 = (bf16[128,64]{0,1:T(8,128)(2,1)S(1)}, bf16[128,64]{0,1:T(8,128)(2,1)}, u32[]{:S(2)}) copy-start(bf16[128,64]{0,1:T(8,128)(2,1)} %param.38) | copy-start | bytes 49156
  67.1 2.7 %copy-start.6 = (f32[4]{0:T(128)S(1)}, f32[4]{0:T(128)}, u32[]{:S(2)}) copy-start(f32[4]{0:T(128)} %param.40) | copy-start | bytes 52
  71.9 17.4 %copy-start.9 = (f32[2,4,16,16]{3,2,1,0:T(8,128)S(1)}, f32[2,4,16,16]{3,2,1,0:T(8,128)}, u32[]{:S(2)}) copy-start(f32[2,4,16,16]{3,2,1,0:T(8,128)} %param.41) | copy-start | bytes 24580
  71.9 18.7 %copy-start.11 = (f32[4,16,16]{2,1,0:T(8,128)S(1)}, f32[4,16,16]{2,1,0:T(8,128)}, u32[]{:S(2)}) copy-start(f32[4,16,16]{2,1,0:T(8,128)} %param.42) | copy-start | bytes 12292
  91.3 0.7 copy-start.4

commit v8 on v7

--- a/solution.py
+++ b/solution.py
@@ -69,7 +69,7 @@
 
 def dom_sum(flat):
     count = lax.axis_size("dom")
-    radix = 4
+    radix = 8
     steps = 0
     while radix ** (steps + 1) <= count:
         steps += 1

time: 103 us -> 102 us (level)
    pallas_call x2, Pallas kernels: 11.8 us -> 10.7 us  [sibling_sum(): pl.pallas_call(_sibling_kernel, out_shape=jax.ShapeDtypeStruct(x.shape, j...]
where the time goes in v8:
time: 102 us; the launch traced here: 101 us
  Pallas kernels  69.7 us (68%)
  matrix products  10.7 us (10%)
  other arithmetic  9.95 us (10%)
  local copies, waits for them, and re-layouts  9.7 us (10%)
  between operations  1.03 us (1%)
    pallas_call x1, Pallas kernels, edge_messages(): pl.pallas_call(functools.partial(_edge_kernel, fold), out_shape=jax.Shape...  25.8 us
    pallas_call x1, Pallas kernels, exchange_halos(): pl.pallas_call(functools.partial(_halo_kernel, offsets), out_shape=jax.Sh...  18.8 us
    pallas_call x1, Pallas kernels, dom_sum(): pl.pallas_call(functools.partial(_radix_kernel, radix, steps), out_shape=...  14.4 us
    pallas_call x2, Pallas kernels, sibling_sum(): pl.pallas_call(_sibling_kernel, out_shape=jax.ShapeDtypeStruct(x.shape, j...  10.7 us
    dot_general x4, matrix products, pick_rows(): jnp.dot(selector, table, preferred_element_type=jnp.float32)  3.39 us
    squeeze x1, local copies, waits for them, and re-layouts, edge_messages(): columns[1]  2.22 us
    squeeze x1, local copies, waits for them, and re-layouts, edge_messages(): columns[0]  2.18 us
    convert_element_type x1, other arithmetic, body(): (refreshed_vertices.astype(jnp.float32) + projected.astype(jnp.float32))....  2.12 us

profile of v8, /device:TPU:1, one launch (start us, length us, event | category | flops | bytes accessed | tf_op | source)
XLA Modules:
  0.0 101.0 jit_solution(6395242118230433588)
XLA Ops:
  1.3 0.9 fusion.27
  2.2 0.6 fusion.46
  2.8 2.2 %copy.31.src_ref = s32[6144,1]{1,0:T(8,128)} copy(s32[6144,1]{0,1:T(1,128)S(1)} %get-tuple-element.25) | data formatting | bytes 49152 | tf_op jit(solution)/shard_map/squeeze | solution.py:292
  5.0 2.2 %copy.32.dst_ref = s32[6144,1]{1,0:T(8,128)} copy(s32[6144,1]{0,1:T(1,128)S(1)} %get-tuple-element.24) | data formatting | bytes 49152 | tf_op jit(solution)/shard_map/squeeze | solution.py:293
  8.1 0.8 fusion.13
  8.9 0.8 fusion.14
  9.8 0.8 fusion.15
  10.6 0.8 fusion.16
  11.5 0.8 pad_maximum_fusion.out_ref
  12.3 1.1 %reshape.96.own_ref = bf16[512,512]{1,0:T(8,128)(2,1)} reshape(bf16[2048,128]{1,0:T(8,128)(2,1)S(1)} %copy-done.1) | data formatting | bytes 1048576 | tf_op jit(solution)/shard_map/reshape | solution.py:464
  13.4 18.8 %shard_map.199.ext_ref = bf16[1024,512]{1,0:T(8,128)(2,1)} custom-call(bf16[512,512]{1,0:T(8,128)(2,1)} %reshape.96.own_ref, bf16[512,512]{1,0:T(8,128)(2,1)} %pad_maximum_fusion.out_ref), custom_call_target="tpu_custom_call" | custom-call | tf_op jit(solution)/shard_map/pallas_call | solution.py:148
  32.2 25.8 %shard_map.200.x_ref = f32[512,512]{1,0:T(8,128)} custom-call(s32[3]{0:T(128)} %pad_add_fusion.scalars, bf16[12288,128]{1,0:T(8,128)(2,1)} %edge_ref.1, s32[6144,1]{1,0:T(8,128)} %copy.31.src_ref, s32[6144,1]{1,0:T(8,128)} %copy.32.dst_ref, s32[6,1,1024]{2,1,0:T(1,128)} %bitcast.60, bf16[1024,512]{1,0:T(8,128)(2,1)} %shard_map.199.ext_ref, ...), custom_call_target="tpu_custom_call" | custom-call | tf_op jit(solution)/shard_map/pallas_call | solution.py:285
  58.0 5.0 %shard_map.201 = f32[512,512]{1,0:T(8,128)} custom-call(f32[512,512]{1,0:T(8,128)} %shard_map.200.x_ref), custom_call_target="tpu_custom_call" | custom-call | tf_op jit(solution)/shard_map/pallas_call | solution.py:178
  63.1 1.3 %convert_element_type.67 = bf16[512,512]{1,0:T(8,128)(2,1)S(1)} convert(f32[512,512]{1,0:T(8,128)} %shard_map.201) | non-fusion elementwise | flops 262144 | bytes 1572864 | tf_op jit(solution)/shard_map/convert_element_type | solution.py:486
  65.0 0.7 multiply_convert_fusion
  67.1 1.2 %convert_reduce_fusion = (f32[2048]{0:T(1024)S(1)}, bf16[2048,128]{1,0:T(8,128)(2,1)S(1)}) fusion(f32[128]{0:T(128)S(1)} %copy-done.7, f32[2048]{0:T(1024)S(1)} %add_rsqrt_fusion.1, f32[2048,128]{1,0:T(8,128)S(1)} %copy.33, f32[2048]{0:T(1024)S(1)} %broadcast_multiply_fusion.1, bf16[2048,128]{1,0:T(8,128)(2,1)S(1)} %copy-done.1), kind=kLoop, calls=%fused_computation.25 | loop fusion | flops 2095104 | bytes 2122240 | tf_op jit(solution)/shard_map/reduce_sum | solution.py:318
  69.0 0.8 convolution_convert_fusion.2
  69.8 0.9 fusion.44
  73.3 14.4 %shard_map.202 = f32[40,128]{1,0:T(8,128)} custom-call(f32[40,128]{1,0:T(8,128)} %fusion.38.x_ref), custom_call_target="tpu_custom_call" | custom-call | tf_op jit(solution)/shard_map/pallas_call | solution.py:77
  87.8 0.7 slice.60
  88.6 0.7 slice.61
  92.1 1.1 %convolution_convert_fusion.x_ref = bf16[2048,128]{1,0:T(8,128)(2,1)} fusion(bf16[2048,64]{0,1:T(8,128)(2,1)S(1)} %bitcast.59, bf16[64,128]{1,0:T(8,128)(2,1)S(1)} %copy-done.4), kind=kOutput, calls=%fused_computation.9 | convolution fusion | flops 33816576 | bytes 802816 | tf_op jit(solution)/shard_map/dot_general | solution.py:506
  93.2 5.7 %shard_map.203 = f32[2048,128]{1,0:T(8,128)} custom-call(bf16[2048,128]{1,0:T(8,128)(2,1)} %convolution_convert_fusion.x_ref), custom_call_target="tpu_custom_call" | custom-call | tf_op jit(solution)/shard_map/pallas_call | solution.py:178
  98.9 2.1 %fusion.20 = bf16[2048,128]{1,0:T(8,128)(2,1)} fusion(f32[2048,128]{1,0:T(8,128)} %shard_map.203, bf16[2048,128]{1,0:T(8,128)(2,1)S(1)} %get-tuple-element.22), kind=kLoop, calls=%fused_computation.37 | loop fusion | flops 786432 | bytes 2097152 | tf_op jit(solution)/shard_map/convert_element_type | solution.py:511
  (55 shorter events, 9.5 us)
Async XLA Ops:
  0.0 69.8 %copy-start = (bf16[128,256]{1,0:T(8,128)(2,1)S(1)}, bf16[128,256]{1,0:T(8,128)(2,1)}, u32[]{:S(2)}) copy-start(bf16[128,256]{1,0:T(8,128)(2,1)} %param.39) | copy-start | bytes 196612
  5.0 2.2 %copy-start.5 = (s32[1,4,512]{2,1,0:T(4,128)S(1)}, s32[1,4,512]{2,1,0:T(4,128)}, u32[]{:S(2)}) copy-start(s32[1,4,512]{2,1,0:T(4,128)} %param.28) | copy-start | bytes 24580
  5.0 3.1 %copy-start.1 = (bf16[2048,128]{1,0:T(8,128)(2,1)S(1)}, bf16[2048,128]{1,0:T(8,128)(2,1)}, u32[]{:S(2)}) copy-start(bf16[2048,128]{1,0:T(8,128)(2,1)} %param.23) | copy-start | bytes 1572868
  58.0 6.7 %copy-start.3 = (bf16[256,128]{1,0:T(8,128)(2,1)S(1)}, bf16[256,128]{1,0:T(8,128)(2,1)}, u32[]{:S(2)}) copy-start(bf16[256,128]{1,0:T(8,128)(2,1)} %param.33) | copy-start | bytes 196612
  63.0 1.9 %copy-start.10 = (bf16[128,128]{1,0:T(8,128)(2,1)S(1)}, bf16[128,128]{1,0:T(8,128)(2,1)}, u32[]{:S(2)}) copy-start(bf16[128,128]{1,0:T(8,128)(2,1)} %param.34) | copy-start | bytes 98308
  65.0 0.8 copy-start.2
  65.7 1.4 %copy-start.7 = (f32[128]{0:T(128)S(1)}, f32[128]{0:T(128)}, u32[]{:S(2)}) copy-start(f32[128]{0:T(128)} %param.36) | copy-start | bytes 1540
  66.4 2.6 %copy-start.8 = (f32[128]{0:T(128)S(1)}, f32[128]{0:T(128)}, u32[]{:S(2)}) copy-start(f32[128]{0:T(128)} %param.37) | copy-start | bytes 1540
  66.4 2.6 %copy-start.12 = (bf16[128,64]{0,1:T(8,128)(2,1)S(1)}, bf16[128,64]{0,1:T(8,128)(2,1)}, u32[]{:S(2)}) copy-start(bf16[128,64]{0,1:T(8,128)(2,1)} %param.38) | copy-start | bytes 49156
  67.1 2.7 %copy-start.6 = (f32[4]{0:T(128)S(1)}, f32[4]{0:T(128)}, u32[]{:S(2)}) copy-start(f32[4]{0:T(128)} %param.40) | copy-start | bytes 52
  71.9 17.5 %copy-start.9 = (f32[2,4,16,16]{3,2,1,0:T(8,128)S(1)}, f32[2,4,16,16]{3,2,1,0:T(8,128)}, u32[]{:S(2)}) copy-start(f32[2,4,16,16]{3,2,1,0:T(8,128)} %param.41) | copy-start | bytes 24580
  71.9 18.8 %copy-start.11 = (f32[4,16,16]{2,1,0:T(8,128)S(1)}, f32[4,16,16]{2,1,0:T(8,128)}, u32[]{:S(2)}) copy-start(f32[4,16,16]{2,1,0:T(8,128)} %param.42) | copy-start | bytes 12292
  91.4 0.7 copy-start.4

commit v9 on v8

--- a/solution.py
+++ b/solution.py
@@ -483,7 +483,8 @@
         share,
         active_link_tally[0],
     )
-    summed = sibling_sum(total, 2).astype(jnp.bfloat16).reshape(vertex_state.shape)
+    summed = sibling_sum(total.astype(jnp.bfloat16), 2).astype(jnp.bfloat16)
+    summed = summed.reshape(vertex_state.shape)
     refreshed_vertices = node_section(
         vertex_state,
         summed.astype(jnp.bfloat16),

time: 102 us -> 103 us (level)
  other arithmetic: 9.95 us -> 12 us
    convert_element_type x1 -> x2, other arithmetic: 1.3 us -> 3.38 us  [body(): summed = sibling_sum(total.astype(jnp.bfloat16), 2).astype(jnp.bfloat16)]
where the time goes in v9:
time: 103 us; the launch traced here: 102 us
  Pallas kernels  68.8 us (67%)
  other arithmetic  12 us (12%)
  matrix products  10.7 us (10%)
  local copies, waits for them, and re-layouts  9.7 us (9%)
  between operations  1.03 us (1%)
    pallas_call x1, Pallas kernels, edge_messages(): pl.pallas_call(functools.partial(_edge_kernel, fold), out_shape=jax.Shape...  25.8 us
    pallas_call x1, Pallas kernels, exchange_halos(): pl.pallas_call(functools.partial(_halo_kernel, offsets), out_shape=jax.Sh...  18.8 us
    pallas_call x1, Pallas kernels, dom_sum(): pl.pallas_call(functools.partial(_radix_kernel, radix, steps), out_shape=...  14.4 us
    pallas_call x2, Pallas kernels, sibling_sum(): pl.pallas_call(_sibling_kernel, out_shape=jax.ShapeDtypeStruct(x.shape, j...  9.78 us
    dot_general x4, matrix products, pick_rows(): jnp.dot(selector, table, preferred_element_type=jnp.float32)  3.39 us
    convert_element_type x2, other arithmetic, body(): summed = sibling_sum(total.astype(jnp.bfloat16), 2).astype(jnp.bfloat16)  3.38 us
    squeeze x1, local copies, waits for them, and re-layouts, edge_messages(): columns[1]  2.22 us
    squeeze x1, local copies, waits for them, and re-layouts, edge_messages(): columns[0]  2.18 us

profile of v9, /device:TPU:1, one launch (start us, length us, event | category | flops | bytes accessed | tf_op | source)
XLA Modules:
  0.0 102.2 jit_solution(12302468361037362505)
XLA Ops:
  1.3 0.9 fusion.27
  2.8 2.2 %copy.31.src_ref = s32[6144,1]{1,0:T(8,128)} copy(s32[6144,1]{0,1:T(1,128)S(1)} %get-tuple-element.25) | data formatting | bytes 49152 | tf_op jit(solution)/shard_map/squeeze | solution.py:292
  5.0 2.2 %copy.32.dst_ref = s32[6144,1]{1,0:T(8,128)} copy(s32[6144,1]{0,1:T(1,128)S(1)} %get-tuple-element.24) | data formatting | bytes 49152 | tf_op jit(solution)/shard_map/squeeze | solution.py:293
  8.1 0.8 fusion.13
  8.9 0.8 fusion.14
  9.8 0.8 fusion.15
  10.6 0.8 fusion.16
  11.5 0.8 pad_maximum_fusion.out_ref
  12.3 1.1 %reshape.96.own_ref = bf16[512,512]{1,0:T(8,128)(2,1)} reshape(bf16[2048,128]{1,0:T(8,128)(2,1)S(1)} %copy-done.1) | data formatting | bytes 1048576 | tf_op jit(solution)/shard_map/reshape | solution.py:464
  13.4 18.8 %shard_map.199.ext_ref = bf16[1024,512]{1,0:T(8,128)(2,1)} custom-call(bf16[512,512]{1,0:T(8,128)(2,1)} %reshape.96.own_ref, bf16[512,512]{1,0:T(8,128)(2,1)} %pad_maximum_fusion.out_ref), custom_call_target="tpu_custom_call" | custom-call | tf_op jit(solution)/shard_map/pallas_call | solution.py:148
  32.2 25.8 %shard_map.200 = f32[512,512]{1,0:T(8,128)} custom-call(s32[3]{0:T(128)} %pad_add_fusion.scalars, bf16[12288,128]{1,0:T(8,128)(2,1)} %edge_ref.1, s32[6144,1]{1,0:T(8,128)} %copy.31.src_ref, s32[6144,1]{1,0:T(8,128)} %copy.32.dst_ref, s32[6,1,1024]{2,1,0:T(1,128)} %bitcast.60, bf16[1024,512]{1,0:T(8,128)(2,1)} %shard_map.199.ext_ref, ...), custom_call_target="tpu_custom_call" | custom-call | tf_op jit(solution)/shard_map/pallas_call | solution.py:285
  58.0 2.1 %convert_element_type.70.x_ref = bf16[512,512]{1,0:T(8,128)(2,1)} convert(f32[512,512]{1,0:T(8,128)} %shard_map.200) | non-fusion elementwise | flops 262144 | bytes 1572864 | tf_op jit(solution)/shard_map/convert_element_type | solution.py:486
  60.1 4.1 %shard_map.201 = f32[512,512]{1,0:T(8,128)} custom-call(bf16[512,512]{1,0:T(8,128)(2,1)} %convert_element_type.70.x_ref), custom_call_target="tpu_custom_call" | custom-call | tf_op jit(solution)/shard_map/pallas_call | solution.py:178
  64.2 1.3 %convert_element_type.71 = bf16[512,512]{1,0:T(8,128)(2,1)S(1)} convert(f32[512,512]{1,0:T(8,128)} %shard_map.201) | non-fusion elementwise | flops 262144 | bytes 1572864 | tf_op jit(solution)/shard_map/convert_element_type | solution.py:486
  66.1 0.7 multiply_convert_fusion
  68.3 1.2 %convert_reduce_fusion = (f32[2048]{0:T(1024)S(1)}, bf16[2048,128]{1,0:T(8,128)(2,1)S(1)}) fusion(f32[128]{0:T(128)S(1)} %copy-done.7, f32[2048]{0:T(1024)S(1)} %add_rsqrt_fusion.1, f32[2048,128]{1,0:T(8,128)S(1)} %copy.33, f32[2048]{0:T(1024)S(1)} %broadcast_multiply_fusion.1, bf16[2048,128]{1,0:T(8,128)(2,1)S(1)} %copy-done.1), kind=kLoop, calls=%fused_computation.25 | loop fusion | flops 2095104 | bytes 2122240 | tf_op jit(solution)/shard_map/reduce_sum | solution.py:318
  70.2 0.8 convolution_convert_fusion.2
  71.0 0.9 fusion.44
  74.5 14.4 %shard_map.202 = f32[40,128]{1,0:T(8,128)} custom-call(f32[40,128]{1,0:T(8,128)} %fusion.38.x_ref), custom_call_target="tpu_custom_call" | custom-call | tf_op jit(solution)/shard_map/pallas_call | solution.py:77
  88.9 0.7 slice.60
  89.7 0.7 slice.61
  93.2 1.1 %convolution_convert_fusion.x_ref = bf16[2048,128]{1,0:T(8,128)(2,1)} fusion(bf16[2048,64]{0,1:T(8,128)(2,1)S(1)} %bitcast.59, bf16[64,128]{1,0:T(8,128)(2,1)S(1)} %copy-done.4), kind=kOutput, calls=%fused_computation.9 | convolution fusion | flops 33816576 | bytes 802816 | tf_op jit(solution)/shard_map/dot_general | solution.py:507
  94.4 5.7 %shard_map.203 = f32[2048,128]{1,0:T(8,128)} custom-call(bf16[2048,128]{1,0:T(8,128)(2,1)} %convolution_convert_fusion.x_ref), custom_call_target="tpu_custom_call" | custom-call | tf_op jit(solution)/shard_map/pallas_call | solution.py:178
  100.0 2.1 %fusion.20 = bf16[2048,128]{1,0:T(8,128)(2,1)} fusion(f32[2048,128]{1,0:T(8,128)} %shard_map.203, bf16[2048,128]{1,0:T(8,128)(2,1)S(1)} %get-tuple-element.22), kind=kLoop, calls=%fused_computation.37 | loop fusion | flops 786432 | bytes 2097152 | tf_op jit(solution)/shard_map/convert_element_type | solution.py:512
  (56 shorter events, 10.2 us)
Async XLA Ops:
  0.0 71.0 %copy-start = (bf16[128,256]{1,0:T(8,128)(2,1)S(1)}, bf16[128,256]{1,0:T(8,128)(2,1)}, u32[]{:S(2)}) copy-start(bf16[128,256]{1,0:T(8,128)(2,1)} %param.39) | copy-start | bytes 196612
  5.0 2.2 %copy-start.5 = (s32[1,4,512]{2,1,0:T(4,128)S(1)}, s32[1,4,512]{2,1,0:T(4,128)}, u32[]{:S(2)}) copy-start(s32[1,4,512]{2,1,0:T(4,128)} %param.28) | copy-start | bytes 24580
  5.0 3.1 %copy-start.1 = (bf16[2048,128]{1,0:T(8,128)(2,1)S(1)}, bf16[2048,128]{1,0:T(8,128)(2,1)}, u32[]{:S(2)}) copy-start(bf16[2048,128]{1,0:T(8,128)(2,1)} %param.23) | copy-start | bytes 1572868
  60.1 5.7 %copy-start.3 = (bf16[256,128]{1,0:T(8,128)(2,1)S(1)}, bf16[256,128]{1,0:T(8,128)(2,1)}, u32[]{:S(2)}) copy-start(bf16[256,128]{1,0:T(8,128)(2,1)} %param.33) | copy-start | bytes 196612
  64.2 1.9 %copy-start.10 = (bf16[128,128]{1,0:T(8,128)(2,1)S(1)}, bf16[128,128]{1,0:T(8,128)(2,1)}, u32[]{:S(2)}) copy-start(bf16[128,128]{1,0:T(8,128)(2,1)} %param.34) | copy-start | bytes 98308
  66.1 0.8 copy-start.2
  66.9 1.4 %copy-start.7 = (f32[128]{0:T(128)S(1)}, f32[128]{0:T(128)}, u32[]{:S(2)}) copy-start(f32[128]{0:T(128)} %param.36) | copy-start | bytes 1540
  67.6 2.6 %copy-start.8 = (f32[128]{0:T(128)S(1)}, f32[128]{0:T(128)}, u32[]{:S(2)}) copy-start(f32[128]{0:T(128)} %param.37) | copy-start | bytes 1540
  67.6 2.6 %copy-start.12 = (bf16[128,64]{0,1:T(8,128)(2,1)S(1)}, bf16[128,64]{0,1:T(8,128)(2,1)}, u32[]{:S(2)}) copy-start(bf16[128,64]{0,1:T(8,128)(2,1)} %param.38) | copy-start | bytes 49156
  68.2 2.7 %copy-start.6 = (f32[4]{0:T(128)S(1)}, f32[4]{0:T(128)}, u32[]{:S(2)}) copy-start(f32[4]{0:T(128)} %param.40) | copy-start | bytes 52
  73.0 17.5 %copy-start.9 = (f32[2,4,16,16]{3,2,1,0:T(8,128)S(1)}, f32[2,4,16,16]{3,2,1,0:T(8,128)}, u32[]{:S(2)}) copy-start(f32[2,4,16,16]{3,2,1,0:T(8,128)} %param.41) | copy-start | bytes 24580
  73.0 18.8 %copy-start.11 = (f32[4,16,16]{2,1,0:T(8,128)S(1)}, f32[4,16,16]{2,1,0:T(8,128)}, u32[]{:S(2)}) copy-start(f32[4,16,16]{2,1,0:T(8,128)} %param.42) | copy-start | bytes 12292
  92.5 0.7 copy-start.4

commit v10 on v8

--- a/solution.py
+++ b/solution.py
@@ -211,7 +211,7 @@
     return rows.astype(jnp.bfloat16)
 
 
-def _edge_kernel(fold, scalars, edge_ref, src_ref, dst_ref, dst_row_ref, ext_ref, own_ref,
+def _edge_kernel(fold, scalars, edge_ref, ids_ref, dst_row_ref, ext_ref, own_ref,
                  alpha_ref, beta_ref, gamma_ref, gain_ref, out_ref):
     step = pl.program_id(0)
     chunk, width = edge_ref.shape
@@ -221,8 +221,8 @@
         out_ref[...] = jnp.zeros_like(out_ref)
 
     edge = edge_ref[...]
-    dst = dst_ref[...]
-    sender = _fold_pick(ext_ref, src_ref[...], fold)
+    dst = ids_ref[1]
+    sender = _fold_pick(ext_ref, ids_ref[0], fold)
     receiver = _fold_pick(own_ref, dst, fold)
     pre = jnp.dot(edge, alpha_ref[0:width], preferred_element_type=jnp.float32)
     pre = pre + jnp.dot(sender, alpha_ref[width : 2 * width], preferred_element_type=jnp.float32)
@@ -270,8 +270,7 @@
         grid=(turns,),
         in_specs=[
             pl.BlockSpec((chunk, width), lambda i, s: (s[0] + i, 0)),
-            pl.BlockSpec((chunk, 1), lambda i, s: (i, 0)),
-            pl.BlockSpec((chunk, 1), lambda i, s: (i, 0)),
+            pl.BlockSpec((2, chunk, 1), lambda i, s: (0, i, 0)),
             pl.BlockSpec((1, 1, chunk), lambda i, s: (i, 0, 0)),
             full(ext_wide.shape),
             full(own_wide.shape),
@@ -289,8 +288,7 @@
     )(
         scalars,
         edges,
-        columns[0],
-        columns[1],
+        columns,
         recv_ids.reshape(turns, 1, chunk),
         ext_wide,
         own_wide,

time: 102 us -> 101 us (level)
    squeeze x2 -> x0, local copies, waits for them, and re-layouts: 4.4 us -> none  [the longest x1 2.22 us: edge_messages(): columns[1]]
    reshape x0 -> x1, local copies, waits for them, and re-layouts: none -> 3.94 us  [edge_messages(): columns = both_ids.reshape(2, share, 1)]
where the time goes in v10:
time: 101 us
  Pallas kernels  69.5 us (69%)
  matrix products  10.7 us (11%)
  other arithmetic  10.1 us (10%)
  local copies, waits for them, and re-layouts  9.25 us (9%)
  between operations  1.06 us (1%)
    pallas_call x1, Pallas kernels, edge_messages(): pl.pallas_call(functools.partial(_edge_kernel, fold), out_shape=jax.Shape...  25.6 us
    pallas_call x1, Pallas kernels, exchange_halos(): pl.pallas_call(functools.partial(_halo_kernel, offsets), out_shape=jax.Sh...  18.8 us
    pallas_call x1, Pallas kernels, dom_sum(): pl.pallas_call(functools.partial(_radix_kernel, radix, steps), out_shape=...  14.4 us
    pallas_call x2, Pallas kernels, sibling_sum(): pl.pallas_call(_sibling_kernel, out_shape=jax.ShapeDtypeStruct(x.shape, j...  10.7 us
    reshape x1, local copies, waits for them, and re-layouts, edge_messages(): columns = both_ids.reshape(2, share, 1)  3.94 us
    dot_general x4, matrix products, pick_rows(): jnp.dot(selector, table, preferred_element_type=jnp.float32)  3.38 us
    convert_element_type x1, other arithmetic, body(): (refreshed_vertices.astype(jnp.float32) + projected.astype(jnp.float32))....  2.12 us

profile of v10, /device:TPU:1, one launch (start us, length us, event | category | flops | bytes accessed | tf_op | source)
XLA Modules:
  0.0 100.6 jit_solution(16553531522365944342)
XLA Ops:
  1.3 0.9 fusion.67
  2.2 3.9 %copy.31.ids_ref = s32[2,6144,1]{2,1,0:T(8,128)} copy(s32[2,6144,1]{1,0,2:T(2,128)S(1)} %fusion.67) | data formatting | bytes 98304 | tf_op jit(solution)/shard_map/reshape | solution.py:263
  7.8 0.8 fusion.13
  8.6 0.8 fusion.14
  9.5 0.8 fusion.15
  10.3 0.8 fusion.16
  11.2 0.8 pad_maximum_fusion.out_ref
  12.0 1.1 %reshape.95.own_ref = bf16[512,512]{1,0:T(8,128)(2,1)} reshape(bf16[2048,128]{1,0:T(8,128)(2,1)S(1)} %copy-done.1) | data formatting | bytes 1048576 | tf_op jit(solution)/shard_map/reshape | solution.py:462
  13.1 18.8 %shard_map.199.ext_ref = bf16[1024,512]{1,0:T(8,128)(2,1)} custom-call(bf16[512,512]{1,0:T(8,128)(2,1)} %reshape.95.own_ref, bf16[512,512]{1,0:T(8,128)(2,1)} %pad_maximum_fusion.out_ref), custom_call_target="tpu_custom_call" | custom-call | tf_op jit(solution)/shard_map/pallas_call | solution.py:148
  31.9 25.6 %shard_map.200.x_ref = f32[512,512]{1,0:T(8,128)} custom-call(s32[3]{0:T(128)} %pad_add_fusion.scalars, bf16[12288,128]{1,0:T(8,128)(2,1)} %edge_ref.1, s32[2,6144,1]{2,1,0:T(8,128)} %copy.31.ids_ref, s32[6,1,1024]{2,1,0:T(1,128)} %bitcast.62, bf16[1024,512]{1,0:T(8,128)(2,1)} %shard_map.199.ext_ref, bf16[512,512]{1,0:T(8,128)(2,1)} %reshape.95.own_ref, ...), custom_call_target="tpu_custom_call" | custom-call | tf_op jit(solution)/shard_map/pallas_call | solution.py:284
  57.5 5.0 %shard_map.201 = f32[512,512]{1,0:T(8,128)} custom-call(f32[512,512]{1,0:T(8,128)} %shard_map.200.x_ref), custom_call_target="tpu_custom_call" | custom-call | tf_op jit(solution)/shard_map/pallas_call | solution.py:178
  62.6 1.3 %convert_element_type.67 = bf16[512,512]{1,0:T(8,128)(2,1)S(1)} convert(f32[512,512]{1,0:T(8,128)} %shard_map.201) | non-fusion elementwise | flops 262144 | bytes 1572864 | tf_op jit(solution)/shard_map/convert_element_type | solution.py:484
  64.5 0.7 multiply_convert_fusion
  66.0 0.6 multiply_reduce_fusion
  66.7 1.2 %convert_reduce_fusion = (f32[2048]{0:T(1024)S(1)}, bf16[2048,128]{1,0:T(8,128)(2,1)S(1)}) fusion(f32[128]{0:T(128)S(1)} %copy-done.9, f32[2048]{0:T(1024)S(1)} %add_rsqrt_fusion.1, f32[2048,128]{1,0:T(8,128)S(1)} %copy.32, f32[2048]{0:T(1024)S(1)} %broadcast_multiply_fusion.1, bf16[2048,128]{1,0:T(8,128)(2,1)S(1)} %copy-done.1), kind=kLoop, calls=%fused_computation.25 | loop fusion | flops 2095104 | bytes 2122240 | tf_op jit(solution)/shard_map/reduce_sum | solution.py:316
  67.9 0.6 fusion.17
  68.6 0.8 convolution_convert_fusion.2
  69.4 0.9 fusion.44
  72.9 14.4 %shard_map.202 = f32[40,128]{1,0:T(8,128)} custom-call(f32[40,128]{1,0:T(8,128)} %fusion.38.x_ref), custom_call_target="tpu_custom_call" | custom-call | tf_op jit(solution)/shard_map/pallas_call | solution.py:77
  87.3 0.7 slice.53
  88.1 0.7 slice.54
  91.6 1.1 %convolution_convert_fusion.x_ref = bf16[2048,128]{1,0:T(8,128)(2,1)} fusion(bf16[2048,64]{0,1:T(8,128)(2,1)S(1)} %bitcast.57, bf16[64,128]{1,0:T(8,128)(2,1)S(1)} %copy-done.6), kind=kOutput, calls=%fused_computation.9 | convolution fusion | flops 33816576 | bytes 802816 | tf_op jit(solution)/shard_map/dot_general | solution.py:504
  92.8 5.7 %shard_map.203 = f32[2048,128]{1,0:T(8,128)} custom-call(bf16[2048,128]{1,0:T(8,128)(2,1)} %convolution_convert_fusion.x_ref), custom_call_target="tpu_custom_call" | custom-call | tf_op jit(solution)/shard_map/pallas_call | solution.py:178
  98.4 2.1 %fusion.20 = bf16[2048,128]{1,0:T(8,128)(2,1)} fusion(f32[2048,128]{1,0:T(8,128)} %shard_map.203, bf16[2048,128]{1,0:T(8,128)(2,1)S(1)} %get-tuple-element.22), kind=kLoop, calls=%fused_computation.37 | loop fusion | flops 786432 | bytes 2097152 | tf_op jit(solution)/shard_map/convert_element_type | solution.py:509
  (59 shorter events, 9.0 us)
Async XLA Ops:
  0.0 69.4 %copy-start = (bf16[128,256]{1,0:T(8,128)(2,1)S(1)}, bf16[128,256]{1,0:T(8,128)(2,1)}, u32[]{:S(2)}) copy-start(bf16[128,256]{1,0:T(8,128)(2,1)} %param.39) | copy-start | bytes 196612
  2.2 4.0 %copy-start.2 = (s32[12288]{0:T(1024)S(1)}, s32[12288]{0:T(1024)}, u32[]{:S(2)}) copy-start(s32[12288]{0:T(1024)} %param.26) | copy-start | bytes 147460
  2.2 4.0 %copy-start.3 = (s32[12288]{0:T(1024)S(1)}, s32[12288]{0:T(1024)}, u32[]{:S(2)}) copy-start(s32[12288]{0:T(1024)} %param.25) | copy-start | bytes 147460
  2.2 4.7 %copy-start.7 = (s32[1,4,512]{2,1,0:T(4,128)S(1)}, s32[1,4,512]{2,1,0:T(4,128)}, u32[]{:S(2)}) copy-start(s32[1,4,512]{2,1,0:T(4,128)} %param.28) | copy-start | bytes 24580
  2.2 5.6 %copy-start.1 = (bf16[2048,128]{1,0:T(8,128)(2,1)S(1)}, bf16[2048,128]{1,0:T(8,128)(2,1)}, u32[]{:S(2)}) copy-start(bf16[2048,128]{1,0:T(8,128)(2,1)} %param.23) | copy-start | bytes 1572868
  57.5 6.7 %copy-start.5 = (bf16[256,128]{1,0:T(8,128)(2,1)S(1)}, bf16[256,128]{1,0:T(8,128)(2,1)}, u32[]{:S(2)}) copy-start(bf16[256,128]{1,0:T(8,128)(2,1)} %param.33) | copy-start | bytes 196612
  62.6 1.9 %copy-start.12 = (bf16[128,128]{1,0:T(8,128)(2,1)S(1)}, bf16[128,128]{1,0:T(8,128)(2,1)}, u32[]{:S(2)}) copy-start(bf16[128,128]{1,0:T(8,128)(2,1)} %param.34) | copy-start | bytes 98308
  64.5 0.8 copy-start.4
  65.3 1.4 %copy-start.9 = (f32[128]{0:T(128)S(1)}, f32[128]{0:T(128)}, u32[]{:S(2)}) copy-start(f32[128]{0:T(128)} %param.36) | copy-start | bytes 1540
  66.0 2.6 %copy-start.10 = (f32[128]{0:T(128)S(1)}, f32[128]{0:T(128)}, u32[]{:S(2)}) copy-start(f32[128]{0:T(128)} %param.37) | copy-start | bytes 1540
  66.0 2.6 %copy-start.14 = (bf16[128,64]{0,1:T(8,128)(2,1)S(1)}, bf16[128,64]{0,1:T(8,128)(2,1)}, u32[]{:S(2)}) copy-start(bf16[128,64]{0,1:T(8,128)(2,1)} %param.38) | copy-start | bytes 49156
  66.6 2.7 %copy-start.8 = (f32[4]{0:T(128)S(1)}, f32[4]{0:T(128)}, u32[]{:S(2)}) copy-start(f32[4]{0:T(128)} %param.40) | copy-start | bytes 52
  71.4 17.5 %copy-start.11 = (f32[2,4,16,16]{3,2,1,0:T(8,128)S(1)}, f32[2,4,16,16]{3,2,1,0:T(8,128)}, u32[]{:S(2)}) copy-start(f32[2,4,16,16]{3,2,1,0:T(8,128)} %param.41) | copy-start | bytes 24580
  71.4 18.8 %copy-start.13 = (f32[4,16,16]{2,1,0:T(8,128)S(1)}, f32[4,16,16]{2,1,0:T(8,128)}, u32[]{:S(2)}) copy-start(f32[4,16,16]{2,1,0:T(8,128)} %param.42) | copy-start | bytes 12292
  90.9 0.7 copy-start.6

commit v11 on v10

--- a/solution.py
+++ b/solution.py
@@ -462,7 +462,7 @@
     own_wide = vertex_state.reshape(node_count // FOLD, FOLD * feature_width)
     picked_ids = halo_outgoing_ids[0].reshape(-1, FOLD)
     outgoing = jnp.concatenate(
-        [pick_rows(vertex_state, picked_ids[:, j]) for j in range(FOLD)], axis=1
+        [gather_rows(vertex_state, picked_ids[:, j], FOLD) for j in range(FOLD)], axis=1
     )
     extended = exchange_halos(own_wide, outgoing, offsets)
     share = capacity // lax.axis_size("head")

time: 101 us -> 102 us (level)
  other arithmetic: 10.1 us -> 13.2 us
  matrix products: 10.7 us -> 9.19 us
    dot_general x4, matrix products: 3.38 us -> 1.91 us  [gather_rows(): picked = jnp.dot(hot, wide, preferred_element_type=jnp.float32)]
    convert_element_type x0 -> x2, other arithmetic: none -> 1.47 us  [gather_rows(): return rows.astype(jnp.bfloat16)]
    eq x0 -> x1, other arithmetic: none -> 1.37 us  [gather_rows(): lane == j]
where the time goes in v11:
time: 102 us
  Pallas kernels  69.5 us (68%)
  other arithmetic  13.2 us (13%)
  matrix products  9.19 us (9%)
  local copies, waits for them, and re-layouts  8.63 us (8%)
  between operations  1.07 us (1%)
    pallas_call x1, Pallas kernels, edge_messages(): pl.pallas_call(functools.partial(_edge_kernel, fold), out_shape=jax.Shape...  25.6 us
    pallas_call x1, Pallas kernels, exchange_halos(): pl.pallas_call(functools.partial(_halo_kernel, offsets), out_shape=jax.Sh...  18.8 us
    pallas_call x1, Pallas kernels, dom_sum(): pl.pallas_call(functools.partial(_radix_kernel, radix, steps), out_shape=...  14.4 us
    pallas_call x2, Pallas kernels, sibling_sum(): pl.pallas_call(_sibling_kernel, out_shape=jax.ShapeDtypeStruct(x.shape, j...  10.7 us
    reshape x1, local copies, waits for them, and re-layouts, edge_messages(): columns = both_ids.reshape(2, share, 1)  3.94 us
    convert_element_type x1, other arithmetic, body(): (refreshed_vertices.astype(jnp.float32) + projected.astype(jnp.float32))....  2.12 us

profile of v11, /device:TPU:1, one launch (start us, length us, event | category | flops | bytes accessed | tf_op | source)
XLA Modules:
  0.0 101.7 jit_solution(11433264629120893462)
XLA Ops:
  0.0 1.0 %reshape_squeeze.7 = s32[512,4]{1,0:T(8,128)S(1)} reshape(s32[1,4,512]{2,1,0:T(4,128)} %param.28) | data formatting | bytes 16384 | tf_op jit(solution)/shard_map/reshape;squeeze | solution.py:463
  1.0 1.4 %compare_reduce_fusion.2 = (pred[512]{0:T(512)(128)(4,1)S(1)}, pred[512]{0:T(512)(128)(4,1)S(1)}, pred[512]{0:T(512)(128)(4,1)S(1)}, pred[512,1]{1,0:T(8,128)(4,...) fusion(s32[512,4]{1,0:T(8,128)S(1)} %reshape_squeeze.7), kind=kLoop, calls=%fused_computation.92 | loop fusion | flops 28672 | bytes 18432 | tf_op jit(solution)/shard_map/eq | solution.py:415
  2.4 1.0 %fusion.19 = (s32[512]{0:T(512)S(1)}, s32[512]{0:T(512)S(1)}, s32[512]{0:T(512)S(1)}, s32[512]{0:T(512)S(1)}) fusion(pred[512,1]{1,0:T(8,128)(4,1)S(1)} %get-tuple-element.63, pred[512,1]{1,0:T(8,128)(4,1)S(1)} %get-tuple-element.62, s32[512,4]{1,0:T(8,128)S(1)} %reshape_squeeze.7, pred[512,1]{1,0:T(8,128)(4,1)S(1)} %get-tuple-element.58, ...), kind=kLoop, calls=%fused_computation.62 | loop fusion | flops 20480 | bytes 20480 | tf_op jit(solution)/shard_map/jit(floor_divide)/jit(_where)/select_n | solution.py:408
  4.7 0.8 fusion.31
  6.6 0.6 fusion.25
  7.2 0.9 pad_maximum_fusion.out_ref
  8.1 18.8 %shard_map.199.ext_ref = bf16[1024,512]{1,0:T(8,128)(2,1)} custom-call(bf16[512,512]{1,0:T(8,128)(2,1)} %copy-done.2, bf16[512,512]{1,0:T(8,128)(2,1)} %pad_maximum_fusion.out_ref), custom_call_target="tpu_custom_call" | custom-call | tf_op jit(solution)/shard_map/pallas_call | solution.py:148
  28.3 3.9 %copy.55.ids_ref = s32[2,6144,1]{2,1,0:T(8,128)} copy(s32[2,6144,1]{1,0,2:T(2,128)S(1)} %fusion.91) | data formatting | bytes 98304 | tf_op jit(solution)/shard_map/reshape | solution.py:263
  32.4 0.6 slice.121
  33.0 25.6 %shard_map.200.x_ref = f32[512,512]{1,0:T(8,128)} custom-call(s32[3]{0:T(128)} %pad_add_fusion.scalars, bf16[12288,128]{1,0:T(8,128)(2,1)} %edge_ref.1, s32[2,6144,1]{2,1,0:T(8,128)} %copy.55.ids_ref, s32[6,1,1024]{2,1,0:T(1,128)} %bitcast.62, bf16[1024,512]{1,0:T(8,128)(2,1)} %shard_map.199.ext_ref, bf16[512,512]{1,0:T(8,128)(2,1)} %copy-done.2, ...), custom_call_target="tpu_custom_call" | custom-call | tf_op jit(solution)/shard_map/pallas_call | solution.py:284
  58.6 5.0 %shard_map.201 = f32[512,512]{1,0:T(8,128)} custom-call(f32[512,512]{1,0:T(8,128)} %shard_map.200.x_ref), custom_call_target="tpu_custom_call" | custom-call | tf_op jit(solution)/shard_map/pallas_call | solution.py:178
  63.7 1.3 %convert_element_type.67 = bf16[512,512]{1,0:T(8,128)(2,1)S(1)} convert(f32[512,512]{1,0:T(8,128)} %shard_map.201) | non-fusion elementwise | flops 262144 | bytes 1572864 | tf_op jit(solution)/shard_map/convert_element_type | solution.py:484
  65.6 0.7 multiply_convert_fusion
  67.1 0.6 multiply_reduce_fusion
  67.7 1.2 %convert_reduce_fusion = (f32[2048]{0:T(1024)S(1)}, bf16[2048,128]{1,0:T(8,128)(2,1)S(1)}) fusion(f32[128]{0:T(128)S(1)} %copy-done.9, f32[2048]{0:T(1024)S(1)} %add_rsqrt_fusion.1, f32[2048,128]{1,0:T(8,128)S(1)} %copy.56, f32[2048]{0:T(1024)S(1)} %broadcast_multiply_fusion.1, bf16[2048,128]{1,0:T(8,128)(2,1)S(1)} %copy-done.1), kind=kLoop, calls=%fused_computation.13 | loop fusion | flops 2095104 | bytes 2122240 | tf_op jit(solution)/shard_map/reduce_sum | solution.py:316
  69.0 0.6 fusion.5
  69.7 0.8 convolution_convert_fusion.2
  70.5 0.9 fusion.64
  74.0 14.4 %shard_map.202 = f32[40,128]{1,0:T(8,128)} custom-call(f32[40,128]{1,0:T(8,128)} %fusion.58.x_ref), custom_call_target="tpu_custom_call" | custom-call | tf_op jit(solution)/shard_map/pallas_call | solution.py:77
  88.4 0.7 slice.117
  89.2 0.7 slice.118
  92.7 1.1 %convolution_convert_fusion.x_ref = bf16[2048,128]{1,0:T(8,128)(2,1)} fusion(bf16[2048,64]{0,1:T(8,128)(2,1)S(1)} %bitcast.57, bf16[64,128]{1,0:T(8,128)(2,1)S(1)} %copy-done.7), kind=kOutput, calls=%fused_computation.1 | convolution fusion | flops 33816576 | bytes 802816 | tf_op jit(solution)/shard_map/dot_general | solution.py:504
  93.8 5.7 %shard_map.203 = f32[2048,128]{1,0:T(8,128)} custom-call(bf16[2048,128]{1,0:T(8,128)(2,1)} %convolution_convert_fusion.x_ref), custom_call_target="tpu_custom_call" | custom-call | tf_op jit(solution)/shard_map/pallas_call | solution.py:178
  99.5 2.1 %fusion.8 = bf16[2048,128]{1,0:T(8,128)(2,1)} fusion(f32[2048,128]{1,0:T(8,128)} %shard_map.203, bf16[2048,128]{1,0:T(8,128)(2,1)S(1)} %get-tuple-element.40), kind=kLoop, calls=%fused_computation.21 | loop fusion | flops 786432 | bytes 2097152 | tf_op jit(solution)/shard_map/convert_element_type | solution.py:509
  (62 shorter events, 9.9 us)
Async XLA Ops:
  0.0 70.5 %copy-start = (bf16[128,256]{1,0:T(8,128)(2,1)S(1)}, bf16[128,256]{1,0:T(8,128)(2,1)}, u32[]{:S(2)}) copy-start(bf16[128,256]{1,0:T(8,128)(2,1)} %param.39) | copy-start | bytes 196612
  0.0 3.4 %copy-start.1 = (bf16[2048,128]{1,0:T(8,128)(2,1)S(1)}, bf16[2048,128]{1,0:T(8,128)(2,1)}, u32[]{:S(2)}) copy-start(bf16[2048,128]{1,0:T(8,128)(2,1)} %param.23) | copy-start | bytes 1572868
  3.8 2.3 %copy-start.2 = (bf16[512,512]{1,0:T(8,128)(2,1)}, bf16[512,512]{1,0:T(8,128)(2,1)S(1)}, u32[]{:S(2)}) copy-start(bf16[512,512]{1,0:T(8,128)(2,1)S(1)} %reshape.99.own_ref) | copy-start | bytes 1572868
  6.5 21.6 %copy-start.3 = (s32[12288]{0:T(1024)S(1)}, s32[12288]{0:T(1024)}, u32[]{:S(2)}) copy-start(s32[12288]{0:T(1024)} %param.26) | copy-start | bytes 147460
  6.6 21.6 %copy-start.4 = (s32[12288]{0:T(1024)S(1)}, s32[12288]{0:T(1024)}, u32[]{:S(2)}) copy-start(s32[12288]{0:T(1024)} %param.25) | copy-start | bytes 147460
  58.6 6.7 %copy-start.6 = (bf16[256,128]{1,0:T(8,128)(2,1)S(1)}, bf16[256,128]{1,0:T(8,128)(2,1)}, u32[]{:S(2)}) copy-start(bf16[256,128]{1,0:T(8,128)(2,1)} %param.33) | copy-start | bytes 196612
  63.7 1.9 %copy-start.12 = (bf16[128,128]{1,0:T(8,128)(2,1)S(1)}, bf16[128,128]{1,0:T(8,128)(2,1)}, u32[]{:S(2)}) copy-start(bf16[128,128]{1,0:T(8,128)(2,1)} %param.34) | copy-start | bytes 98308
  65.6 0.8 copy-start.5
  66.4 1.4 %copy-start.9 = (f32[128]{0:T(128)S(1)}, f32[128]{0:T(128)}, u32[]{:S(2)}) copy-start(f32[128]{0:T(128)} %param.36) | copy-start | bytes 1540
  67.0 2.6 %copy-start.10 = (f32[128]{0:T(128)S(1)}, f32[128]{0:T(128)}, u32[]{:S(2)}) copy-start(f32[128]{0:T(128)} %param.37) | copy-start | bytes 1540
  67.1 2.6 %copy-start.14 = (bf16[128,64]{0,1:T(8,128)(2,1)S(1)}, bf16[128,64]{0,1:T(8,128)(2,1)}, u32[]{:S(2)}) copy-start(bf16[128,64]{0,1:T(8,128)(2,1)} %param.38) | copy-start | bytes 49156
  67.7 2.8 %copy-start.8 = (f32[4]{0:T(128)S(1)}, f32[4]{0:T(128)}, u32[]{:S(2)}) copy-start(f32[4]{0:T(128)} %param.40) | copy-start | bytes 52
  72.5 17.5 %copy-start.11 = (f32[2,4,16,16]{3,2,1,0:T(8,128)S(1)}, f32[2,4,16,16]{3,2,1,0:T(8,128)}, u32[]{:S(2)}) copy-start(f32[2,4,16,16]{3,2,1,0:T(8,128)} %param.41) | copy-start | bytes 24580
  72.5 18.8 %copy-start.13 = (f32[4,16,16]{2,1,0:T(8,128)S(1)}, f32[4,16,16]{2,1,0:T(8,128)}, u32[]{:S(2)}) copy-start(f32[4,16,16]{2,1,0:T(8,128)} %param.42) | copy-start | bytes 12292
  92.0 0.7 copy-start.7
